TPU v7x, 32 devices: a whole 2x2x4 slice. The times are simulated.
32 devices in a mesh: lat: 4 (over y, x), lon: 8 (over z, core).
Axes of the slice: x: 2, y: 2, z: 4, core: 2. Of those that a mesh axis runs over, the one named last changes fastest.
Arguments:
- background: bfloat16 [64, 256, 512], P('lat', 'lon'), may hold values from -6 to 6
- obs_rows: bfloat16 [16384, 256], P(('lat', 'lon')), may hold values from -6 to 6
- obs_pixel: int32 [16384], P(('lat', 'lon')), may hold values from 0 to 16383, as said below
- obs_count: int32 [32], P(('lat', 'lon')), may hold values from 256 to 512, as said below
- block_pattern: int32 [8, 32, 4], P('lat', 'lon'), may hold values 0 or 1
- w_enc: bfloat16 [256, 512], replicated, may hold values from -0.375 to 0.375
- w_qkv: bfloat16 [512, 1536], replicated, may hold values from -0.375 to 0.375
- w_out: bfloat16 [512, 512], replicated, may hold values from -0.25 to 0.25
- cotangent: bfloat16 [64, 256, 512], P('lat', 'lon'), may hold values from -6 to 6
Outputs:
- updated: bfloat16 [64, 256, 512], P('lat', 'lon')
- grad_background: bfloat16 [64, 256, 512], P('lat', 'lon')
- grad_obs: bfloat16 [16384, 256], P(('lat', 'lon'))
Inputs may be any that keep to these rules, and one draw needn't show every extreme that they name: obs_count[d] counts the live rows of device d of lat+lon; its rows are the 512 rows starting at d * 512. `obs_pixel`: each entry names a pixel as latitude_row * 256 + column, with latitude_row its row index in the slab and column its index along the row. Among the live rows of one device, at most 18 name pixels of one device of lat+lon; in every draw one device receives exactly 18 live rows from every device.
All inputs are finite; a program needn't handle non-finite values. No bound on the sum of `block_pattern` on one device may be relied on, other than what follows from the above.
Results may differ from a plain program's by a relative error of at most 0.018.
Values may be sent and summed in bfloat16 or wider, within the bound.
No kernel may reach another device: no remote copies, remote signals or barrier semaphores. Data moves between devices by JAX's collectives and lax.ppermute only.
A program may use at most 192 MiB of HBM per device.

v0:
```python
import math

import jax
import jax.numpy as jnp
from jax import lax
from jax.sharding import PartitionSpec as P

HEADS = 8
BLOCK = 8


norm_eps = 1e-06
gelu_coef = 0.7978845608028654


def extended_2(shard, sides, width):
    for axis, dim in sides:
        peers, length = (lax.axis_size(axis), shard.shape[dim])
        up = [(i, (i + 1) % peers) for i in range(peers)]
        down = [(j, i) for i, j in up]
        last = lax.slice_in_dim(shard, length - width, length, axis=dim)
        first = lax.slice_in_dim(shard, 0, width, axis=dim)
        before = lax.ppermute(last, axis, up)
        after = lax.ppermute(first, axis, down)
        shard = jnp.concatenate([before, shard, after], axis=dim)
    return shard


def gelu_tanh(inputs):
    inner_arg = gelu_coef * (inputs + 0.044715 * inputs * inputs * inputs)
    return 0.5 * inputs * (1.0 + jnp.tanh(inner_arg))


def gelu_slope(inputs):
    inner_arg = gelu_coef * (inputs + 0.044715 * inputs * inputs * inputs)
    tangent = jnp.tanh(inner_arg)
    return 0.5 * (1.0 + tangent) + 0.5 * inputs * (1.0 - tangent * tangent) * gelu_coef * (
        1.0 + 3.0 * 0.044715 * inputs * inputs
    )


def to_blocks(field_grid):
    rows_all, cols_all, depth_dim = field_grid.shape
    shaped = field_grid.reshape(rows_all // BLOCK, BLOCK, cols_all // BLOCK, BLOCK, depth_dim)
    return shaped.transpose(0, 2, 1, 3, 4).reshape(
        rows_all // BLOCK, cols_all // BLOCK, BLOCK * BLOCK, depth_dim
    )


def from_blocks(blocks):
    row_blocks, col_blocks, block_area, depth_dim = blocks.shape
    shaped = blocks.reshape(row_blocks, col_blocks, BLOCK, BLOCK, depth_dim)
    return shaped.transpose(0, 2, 1, 3, 4).reshape(
        row_blocks * BLOCK, col_blocks * BLOCK, depth_dim
    )


def mask_from_pattern(pattern):
    pattern_float = pattern.astype(jnp.float32)
    self_column = jnp.ones(pattern_float.shape[:2] + (1,), jnp.float32)
    return jnp.concatenate([pattern_float[..., :2], self_column, pattern_float[..., 2:]], axis=-1)


def attend(queries, key_rows, grad_heads, key_mask):
    row_blocks, col_blocks, block_area, channels = queries.shape
    head_dim = channels // HEADS
    query_shape = (row_blocks, col_blocks, block_area, HEADS, head_dim)
    key_shape = (row_blocks, col_blocks, 5, block_area, HEADS, head_dim)
    query_heads = queries.reshape(query_shape)
    key_heads = key_rows[..., :channels].reshape(key_shape)
    value_heads = key_rows[..., channels:].reshape(key_shape)
    grad_split = grad_heads.reshape(query_shape)
    score_scale = 1.0 / math.sqrt(head_dim)
    scores = jnp.einsum(
        "abqhd,abokhd->abhqok", query_heads, key_heads, preferred_element_type=jnp.float32
    )
    live_keys = jnp.sum(key_mask, axis=-1) * float(block_area)
    offset_bias = -jnp.log(live_keys)[:, :, None, None, None, None]
    gate_mask = key_mask[:, :, None, None, :, None]
    weights = jax.nn.sigmoid(scores * score_scale + offset_bias) * gate_mask
    weights_bf = weights.astype(jnp.bfloat16)
    mixed_heads = jnp.einsum(
        "abhqok,abokhd->abqhd", weights_bf, value_heads, preferred_element_type=jnp.float32
    )
    mixed_heads = mixed_heads.astype(jnp.bfloat16).reshape(
        row_blocks, col_blocks, block_area, channels
    )
    grad_weights = jnp.einsum(
        "abqhd,abokhd->abhqok", grad_split, value_heads, preferred_element_type=jnp.float32
    )
    grad_scores = (grad_weights * weights * (1.0 - weights) * score_scale).astype(jnp.bfloat16)
    grad_query = jnp.einsum(
        "abhqok,abokhd->abqhd", grad_scores, key_heads, preferred_element_type=jnp.float32
    )
    grad_query = grad_query.astype(jnp.bfloat16).reshape(
        row_blocks, col_blocks, block_area, channels
    )
    grad_key = jnp.einsum(
        "abhqok,abqhd->abokhd", grad_scores, query_heads, preferred_element_type=jnp.float32
    )
    grad_value = jnp.einsum(
        "abhqok,abqhd->abokhd", weights_bf, grad_split, preferred_element_type=jnp.float32
    )
    flat_shape = (row_blocks, col_blocks, 5, block_area, channels)
    contrib = jnp.concatenate(
        [grad_key.reshape(flat_shape), grad_value.reshape(flat_shape)], axis=-1
    )
    return (mixed_heads, grad_query, contrib)


def shards(
    background, obs_rows, obs_pixel, obs_count, block_pattern, w_enc, w_qkv, w_out, cotangent
):
    lat_rows, lon_cols, channels = background.shape
    pixels = lat_rows * lon_cols
    obs_slots = obs_rows.shape[0]
    lat_devices = lax.axis_size("lat")
    lon_devices = lax.axis_size("lon")
    dev_count = lat_devices * lon_devices
    capacity = (obs_slots + dev_count - 1) // dev_count + 2
    send_total = dev_count * capacity
    lon_all = lon_cols * lon_devices
    halo_width = 2 * BLOCK
    lat_index = obs_pixel // lon_all
    lon_index = obs_pixel % lon_all
    owner_dev = lat_index // lat_rows * lon_devices + lon_index // lon_cols
    local_pixel = lat_index % lat_rows * lon_cols + lon_index % lon_cols
    is_live = jnp.arange(obs_slots, dtype=jnp.int32) < obs_count[0]
    owner_table = (
        (owner_dev[:, None] == jnp.arange(dev_count, dtype=jnp.int32)[None, :]) & is_live[:, None]
    ).astype(jnp.int32)
    running = jnp.cumsum(owner_table, axis=0)
    rank_in = jnp.sum(running * owner_table, axis=1) - 1
    send_slot = jnp.where(is_live, owner_dev * capacity + rank_in, send_total)
    send_pixel = jnp.full((send_total,), -1, jnp.int32).at[send_slot].set(local_pixel, mode="drop")
    payload = (
        jnp.zeros((send_total, obs_rows.shape[1]), jnp.bfloat16)
        .at[send_slot]
        .set(obs_rows, mode="drop")
    )
    payload_cube = payload.reshape(dev_count, capacity, payload.shape[1])
    pixel_grid = send_pixel.reshape(dev_count, capacity)
    arrived, arrived_pixel = (
        lax.all_to_all(payload_cube, ("lat", "lon"), split_axis=0, concat_axis=0, tiled=True),
        lax.all_to_all(pixel_grid, ("lat", "lon"), split_axis=0, concat_axis=0, tiled=True),
    )
    arrived = arrived.reshape(send_total, payload.shape[1])
    arrived_pixel = arrived_pixel.reshape(send_total)
    owner_pre = jnp.dot(arrived, w_enc, preferred_element_type=jnp.float32)
    encoded = gelu_tanh(owner_pre).astype(jnp.bfloat16)
    pixel_table = jnp.arange(pixels, dtype=jnp.int32)[:, None] == arrived_pixel[None, :]
    obs_sum = jnp.dot(pixel_table.astype(jnp.bfloat16), encoded, preferred_element_type=jnp.float32)
    obs_number = jnp.sum(pixel_table.astype(jnp.float32), axis=1)
    denominator = 1.0 + obs_number
    state_in = (
        background.reshape(pixels, channels).astype(jnp.float32) + obs_sum / denominator[:, None]
    ).astype(jnp.bfloat16)
    state_f32 = state_in.astype(jnp.float32)
    inv_rms = lax.rsqrt(jnp.mean(state_f32 * state_f32, axis=1, keepdims=True) + norm_eps)
    normed = state_f32 * inv_rms
    normed_bf = normed.astype(jnp.bfloat16)
    projected = jnp.dot(normed_bf, w_qkv, preferred_element_type=jnp.float32).astype(jnp.bfloat16)
    queries = projected[:, :channels].reshape(lat_rows, lon_cols, channels)
    key_vals = projected[:, channels:].reshape(lat_rows, lon_cols, 2 * channels)
    normed_ext = extended_2(
        normed_bf.reshape(lat_rows, lon_cols, channels), (("lon", 1),), halo_width
    )
    rim_states = jnp.concatenate(
        [normed_ext[:, :halo_width], normed_ext[:, halo_width + lon_cols :]], axis=1
    )
    rim_proj = jnp.dot(
        rim_states.reshape(lat_rows * 2 * halo_width, channels),
        w_qkv[:, channels:],
        preferred_element_type=jnp.float32,
    ).astype(jnp.bfloat16)
    rim_proj = rim_proj.reshape(lat_rows, 2 * halo_width, 2 * channels)
    extended = jnp.concatenate(
        [rim_proj[:, :halo_width], key_vals, rim_proj[:, halo_width:]], axis=1
    )
    key_mask = mask_from_pattern(block_pattern)
    ext_blocks = to_blocks(extended)
    col_blocks = lon_cols // BLOCK
    key_rows = jnp.stack(
        [ext_blocks[:, offset : offset + col_blocks] for offset in range(5)], axis=2
    )
    cot_rows = cotangent.reshape(pixels, channels)
    grad_out = jnp.dot(cot_rows, w_out.T, preferred_element_type=jnp.float32).astype(jnp.bfloat16)
    grad_grid = grad_out.reshape(lat_rows, lon_cols, channels)
    mixed_heads, grad_query, contrib = attend(
        to_blocks(queries), key_rows, to_blocks(grad_grid), key_mask
    )
    attn_out = jnp.dot(
        from_blocks(mixed_heads).reshape(pixels, channels),
        w_out,
        preferred_element_type=jnp.float32,
    )
    updated = (state_f32 + attn_out).astype(jnp.bfloat16).reshape(lat_rows, lon_cols, channels)
    grad_ext_blocks = jnp.pad(contrib[:, :, 0], ((0, 0), (0, 4), (0, 0), (0, 0)))
    for offset in range(1, 5):
        grad_ext_blocks = grad_ext_blocks + jnp.pad(
            contrib[:, :, offset], ((0, 0), (offset, 4 - offset), (0, 0), (0, 0))
        )
    grad_ext = from_blocks(grad_ext_blocks)
    own_part = lax.optimization_barrier(
        grad_ext[:, halo_width : halo_width + lon_cols].astype(jnp.bfloat16)
    )
    rim_pair = jnp.concatenate(
        [grad_ext[:, :halo_width], grad_ext[:, halo_width + lon_cols :]], axis=1
    ).astype(jnp.bfloat16)
    received = extended_2(rim_pair, (("lon", 1),), halo_width)
    from_west = received[:, :halo_width].astype(jnp.float32)
    from_east = received[:, 3 * halo_width :].astype(jnp.float32)
    grad_total = own_part.astype(jnp.float32)
    grad_total = grad_total + jnp.pad(from_west, ((0, 0), (0, lon_cols - halo_width), (0, 0)))
    grad_total = grad_total + jnp.pad(from_east, ((0, 0), (lon_cols - halo_width, 0), (0, 0)))
    grad_keyval = grad_total.astype(jnp.bfloat16).reshape(pixels, 2 * channels)
    grad_proj = jnp.concatenate(
        [from_blocks(grad_query).reshape(pixels, channels), grad_keyval], axis=1
    )
    grad_normed = jnp.dot(grad_proj, w_qkv.T, preferred_element_type=jnp.float32)
    grad_state = cot_rows.astype(jnp.float32) + inv_rms * (
        grad_normed - normed * jnp.mean(grad_normed * normed, axis=1, keepdims=True)
    )
    grad_background = grad_state.astype(jnp.bfloat16).reshape(lat_rows, lon_cols, channels)
    grad_scaled = grad_state / denominator[:, None]
    safe_pixel = jnp.clip(arrived_pixel, 0, pixels - 1)
    grad_enc = jnp.where(
        (arrived_pixel >= 0)[:, None], jnp.take(grad_scaled, safe_pixel, axis=0), 0.0
    ).astype(jnp.bfloat16)
    grad_pre = (grad_enc.astype(jnp.float32) * gelu_slope(owner_pre)).astype(jnp.bfloat16)
    reply_rows = jnp.dot(grad_pre, w_enc.T, preferred_element_type=jnp.float32).astype(jnp.bfloat16)
    reply_cube = reply_rows.reshape(dev_count, capacity, reply_rows.shape[1])
    returned = lax.all_to_all(reply_cube, ("lat", "lon"), split_axis=0, concat_axis=0, tiled=True)
    returned = returned.reshape(send_total, reply_rows.shape[1])
    grad_obs = jnp.where(
        is_live[:, None],
        jnp.take(returned, jnp.clip(send_slot, 0, send_total - 1), axis=0),
        jnp.zeros((), jnp.bfloat16),
    )
    return (updated, grad_background, grad_obs)


def solution(mesh):
    return jax.shard_map(
        shards,
        mesh=mesh,
        in_specs=(
            P("lat", "lon", None),
            P(("lat", "lon"), None),
            P(("lat", "lon")),
            P(("lat", "lon")),
            P("lat", "lon", None),
            P(),
            P(),
            P(),
            P("lat", "lon", None),
        ),
        out_specs=(P("lat", "lon", None), P("lat", "lon", None), P(("lat", "lon"), None)),
        check_vma=False,
    )
```

profile of v0, /device:TPU:0, one launch (start us, length us, event | category | flops | bytes accessed | tf_op | source)
XLA Modules:
  0.0 224.0 jit_solution(18242425901806227023)
XLA Ops:
  1.4 0.7 fusion.64
  2.1 1.2 reduce-window.6
  3.7 2.4 %scatter_custom_fusion = s32[576]{0:T(1024)S(1)} fusion(s32[512]{0:T(512)S(1)} %compare_select_fusion.3, s32[512]{0:T(512)S(1)} %get-tuple-element.26, s32[]{:T(128)} %constant.117.clone.1), kind=kCustom, calls=%fused_computation.136 | custom fusion | bytes 2308 | tf_op jit(solution)/shard_map/scatter | solution.py:135
  6.1 0.7 all_to_all.12
  6.8 7.3 %all-to-all-start = ((s32[32,1,18]{2,1,0:T(1,128)}), s32[32,1,18]{2,1,0:T(1,128)S(1)}, u32[]{:S(2)}, u32[]{:S(2)}) async-start(s32[32,1,18]{2,1,0:T(1,128)} %bitcast.4), calls=%async_computation | async-start | bytes 32768 | tf_op jit(solution)/shard_map/all_to_all | solution.py:145
  14.1 0.7 convert_element_type.112
  15.0 0.6 compare_and_fusion.1
  15.6 1.5 convolution_convert_fusion.2
  17.2 2.8 %scatter_custom_fusion.1 = bf16[576,256]{1,0:T(8,128)(2,1)S(1)} fusion(s32[512]{0:T(512)S(1)} %compare_select_fusion.3, bf16[512,256]{1,0:T(8,128)(2,1)} %param.10, bf16[]{:T(256)} %constant.132.clone.1), kind=kCustom, calls=%fused_computation.85 | custom fusion | bytes 295424 | tf_op jit(solution)/shard_map/scatter | solution.py:139
  20.0 0.8 reshape.173
  20.9 0.5 reshape_reshape.29
  21.5 1.5 copy.127
  23.0 5.8 %all-to-all-start.1 = ((bf16[32,18,256]{2,1,0:T(8,128)(2,1)}), bf16[32,18,256]{2,1,0:T(8,128)(2,1)S(1)}, u32[]{:S(2)}, u32[]{:S(2)}) async-start(bf16[32,18,256]{2,1,0:T(8,128)(2,1)} %reshape.173), calls=%async_computation.1 | async-start | bytes 786432 | tf_op jit(solution)/shard_map/all_to_all | solution.py:144
  28.8 0.5 broadcast.304
  29.3 0.7 clamp_reduce_fusion
  30.5 11.8 %all-to-all-done.1 = bf16[32,18,256]{2,1,0:T(8,128)(2,1)S(1)} async-done(((bf16[32,18,256]{2,1,0:T(8,128)(2,1)}), bf16[32,18,256]{2,1,0:T(8,128)(2,1)S(1)}, u32[]{:S(2)}, u32[]{:S(2)}) %all-to-all-start.1) | async-done | bytes 294944 | tf_op jit(solution)/shard_map/all_to_all | solution.py:144
  42.8 1.1 fusion.40
  43.9 0.8 copy-done.3
  44.8 0.8 fusion.86
  45.8 3.4 %collective-permute-start.1 = (bf16[16,16,512]{2,1,0:T(8,128)(2,1)}, bf16[16,16,512]{2,1,0:T(8,128)(2,1)}, u32[]{:S(2)}, u32[]{:S(2)}) collective-permute-start(bf16[16,16,512]{2,1,0:T(8,128)(2,1)} %get-tuple-element.21), channel_id=1, source_target_pairs={{1,0},{2,1},{3,2},{4,3},{5,4},{6,5},{7,6},{0,7},{9,8},{10,9},{11,1... | collective-permute-start | bytes 786440 | tf_op jit(solution)/shard_map/ppermute | solution.py:24
  49.2 1.0 convolution_convert_fusion
  50.3 0.9 copy.161
  51.2 1.6 reshape_reshape.25
  52.9 1.5 copy.126
  54.4 0.4 collective-permute-done
  54.8 1.1 pad_maximum_fusion.1
  55.9 0.7 convolution_convert_fusion.1
  56.7 0.4 slice-done.6
  58.0 2.2 fusion.83
  60.1 7.4 %reshape.248 = bf16[2,4,5,64,8,64]{5,4,3,1,0,2:T(8,128)(2,1)} reshape(bf16[2,4,5,64,512]{4,3,1,0,2:T(8,128)(2,1)} %get-tuple-element.14) | data formatting | bytes 5242880 | tf_op jit(solution)/shard_map/reshape | solution.py:71
  67.6 4.5 %reshape.249 = bf16[2,4,5,64,8,64]{5,4,3,1,0,2:T(8,128)(2,1)} reshape(bf16[2,4,5,64,512]{4,3,1,0,2:T(8,128)(2,1)S(1)} %get-tuple-element.15) | data formatting | bytes 5242880 | tf_op jit(solution)/shard_map/reshape | solution.py:70
  72.1 8.4 %copy.110 = bf16[2,4,5,64,8,64]{3,5,2,4,1,0:T(8,128)(2,1)} copy(bf16[2,4,5,64,8,64]{5,4,3,1,0,2:T(8,128)(2,1)} %reshape.249) | data formatting | bytes 5242880 | tf_op jit(solution)/shard_map/reshape | solution.py:70
  80.6 5.8 %divide_multiply_fusion = f32[2,4,8,64,5,64]{5,3,4,2,1,0:T(8,128)S(1)} fusion(f32[2,4,5]{2,1,0:T(4,128)S(1)} %pad_maximum_fusion.2, f32[2,4]{1,0:T(2,128)S(1)} %log_negate_fusion, bf16[2,4,64,8,64,1]{2,4,5,3,1,0:T(8,128)(2,1)S(1)} %copy-done.5, bf16[2,4,5,64,8,64]{3,5,2,4,1,0:T(8,128)(2,1)} %copy.110), kind=kOutput, calls=%fused_computation.5 | convolution fusion | flops 175636480 | bytes 8388800 | tf_op jit(solution)/shard_map/abqhd,abokhd->abhqok/dot_general | solution.py:74
  86.3 4.0 %copy-done.1 = f32[2,4,8,64,5,64]{5,3,4,2,1,0:T(8,128)} copy-done((f32[2,4,8,64,5,64]{5,3,4,2,1,0:T(8,128)}, f32[2,4,8,64,5,64]{5,3,4,2,1,0:T(8,128)S(1)}, u32[]{:S(2)}) %copy-start.1) | copy-done | bytes 5242904
  90.3 5.3 %convolution_bitcast_fusion = f32[2,4,5,64,8,64]{3,5,2,4,1,0:T(8,128)} fusion(bf16[2,4,64,8,64,1]{2,4,5,3,1,0:T(8,128)(2,1)S(1)} %copy-done.2, f32[2,4,8,64,5,64]{5,3,4,2,1,0:T(8,128)S(1)} %divide_multiply_fusion), kind=kOutput, calls=%fused_computation.11 | convolution fusion | flops 169082880 | bytes 11010048 | tf_op jit(solution)/shard_map/abhqok,abqhd->abokhd/dot_general | solution.py:101
  95.7 8.7 %multiply_convert_fusion = bf16[2,4,8,64,5,64]{5,3,4,2,1,0:T(8,128)(2,1)} fusion(f32[2,4,8,64,5,64]{5,3,4,2,1,0:T(8,128)} %copy-done.1, bf16[2,4,64,8,64,1]{2,4,5,3,1,0:T(8,128)(2,1)S(1)} %copy-done.2, bf16[2,4,5,64,8,64]{5,4,3,1,0,2:T(8,128)(2,1)S(1)} %bitcast.165), kind=kOutput, calls=%fused_computation.4 | convolution fusion | flops 174325760 | bytes 11010048 | tf_op jit(solution)/shard_map/abqhd,abokhd->abhqok/dot_general | solution.py:88
  104.3 11.3 %copy.116 = f32[2,4,5,64,8,64]{5,4,3,2,1,0:T(8,128)} copy(f32[2,4,5,64,8,64]{3,5,2,4,1,0:T(8,128)} %convolution_bitcast_fusion) | data formatting | bytes 10485760 | tf_op jit(solution)/shard_map/abhqok,abqhd->abokhd/transpose | solution.py:101
  115.6 9.5 %reshape.186 = f32[2,4,5,64,512]{4,3,2,1,0:T(8,128)} reshape(f32[2,4,5,64,8,64]{5,4,3,2,1,0:T(8,128)} %copy.116) | data formatting | bytes 10485760 | tf_op jit(solution)/shard_map/reshape | solution.py:106
  125.1 7.9 %convolution_bitcast_fusion.1 = f32[2,4,5,64,8,64]{3,5,2,4,1,0:T(8,128)} fusion(bf16[2,4,64,8,64,1]{2,4,5,3,1,0:T(8,128)(2,1)S(1)} %copy-done.5, bf16[2,4,8,64,5,64]{5,3,4,2,1,0:T(8,128)(2,1)} %multiply_convert_fusion), kind=kOutput, calls=%fused_computation.12 | convolution fusion | flops 167772160 | bytes 8388608 | tf_op jit(solution)/shard_map/abhqok,abqhd->abokhd/dot_general | solution.py:98
  133.0 11.2 %copy.114 = f32[2,4,5,64,8,64]{5,4,3,2,1,0:T(8,128)} copy(f32[2,4,5,64,8,64]{3,5,2,4,1,0:T(8,128)} %convolution_bitcast_fusion.1) | data formatting | bytes 10485760 | tf_op jit(solution)/shard_map/abhqok,abqhd->abokhd/transpose | solution.py:98
  144.2 9.5 %reshape.185 = f32[2,4,5,64,512]{4,3,2,1,0:T(8,128)} reshape(f32[2,4,5,64,8,64]{5,4,3,2,1,0:T(8,128)} %copy.114) | data formatting | bytes 10485760 | tf_op jit(solution)/shard_map/reshape | solution.py:106
  153.7 5.9 %constant_dynamic-update-slice_fusion.1 = f32[2,4,5,64,1024]{4,3,2,1,0:T(8,128)} fusion(f32[2,4,5,64,512]{4,3,2,1,0:T(8,128)} %reshape.185), kind=kLoop, calls=%fused_computation.100 | loop fusion | bytes 10485760
  159.6 5.8 %constant_dynamic-update-slice_fusion = f32[2,4,5,64,1024]{4,3,2,1,0:T(8,128)} fusion(f32[2,4,5,64,1024]{4,3,2,1,0:T(8,128)} %constant_dynamic-update-slice_fusion.1, f32[2,4,5,64,512]{4,3,2,1,0:T(8,128)} %reshape.186), kind=kLoop, calls=%fused_computation.99 | loop fusion | bytes 10485760 | tf_op jit(solution)/shard_map/concatenate | solution.py:105
  165.4 7.9 %slice_bitcast_fusion.4 = (f32[2,4,64,1024]{3,2,1,0:T(8,128)S(1)}, f32[2,4,64,1024]{3,2,1,0:T(8,128)S(1)}, f32[2,4,64,1024]{3,2,1,0:T(8,128)}, f32[2,4,64,1024]{3,2,1,0:T(8,128)}, f32[2,4,64,1024]{3,2,1,0:T(8,128)}) fusion(f32[2,4,5,64,1024]{4,3,2,1,0:T(8,128)} %constant_dynamic-update-slice_fusion), kind=kLoop, calls=%fused_computation.20 | loop fusion | bytes 20971520 | tf_op jit(solution)/shard_map/squeeze | solution.py:198
  173.3 3.4 %fusion.8 = bf16[2,8,8,8,1024]{4,3,2,1,0:T(8,128)(2,1)S(1)} fusion(f32[2,4,64,1024]{3,2,1,0:T(8,128)} %get-tuple-element.12, f32[2,4,64,1024]{3,2,1,0:T(8,128)} %get-tuple-element.13, f32[2,4,64,1024]{3,2,1,0:T(8,128)S(1)} %get-tuple-element.10, f32[2,4,64,1024]{3,2,1,0:T(8,128)} %get-tuple-element.11, f32[2,4,64,1024]{3,2,1,0:T(8,128)S(1)} %get-tuple-element.9), kind=kLoop, calls=%fused_computation.26 | loop fusion | flops 5242880 | bytes 12582912 | tf_op jit(solution)/shard_map/convert.9
  177.0 1.1 fusion.84
  178.1 3.5 %collective-permute-start.3 = (bf16[16,16,1024]{2,1,0:T(8,128)(2,1)}, bf16[16,16,1024]{2,1,0:T(8,128)(2,1)}, u32[]{:S(2)}, u32[]{:S(2)}) collective-permute-start(bf16[16,16,1024]{2,1,0:T(8,128)(2,1)} %get-tuple-element.17), channel_id=1, source_target_pairs={{1,0},{2,1},{3,2},{4,3},{5,4},{6,5},{7,6},{0,7},{9,8},{10,9},{11,1... | collective-permute-start | bytes 1572872 | tf_op jit(solution)/shard_map/ppermute | solution.py:24
  181.7 1.8 fusion.25
  183.4 1.7 copy.111
  185.1 1.9 reshape_reshape.30
  187.2 6.6 %collective-permute-done.2 = bf16[16,16,1024]{2,1,0:T(8,128)(2,1)S(1)} collective-permute-done((bf16[16,16,1024]{2,1,0:T(8,128)(2,1)}, bf16[16,16,1024]{2,1,0:T(8,128)(2,1)S(1)}, u32[]{:S(2)}, u32[]{:S(2)}) %collective-permute-start.2) | collective-permute-done | bytes 524320 | tf_op jit(solution)/shard_map/ppermute | solution.py:23
  193.8 1.4 add_convert_fusion.1
  195.3 1.1 fusion.36
  196.8 3.2 %gather_fusion = bf16[576,512]{1,0:T(8,128)(2,1)} fusion(bf16[512,512]{1,0:T(8,128)(2,1)S(1)} %broadcast_divide_fusion, s32[1024]{0:T(1024)S(1)} %pad_clamp_fusion.1), kind=kCustom, calls=%fused_computation | custom fusion | bytes 1181952 | tf_op jit(solution)/shard_map/jit(_take)/gather | solution.py:228
  200.0 2.5 %convolution_convert_fusion.3 = bf16[576,256]{1,0:T(8,128)(2,1)S(1)} fusion(bf16[256,512]{1,0:T(8,128)(2,1)S(1)} %copy-done.9, f32[576,512]{1,0:T(8,128)} %copy-done.8, bf16[576,512]{1,0:T(8,128)(2,1)} %gather_fusion, pred[576]{0:T(1024)(128)(4,1)S(1)} %get-tuple-element.23, pred[576]{0:T(1024)(128)(4,1)S(1)} %get-tuple-element.22), kind=kOutput, calls=%fused_computation.47 | convolution fusion | flops 157630464 | bytes 2327680 | tf_op jit(solution)/shard_map/dot_general | solution.py:231
  202.5 0.8 reshape.191
  203.3 2.6 %all-to-all-start.2 = ((bf16[32,18,256]{2,1,0:T(8,128)(2,1)}), bf16[32,18,256]{2,1,0:T(8,128)(2,1)S(1)}, u32[]{:S(2)}, u32[]{:S(2)}) async-start(bf16[32,18,256]{2,1,0:T(8,128)(2,1)} %reshape.191), calls=%async_computation.2 | async-start | bytes 786432 | tf_op jit(solution)/shard_map/all_to_all | solution.py:233
  205.9 8.4 %fusion.20 = bf16[2,4,64,8,64]{2,4,3,1,0:T(8,128)(2,1)} fusion(f32[2,4,8,64,5,64]{5,3,4,2,1,0:T(8,128)} %copy-done.1, bf16[2,4,5,64,8,64]{5,4,3,1,0,2:T(8,128)(2,1)} %reshape.248), kind=kOutput, calls=%fused_computation.40 | convolution fusion | flops 169345024 | bytes 8388608 | tf_op jit(solution)/shard_map/abhqok,abokhd->abqhd/dot_general | solution.py:82
  214.3 2.4 %copy.105 = bf16[2,4,64,8,64]{4,3,2,1,0:T(8,128)(2,1)} copy(bf16[2,4,64,8,64]{2,4,3,1,0:T(8,128)(2,1)} %fusion.20) | data formatting | bytes 1048576 | tf_op jit(solution)/shard_map/convert_element_type | solution.py:85
  216.7 1.9 reshape_reshape.26
  218.7 1.2 fusion.28
  219.9 1.1 fusion.82
  221.1 2.0 gather_fusion.1
  223.1 0.9 select_select_fusion
  (91 shorter events, 3.8 us)
Async XLA Ops:
  0.6 15.0 %copy-start = (bf16[512,512]{1,0:T(8,128)(2,1)S(1)}, bf16[512,512]{1,0:T(8,128)(2,1)}, u32[]{:S(2)}) copy-start(bf16[512,512]{1,0:T(8,128)(2,1)} %param.16) | copy-start | bytes 1572868
  6.8 16.1 %all-to-all-start = ((s32[32,1,18]{2,1,0:T(1,128)}), s32[32,1,18]{2,1,0:T(1,128)S(1)}, u32[]{:S(2)}, u32[]{:S(2)}) async-start(s32[32,1,18]{2,1,0:T(1,128)} %bitcast.4), calls=%async_computation | async-start | bytes 32768 | tf_op jit(solution)/shard_map/all_to_all | solution.py:145
  20.9 21.5 %copy-start.9 = (bf16[256,512]{1,0:T(8,128)(2,1)S(1)}, bf16[256,512]{1,0:T(8,128)(2,1)}, u32[]{:S(2)}) copy-start(bf16[256,512]{1,0:T(8,128)(2,1)} %param.14) | copy-start | bytes 786436
  21.5 21.3 %copy-start.14 = (bf16[16,32,512]{2,1,0:T(8,128)(2,1)S(1)}, bf16[16,32,512]{2,1,0:T(8,128)(2,1)}, u32[]{:S(2)}) copy-start(bf16[16,32,512]{2,1,0:T(8,128)(2,1)} %param.9) | copy-start | bytes 1572868
  23.0 19.4 %all-to-all-start.1 = ((bf16[32,18,256]{2,1,0:T(8,128)(2,1)}), bf16[32,18,256]{2,1,0:T(8,128)(2,1)S(1)}, u32[]{:S(2)}, u32[]{:S(2)}) async-start(bf16[32,18,256]{2,1,0:T(8,128)(2,1)} %reshape.173), calls=%async_computation.1 | async-start | bytes 786432 | tf_op jit(solution)/shard_map/all_to_all | solution.py:144
  42.8 1.1 copy-start.8
  42.8 6.4 %copy-start.11 = (bf16[512,1536]{1,0:T(8,128)(2,1)S(1)}, bf16[512,1536]{1,0:T(8,128)(2,1)}, u32[]{:S(2)}) copy-start(bf16[512,1536]{1,0:T(8,128)(2,1)} %param.15) | copy-start | bytes 4718596
  43.9 0.8 copy-start.3
  45.7 9.1 %collective-permute-start = (bf16[16,16,512]{2,1,0:T(8,128)(2,1)}, bf16[16,16,512]{2,1,0:T(8,128)(2,1)}, u32[]{:S(2)}, u32[]{:S(2)}) collective-permute-start(bf16[16,16,512]{2,1,0:T(8,128)(2,1)} %get-tuple-element.20), channel_id=1, source_target_pairs={{0,1},{1,2},{2,3},{3,4},{4,5},{5,6},{6,7},{7,0},{8,9},{9,10},{10,1... | collective-permute-start | bytes 786440 | tf_op jit(solution)/shard_map/ppermute | solution.py:23
  45.8 9.0 %collective-permute-start.1 = (bf16[16,16,512]{2,1,0:T(8,128)(2,1)}, bf16[16,16,512]{2,1,0:T(8,128)(2,1)}, u32[]{:S(2)}, u32[]{:S(2)}) collective-permute-start(bf16[16,16,512]{2,1,0:T(8,128)(2,1)} %get-tuple-element.21), channel_id=1, source_target_pairs={{1,0},{2,1},{3,2},{4,3},{5,4},{6,5},{7,6},{0,7},{9,8},{10,9},{11,1... | collective-permute-start | bytes 786440 | tf_op jit(solution)/shard_map/ppermute | solution.py:24
  50.2 2.7 %copy-start.7 = (bf16[512,1536]{1,0:T(8,128)(2,1)}, bf16[512,1536]{1,0:T(8,128)(2,1)S(1)}, u32[]{:S(2)}) copy-start(bf16[512,1536]{1,0:T(8,128)(2,1)S(1)} %convolution_convert_fusion) | copy-start | bytes 4718596
  52.9 3.0 %copy-start.12 = (bf16[512,1536]{1,0:T(8,128)(2,1)S(1)}, bf16[512,1536]{1,0:T(8,128)(2,1)}, u32[]{:S(2)}) copy-start(bf16[512,1536]{1,0:T(8,128)(2,1)} %param.15) | copy-start | bytes 4718596
  55.9 1.2 slice-start.6
  72.1 8.4 %copy-start.5 = (bf16[2,4,64,8,64,1]{2,4,5,3,1,0:T(8,128)(2,1)S(1)}, bf16[2,4,64,8,64,1]{2,4,5,3,1,0:T(8,128)(2,1)}, u32[]{:S(2)}) copy-start(bf16[2,4,64,8,64,1]{2,4,5,3,1,0:T(8,128)(2,1)} %copy.126) | copy-start | bytes 1572868
  72.1 23.5 %slice-start.2 = ((s8[5242880]{0:T(1024)(128)(4,1)}), s8[1048576]{0:T(1024)(128)(4,1)S(1)}, s32[]{:S(2)}) async-start(s8[5242880]{0:T(1024)(128)(4,1)} %bitcast.164), calls=%async_computation.5 | async-start | bytes 2097152
  80.6 9.8 %copy-start.2 = (bf16[2,4,64,8,64,1]{2,4,5,3,1,0:T(8,128)(2,1)S(1)}, bf16[2,4,64,8,64,1]{2,4,5,3,1,0:T(8,128)(2,1)}, u32[]{:S(2)}) copy-start(bf16[2,4,64,8,64,1]{2,4,5,3,1,0:T(8,128)(2,1)} %copy.127) | copy-start | bytes 1572868
  80.6 15.1 %slice-start.3 = ((s8[5242880]{0:T(1024)(128)(4,1)}), s8[4194304]{0:T(1024)(128)(4,1)S(1)}, s32[]{:S(2)}) async-start(s8[5242880]{0:T(1024)(128)(4,1)} %bitcast.164), calls=%async_computation.6 | async-start | bytes 8388608
  86.3 4.0 %copy-start.1 = (f32[2,4,8,64,5,64]{5,3,4,2,1,0:T(8,128)}, f32[2,4,8,64,5,64]{5,3,4,2,1,0:T(8,128)S(1)}, u32[]{:S(2)}) copy-start(f32[2,4,8,64,5,64]{5,3,4,2,1,0:T(8,128)S(1)} %divide_multiply_fusion) | copy-start | bytes 15728644
  165.4 16.2 %slice-start = ((s8[5242880]{0:T(1024)(128)(4,1)}), s8[1048576]{0:T(1024)(128)(4,1)S(1)}, s32[]{:S(2)}) async-start(s8[5242880]{0:T(1024)(128)(4,1)} %bitcast.162), calls=%async_computation.3 | async-start | bytes 2097152
  165.4 16.2 %slice-start.4 = ((s8[5242880]{0:T(1024)(128)(4,1)}), s8[4194304]{0:T(1024)(128)(4,1)S(1)}, s32[]{:S(2)}) async-start(s8[5242880]{0:T(1024)(128)(4,1)} %bitcast.171), calls=%async_computation.7 | async-start | bytes 8388608
  173.3 8.3 %slice-start.1 = ((s8[5242880]{0:T(1024)(128)(4,1)}), s8[4194304]{0:T(1024)(128)(4,1)S(1)}, s32[]{:S(2)}) async-start(s8[5242880]{0:T(1024)(128)(4,1)} %bitcast.162), calls=%async_computation.4 | async-start | bytes 8388608
  173.3 8.3 %slice-start.5 = ((s8[5242880]{0:T(1024)(128)(4,1)}), s8[1048576]{0:T(1024)(128)(4,1)S(1)}, s32[]{:S(2)}) async-start(s8[5242880]{0:T(1024)(128)(4,1)} %bitcast.171), calls=%async_computation.8 | async-start | bytes 2097152
  178.1 15.7 %collective-permute-start.2 = (bf16[16,16,1024]{2,1,0:T(8,128)(2,1)}, bf16[16,16,1024]{2,1,0:T(8,128)(2,1)S(1)}, u32[]{:S(2)}, u32[]{:S(2)}) collective-permute-start(bf16[16,16,1024]{2,1,0:T(8,128)(2,1)} %get-tuple-element.16), channel_id=1, source_target_pairs={{0,1},{1,2},{2,3},{3,4},{4,5},{5,6},{6,7},{7,0},{8,9},{9,10},{10,1... | collective-permute-start | bytes 1572872 | tf_op jit(solution)/shard_map/ppermute | solution.py:23
  178.1 15.7 %collective-permute-start.3 = (bf16[16,16,1024]{2,1,0:T(8,128)(2,1)}, bf16[16,16,1024]{2,1,0:T(8,128)(2,1)}, u32[]{:S(2)}, u32[]{:S(2)}) collective-permute-start(bf16[16,16,1024]{2,1,0:T(8,128)(2,1)} %get-tuple-element.17), channel_id=1, source_target_pairs={{1,0},{2,1},{3,2},{4,3},{5,4},{6,5},{7,6},{0,7},{9,8},{10,9},{11,1... | collective-permute-start | bytes 1572872 | tf_op jit(solution)/shard_map/ppermute | solution.py:24
  185.1 10.1 %copy-start.4 = (bf16[512,512]{1,0:T(8,128)(2,1)S(1)}, bf16[512,512]{1,0:T(8,128)(2,1)}, u32[]{:S(2)}) copy-start(bf16[512,512]{1,0:T(8,128)(2,1)} %copy-done.3) | copy-start | bytes 1572868
  187.1 8.2 %copy-start.13 = (bf16[512,1536]{1,0:T(8,128)(2,1)S(1)}, bf16[512,1536]{1,0:T(8,128)(2,1)}, u32[]{:S(2)}) copy-start(bf16[512,1536]{1,0:T(8,128)(2,1)} %param.15) | copy-start | bytes 4718596
  195.3 1.1 copy-start.6
  203.3 17.7 %all-to-all-start.2 = ((bf16[32,18,256]{2,1,0:T(8,128)(2,1)}), bf16[32,18,256]{2,1,0:T(8,128)(2,1)S(1)}, u32[]{:S(2)}, u32[]{:S(2)}) async-start(bf16[32,18,256]{2,1,0:T(8,128)(2,1)} %reshape.191), calls=%async_computation.2 | async-start | bytes 786432 | tf_op jit(solution)/shard_map/all_to_all | solution.py:233
  221.0 2.1 copy-start.10
where the time goes:
time: 226 us; the launch traced here: 224 us
  local copies, waits for them, and re-layouts  120 us (53%)
  matrix products  47.2 us (21%)
  starting transfers between devices  22.8 us (10%)
  waiting for transfers between devices  18.9 us (8%)
  other arithmetic  13.3 us (6%)
    reshape x2, local copies, waits for them, and re-layouts, attend(): key_heads = key_rows[..., :channels].reshape(key_shape)  13 us
    all_to_all x1, waiting for transfers between devices, shards(): lax.all_to_all(payload_cube, ('lat', 'lon'), split_axis=0, concat_axis=0,...  11.8 us
    transpose x1, local copies, waits for them, and re-layouts, attend(): jnp.einsum('abhqok,abqhd->abokhd', weights_bf, grad_split, preferred_elem...  11.3 us
    transpose x1, local copies, waits for them, and re-layouts, attend(): jnp.einsum('abhqok,abqhd->abokhd', grad_scores, query_heads, preferred_el...  11.2 us
    unnamed x47, local copies, waits for them, and re-layouts  11 us
    reshape x1, local copies, waits for them, and re-layouts, attend(): grad_key.reshape(flat_shape)  9.51 us
    reshape x1, local copies, waits for them, and re-layouts, attend(): grad_value.reshape(flat_shape)  9.46 us
    dot_general x1, matrix products, attend(): jnp.einsum('abqhd,abokhd->abhqok', grad_split, value_heads, preferred_ele...  8.67 us
  transfers between devices with their start and end apart: 7, of which 3 were waited for; matrix products, arithmetic and copies ran while one was open for 16% of the time, Pallas kernels for 0%

commit v1 on v0

v1 whole, which is shorter than its diff:
```python
import functools
import math

import jax
import jax.numpy as jnp
from jax import lax
from jax.experimental import pallas as pl
from jax.experimental.pallas import tpu as pltpu
from jax.sharding import PartitionSpec as P

HEADS = 8
BLOCK = 8
HALF = 2 * BLOCK
TILE = BLOCK * HALF
SLAB = 128
MASKED = -1e30

norm_eps = 1e-06
gelu_coef = 0.7978845608028654

bf16 = jnp.bfloat16
f32 = jnp.float32
i32 = jnp.int32


def iota(shape, dim):
    return lax.broadcasted_iota(i32, shape, dim)


def mm(lhs, rhs, lhs_dim=1, rhs_dim=0):
    return lax.dot_general(
        lhs, rhs, (((lhs_dim,), (rhs_dim,)), ((), ())), preferred_element_type=f32
    )


def one_hot(cond):
    return jnp.where(cond, 1.0, 0.0).astype(bf16)


def gelu_parts(inputs):
    square = inputs * inputs
    tangent = jnp.tanh(gelu_coef * inputs * (1.0 + 0.044715 * square))
    return square, tangent


def call(body, outs, scratch=(), flops=0, n_smem=(), n_in=0, size=1 << 20):
    in_specs = [
        pl.BlockSpec(memory_space=pltpu.SMEM if k in n_smem else pltpu.VMEM) for k in range(n_in)
    ]
    return pl.pallas_call(
        body,
        out_shape=[jax.ShapeDtypeStruct(s, d) for s, d in outs],
        in_specs=in_specs,
        out_specs=[pl.BlockSpec(memory_space=pltpu.VMEM) for _ in outs],
        scratch_shapes=list(scratch),
        compiler_params=pltpu.CompilerParams(vmem_limit_bytes=40 << 20),
        cost_estimate=pl.CostEstimate(flops=flops, bytes_accessed=size, transcendentals=0),
    )


def chunk(ref, row_block, half):
    part = ref[
        row_block * BLOCK : (row_block + 1) * BLOCK, half * HALF : (half + 1) * HALF, :
    ]
    return part.reshape(TILE, part.shape[-1])


def halves():
    return [(i, u) for i in range(2) for u in range(2)]


def rows_of(i, u):
    return slice((i * 2 + u) * TILE, (i * 2 + u + 1) * TILE)


def key_count(pat, i, b):
    return 1 + pat[i, b, 0] + pat[i, b, 1] + pat[i, b, 2] + pat[i, b, 3]


def mask_value(pat, i, b, shift):
    if abs(shift) > 2:
        return jnp.int32(0)
    if shift == 0:
        return jnp.int32(1)
    return pat[i, b, shift + 2 if shift < 0 else shift + 1]


def half_bias(count):
    bias = jnp.float32(-0.5 * math.log(64.0))
    for n in range(2, 6):
        bias = jnp.where(count == n, jnp.float32(-0.5 * math.log(64.0 * n)), bias)
    return bias


def own_bias(pat, i, u, turn):
    second_q = iota((TILE, TILE), 0) % HALF >= BLOCK
    second_k = iota((TILE, TILE), 1) % HALF >= BLOCK
    parts = []
    for qb in range(2):
        bias = half_bias(key_count(pat, i, 2 * u + qb))
        pair = [
            jnp.where(mask_value(pat, i, 2 * u + qb, 2 * turn + kb - qb) > 0, bias, MASKED)
            for kb in range(2)
        ]
        parts.append(jnp.where(second_k, pair[1], pair[0]))
    return jnp.where(second_q, parts[1], parts[0])


def pack_body(geo, pix_ref, cnt_ref, pat_ref, rows_ref, cot_ref, pay_ref, slot_ref, east_ref, west_ref):
    devs, cap, span, lon_bits, lon_devs = geo
    slots = pix_ref.shape[1]
    pix = pix_ref[...]
    lat = lax.shift_right_logical(pix, lon_bits)
    lon = lax.bitwise_and(pix, (1 << lon_bits) - 1)
    owner = lax.shift_right_logical(lat, 4) * lon_devs + lax.shift_right_logical(lon, 5)
    row = lax.bitwise_and(lat, 15)
    col = lax.bitwise_and(lon, 31)
    code = (
        lax.shift_right_logical(row, 3) * (2 * TILE)
        + lax.shift_right_logical(col, 4) * TILE
        + lax.bitwise_and(row, 7) * HALF
        + lax.bitwise_and(col, 15)
        + 1
    )
    live = iota((1, slots), 1) < cnt_ref[0]
    table = (iota((devs, slots), 0) == owner) & live
    table_f = jnp.where(table, 1.0, 0.0)
    table_b = table_f.astype(bf16)
    upper = one_hot(iota((slots, slots), 0) <= iota((slots, slots), 1))
    running = mm(table_b, upper)
    rank = (jnp.sum(running * table_f, axis=0, keepdims=True) - 1.0).astype(i32)
    slot = jnp.where(live, owner * span + rank, -1)
    slot_ref[...] = slot
    spread = one_hot(iota((devs * span, slots), 0) == slot)
    high = lax.shift_right_logical(code, 5).astype(f32)
    low = lax.bitwise_and(code, 31).astype(f32)
    place = iota((256, slots), 0)
    codes = jnp.where(place == rank, high, 0.0) + jnp.where(place == rank + 128, low, 0.0)
    meta = mm(table_b, codes.astype(bf16), 1, 1)
    lift = one_hot(iota((devs * span, devs), 0) == iota((devs * span, devs), 1) * span + cap)
    pay_ref[...] = (mm(spread, rows_ref[...]) + mm(lift, meta.astype(bf16))).astype(bf16)
    lane = iota((HALF, 4 * TILE), 1)
    line = iota((HALF, 4 * TILE), 0)
    second_k = lane % HALF >= BLOCK
    for ref, u, turn in ((east_ref, 1, 1), (west_ref, 0, -1)):
        extra = jnp.zeros((HALF, 4 * TILE), f32)
        for i in range(2):
            ref[i * TILE : (i + 1) * TILE, :] = chunk(cot_ref, i, u)
            for qb in range(2):
                pair = [
                    mask_value(pat_ref, i, 2 * u + qb, 2 * turn + kb - qb).astype(f32)
                    for kb in range(2)
                ]
                mask = jnp.where(second_k, pair[1], pair[0])
                count = key_count(pat_ref, i, 2 * u + qb).astype(f32)
                here = (line == i) & (lane >= qb * TILE) & (lane < (qb + 1) * TILE)
                there = (line == i) & (lane >= (qb + 2) * TILE) & (lane < (qb + 3) * TILE)
                extra = jnp.where(here, mask, jnp.where(there, count, extra))
        ref[2 * TILE : 2 * TILE + HALF, :] = extra.astype(bf16)


def grad_body(cot_ref, west_ref, east_ref, wout_ref, gm_ref, gmt_ref, gw_ref, gwt_ref, ge_ref, get_ref, bw_ref, be_ref):
    wout = wout_ref[...]
    for i, u in halves():
        part = mm(chunk(cot_ref, i, u), wout, 1, 1)
        gm_ref[rows_of(i, u), :] = part.astype(bf16)
        gmt_ref[:, rows_of(i, u)] = part.T.astype(bf16)
    second_q = iota((TILE, TILE), 0) % HALF >= BLOCK
    for src, dst, dst_t, bias_ref in ((west_ref, gw_ref, gwt_ref, bw_ref), (east_ref, ge_ref, get_ref, be_ref)):
        part = mm(src[0 : 2 * TILE, :], wout, 1, 1)
        dst[...] = part.astype(bf16)
        dst_t[...] = part.T.astype(bf16)
        extra = src[2 * TILE : 2 * TILE + HALF, :].astype(f32)
        for i in range(2):
            line = extra[i : i + 1, :]
            mask = jnp.where(second_q, line[:, TILE : 2 * TILE], line[:, 0:TILE])
            count = jnp.where(second_q, line[:, 3 * TILE : 4 * TILE], line[:, 2 * TILE : 3 * TILE])
            bias = -0.5 * jnp.log(count * 64.0)
            bias_ref[i * TILE : (i + 1) * TILE, :] = jnp.where(mask > 0.5, bias, MASKED)


def state_body(geo, arr_ref, wenc_ref, bg_ref, state_ref, n_ref, n0_ref, n1_ref, inv_ref, oht_ref):
    devs, cap, span = geo
    slots = devs * span
    arr = arr_ref[...]
    pick = one_hot(iota((devs, slots), 1) == iota((devs, slots), 0) * span + cap)
    meta = mm(pick, arr).astype(bf16)
    owner = one_hot(iota((devs, span, devs), 0) == iota((devs, span, devs), 2)).reshape(slots, devs)
    wide = mm(owner, meta)
    here = (iota((devs, span, 128), 1) == iota((devs, span, 128), 2)).reshape(slots, 128)
    code = jnp.sum(
        jnp.where(here, wide[:, 0:128] * 32.0 + wide[:, 128:256], 0.0), axis=1, keepdims=True
    ).astype(i32)
    pixels = n_ref.shape[0]
    oht = one_hot(code == iota((slots, pixels), 1) + 1)
    oht_ref[...] = oht
    pre = mm(arr, wenc_ref[...])
    _, tangent = gelu_parts(pre)
    encoded = (0.5 * pre * (1.0 + tangent)).astype(bf16)
    obs_sum = mm(oht, encoded, 0, 0)
    number = mm(oht, jnp.ones((slots, 128), bf16), 0, 0)
    inverse = 1.0 / (1.0 + number)
    inv_ref[...] = inverse
    for i, u in halves():
        rows = rows_of(i, u)
        fresh = obs_sum[rows] * inverse[rows, 0:1]
        state = (chunk(bg_ref, i, u).astype(f32) + fresh).astype(bf16)
        state_ref[rows, :] = state
        wide_state = state.astype(f32)
        inv_rms = lax.rsqrt(jnp.mean(wide_state * wide_state, axis=1, keepdims=True) + norm_eps)
        normed = (wide_state * inv_rms).astype(bf16)
        n_ref[rows, :] = normed
        side = n1_ref if u else n0_ref
        side[i * TILE : (i + 1) * TILE, :] = normed


def head_lanes(shape, head, dim=1):
    return lax.shift_right_logical(iota(shape, dim), 6) == head


def split_heads(slab):
    return [jnp.where(head_lanes(slab.shape, h), slab, jnp.zeros((), slab.dtype)) for h in range(2)]


def weigh(q2, g2, km, vm, bias):
    tangent = jnp.tanh(mm(q2, km, 1, 1) + bias)
    weight = tangent + 1.0
    slope = mm(g2, vm, 1, 1) * weight * (2.0 - weight)
    return weight.astype(bf16), slope.astype(bf16)


def own_body(
    n_ref, wqkv_ref, gm_ref, gmt_ref, pat_ref, arr_ref, wenc_ref,
    q_ref, qt_ref, k_ref, v_ref, mixed_ref, dq_ref, dkt_ref, dvt_ref, slope_ref,
):
    normed = n_ref[...]
    chans = normed.shape[1]
    queries = mm(normed, wqkv_ref[:, 0:chans]).astype(bf16).astype(f32) * 0.0625
    q_ref[...] = queries.astype(bf16)
    qt_ref[...] = queries.T.astype(bf16)
    k_ref[...] = mm(normed, wqkv_ref[:, chans : 2 * chans]).astype(bf16)
    v_ref[...] = mm(normed, wqkv_ref[:, 2 * chans : 3 * chans]).astype(bf16)
    for i in range(2):
        keys = slice(i * 2 * TILE, (i + 1) * 2 * TILE)
        bias = [
            jnp.concatenate([own_bias(pat_ref, i, u, -u), own_bias(pat_ref, i, u, 1 - u)], axis=1)
            for u in range(2)
        ]
        bias = jnp.concatenate(bias, axis=0)
        for s in range(chans // SLAB):
            lanes = slice(s * SLAB, (s + 1) * SLAB)
            km = split_heads(k_ref[keys, lanes])
            vm = split_heads(v_ref[keys, lanes])
            mixed = jnp.zeros((2 * TILE, SLAB), f32)
            grad_q = jnp.zeros((2 * TILE, SLAB), f32)
            for h in range(2):
                weight, slope = weigh(q_ref[keys, lanes], gm_ref[keys, lanes], km[h], vm[h], bias)
                mixed = mixed + mm(weight, vm[h])
                grad_q = grad_q + mm(slope, km[h])
                chan = slice(s * SLAB + h * 64, s * SLAB + (h + 1) * 64)
                dkt_ref[chan, keys] = mm(qt_ref[chan, keys], slope)
                dvt_ref[chan, keys] = mm(gmt_ref[chan, keys], weight)
            mixed_ref[keys, lanes] = mixed
            dq_ref[keys, lanes] = grad_q
    pre = mm(arr_ref[...], wenc_ref[...])
    square, tangent = gelu_parts(pre)
    slope_ref[...] = 0.5 * (1.0 + tangent) + 0.5 * pre * (1.0 - tangent * tangent) * gelu_coef * (
        1.0 + 3.0 * 0.044715 * square
    )


def rim_body(
    nw_ref, ne_ref, wqkv_ref, q_ref, k_ref, v_ref, gm_ref, gw_ref, gwt_ref, ge_ref, get_ref,
    bw_ref, be_ref, pat_ref, mixed_ref, dq_ref, dkt_ref, dvt_ref, state_ref, cot_ref, inv_ref,
    oht_ref, slope_ref, wenc_ref,
    mout_ref, gback_ref, reply_ref,
    rim_q, rim_qt, rim_k, rim_v, gq, gkt, gvt,
):
    chans = q_ref.shape[1]
    for side, src in enumerate((nw_ref, ne_ref)):
        rows = slice(side * 2 * TILE, (side + 1) * 2 * TILE)
        normed = src[...]
        queries = mm(normed, wqkv_ref[:, 0:chans]).astype(bf16).astype(f32) * 0.0625
        rim_q[rows, :] = queries.astype(bf16)
        rim_qt[:, rows] = queries.T.astype(bf16)
        rim_k[rows, :] = mm(normed, wqkv_ref[:, chans : 2 * chans]).astype(bf16)
        rim_v[rows, :] = mm(normed, wqkv_ref[:, 2 * chans : 3 * chans]).astype(bf16)
    for i in range(2):
        for side, (gh_ref, ght_ref, bias_ref) in enumerate(
            ((gw_ref, gwt_ref, bw_ref), (ge_ref, get_ref, be_ref))
        ):
            own = rows_of(i, side)
            far = slice((side * 2 + i) * TILE, (side * 2 + i + 1) * TILE)
            near = slice(i * TILE, (i + 1) * TILE)
            out_bias = own_bias(pat_ref, i, side, 2 * side - 1)
            in_bias = bias_ref[near, :]
            for s in range(chans // SLAB):
                lanes = slice(s * SLAB, (s + 1) * SLAB)
                km = split_heads(rim_k[far, lanes])
                vm = split_heads(rim_v[far, lanes])
                kin = split_heads(k_ref[own, lanes])
                vin = split_heads(v_ref[own, lanes])
                mixed = mixed_ref[own, lanes]
                grad_q = dq_ref[own, lanes]
                for h in range(2):
                    weight, slope = weigh(q_ref[own, lanes], gm_ref[own, lanes], km[h], vm[h], out_bias)
                    mixed = mixed + mm(weight, vm[h])
                    grad_q = grad_q + mm(slope, km[h])
                    weight, slope = weigh(rim_q[far, lanes], gh_ref[near, lanes], kin[h], vin[h], in_bias)
                    chan = slice(s * SLAB + h * 64, s * SLAB + (h + 1) * 64)
                    gkt[chan, own] = (
                        (dkt_ref[chan, own] + mm(rim_qt[chan, far], slope)) * 0.5
                    ).astype(bf16)
                    gvt[chan, own] = (
                        (dvt_ref[chan, own] + mm(ght_ref[chan, near], weight)) * 0.5
                    ).astype(bf16)
                mout_ref[own, lanes] = (mixed * 0.5).astype(bf16)
                gq[own, lanes] = (grad_q * 0.03125).astype(bf16)
    grad_normed = (
        mm(gq[...], wqkv_ref[:, 0:chans], 1, 1)
        + mm(gkt[...], wqkv_ref[:, chans : 2 * chans], 0, 1)
        + mm(gvt[...], wqkv_ref[:, 2 * chans : 3 * chans], 0, 1)
    )
    scaled = []
    for i, u in halves():
        rows = rows_of(i, u)
        state = state_ref[rows, :].astype(f32)
        inv_rms = lax.rsqrt(jnp.mean(state * state, axis=1, keepdims=True) + norm_eps)
        normed = state * inv_rms
        grad = grad_normed[rows]
        grad_state = chunk(cot_ref, i, u).astype(f32) + inv_rms * (
            grad - normed * jnp.mean(grad * normed, axis=1, keepdims=True)
        )
        gback_ref[i * BLOCK : (i + 1) * BLOCK, u * HALF : (u + 1) * HALF, :] = grad_state.astype(
            bf16
        ).reshape(BLOCK, HALF, chans)
        scaled.append((grad_state * inv_ref[rows, 0:1]).astype(bf16))
    grad_enc = mm(oht_ref[...], jnp.concatenate(scaled, axis=0))
    grad_pre = (grad_enc * slope_ref[...]).astype(bf16)
    reply_ref[...] = mm(grad_pre, wenc_ref[...], 1, 1).astype(bf16)


def out_body(mixed_ref, wout_ref, state_ref, out_ref):
    chans = wout_ref.shape[0]
    for i, u in halves():
        rows = rows_of(i, u)
        total = state_ref[rows, :].astype(f32) + mm(mixed_ref[rows, :], wout_ref[...])
        out_ref[i * BLOCK : (i + 1) * BLOCK, u * HALF : (u + 1) * HALF, :] = total.astype(
            bf16
        ).reshape(BLOCK, HALF, chans)


def unpack_body(back_ref, slot_ref, out_ref):
    total = back_ref.shape[0]
    slots = slot_ref.shape[1]
    spread = one_hot(iota((total, slots), 0) == slot_ref[...])
    out_ref[...] = mm(spread, back_ref[...], 0, 0).astype(bf16)


def shards(
    background, obs_rows, obs_pixel, obs_count, block_pattern, w_enc, w_qkv, w_out, cotangent
):
    lat_rows, lon_cols, chans = background.shape
    pixels = lat_rows * lon_cols
    slots, feats = obs_rows.shape
    lon_devs = lax.axis_size("lon")
    devs = lax.axis_size("lat") * lon_devs
    cap = (slots + devs - 1) // devs + 2
    span = (cap + 1 + 7) // 8 * 8
    total = devs * span
    lon_bits = (lon_cols * lon_devs).bit_length() - 1
    side = pixels // 2
    up = [(i, (i + 1) % lon_devs) for i in range(lon_devs)]
    down = [(j, i) for i, j in up]

    payload, slot, cot_east, cot_west = call(
        functools.partial(pack_body, (devs, cap, span, lon_bits, lon_devs)),
        [
            ((total, feats), bf16),
            ((1, slots), i32),
            ((side + HALF, chans), bf16),
            ((side + HALF, chans), bf16),
        ],
        n_in=5,
        n_smem=(1, 2),
        flops=400 << 20,
    )(obs_pixel.reshape(1, slots), obs_count, block_pattern, obs_rows, cotangent)
    arrived = lax.all_to_all(
        payload.reshape(devs, span, feats), ("lat", "lon"), split_axis=0, concat_axis=0, tiled=True
    ).reshape(total, feats)
    west_cot = lax.ppermute(cot_east, "lon", up)
    east_cot = lax.ppermute(cot_west, "lon", down)
    gm, gmt, gw, gwt, ge, get, bias_w, bias_e = call(
        grad_body,
        [
            ((pixels, chans), bf16),
            ((chans, pixels), bf16),
            ((side, chans), bf16),
            ((chans, side), bf16),
            ((side, chans), bf16),
            ((chans, side), bf16),
            ((side, TILE), f32),
            ((side, TILE), f32),
        ],
        n_in=4,
        flops=1 << 30,
    )(cotangent, west_cot, east_cot, w_out)
    state, normed, n0, n1, inverse, oht = call(
        functools.partial(state_body, (devs, cap, span)),
        [
            ((pixels, chans), bf16),
            ((pixels, chans), bf16),
            ((side, chans), bf16),
            ((side, chans), bf16),
            ((pixels, 128), f32),
            ((total, pixels), bf16),
        ],
        n_in=3,
        flops=1 << 30,
    )(arrived, w_enc, background)
    n_west = lax.ppermute(n1, "lon", up)
    n_east = lax.ppermute(n0, "lon", down)
    q, qt, k, v, mixed, dq, dkt, dvt, slope = call(
        own_body,
        [
            ((pixels, chans), bf16),
            ((chans, pixels), bf16),
            ((pixels, chans), bf16),
            ((pixels, chans), bf16),
            ((pixels, chans), f32),
            ((pixels, chans), f32),
            ((chans, pixels), f32),
            ((chans, pixels), f32),
            ((total, chans), f32),
        ],
        n_in=7,
        n_smem=(4,),
        flops=4 << 30,
    )(normed, w_qkv, gm, gmt, block_pattern, arrived, w_enc)
    mixed, grad_background, reply = call(
        rim_body,
        [
            ((pixels, chans), bf16),
            ((lat_rows, lon_cols, chans), bf16),
            ((total, feats), bf16),
        ],
        scratch=[
            pltpu.VMEM((pixels, chans), bf16),
            pltpu.VMEM((chans, pixels), bf16),
            pltpu.VMEM((pixels, chans), bf16),
            pltpu.VMEM((pixels, chans), bf16),
            pltpu.VMEM((pixels, chans), bf16),
            pltpu.VMEM((chans, pixels), bf16),
            pltpu.VMEM((chans, pixels), bf16),
        ],
        n_in=24,
        n_smem=(13,),
        flops=4 << 30,
    )(
        n_west, n_east, w_qkv, q, k, v, gm, gw, gwt, ge, get, bias_w, bias_e, block_pattern,
        mixed, dq, dkt, dvt, state, cotangent, inverse, oht, slope, w_enc,
    )
    returned = lax.all_to_all(
        reply.reshape(devs, span, feats), ("lat", "lon"), split_axis=0, concat_axis=0, tiled=True
    ).reshape(total, feats)
    (updated,) = call(out_body, [((lat_rows, lon_cols, chans), bf16)], n_in=3, flops=1 << 30)(
        mixed, w_out, state
    )
    (grad_obs,) = call(unpack_body, [((slots, feats), bf16)], n_in=2, flops=1 << 28)(returned, slot)
    return (updated, grad_background, grad_obs)


def solution(mesh):
    return jax.shard_map(
        shards,
        mesh=mesh,
        in_specs=(
            P("lat", "lon", None),
            P(("lat", "lon"), None),
            P(("lat", "lon")),
            P(("lat", "lon")),
            P("lat", "lon", None),
            P(),
            P(),
            P(),
            P("lat", "lon", None),
        ),
        out_specs=(P("lat", "lon", None), P("lat", "lon", None), P(("lat", "lon"), None)),
        check_vma=False,
    )
```

time: 226 us -> 84.3 us (0.37)
  local copies, waits for them, and re-layouts: 120 us -> 8.47 us
  matrix products: 47.2 us -> 0 us
  Pallas kernels: 0 us -> 31.5 us
  other arithmetic: 13.3 us -> 0 us
  waiting for transfers between devices: 18.9 us -> 25.2 us
  starting transfers between devices: 22.8 us -> 17.3 us
    dot_general x14 -> x0, matrix products: 47.2 us -> none  [the longest x1 8.67 us: attend(): jnp.einsum('abqhd,abokhd->abhqok', grad_split, value_heads, preferred_ele...]
    reshape x9 -> x0, local copies, waits for them, and re-layouts: 41.2 us -> none  [the longest x2 13 us: attend(): key_heads = key_rows[..., :channels].reshape(key_shape)]
    pallas_call x0 -> x7, Pallas kernels: none -> 31.5 us  [the longest x1 16.3 us: shards(): call(rim_body, [((pixels, chans), bf16), ((lat_rows, lon_cols, chans), bf...]
    transpose x5 -> x0, local copies, waits for them, and re-layouts: 22.8 us -> none  [the longest x1 11.3 us: attend(): jnp.einsum('abhqok,abqhd->abokhd', weights_bf, grad_split, preferred_elem...]
    another operation x11 -> x0, local copies, waits for them, and re-layouts: 10.2 us -> none  [the longest x2 3.84 us: from_blocks(): shaped = blocks.reshape(row_blocks, col_blocks, BLOCK, BLOCK, depth_dim)]
    squeeze x1 -> x0, local copies, waits for them, and re-layouts: 7.9 us -> none  [shards(): contrib[:, :, 0]]
    concatenate x2 -> x0, local copies, waits for them, and re-layouts: 5.87 us -> none  [the longest x1 5.8 us: attend(): jnp.concatenate([grad_key.reshape(flat_shape), grad_value.reshape(flat_sh...]
    ppermute x4, waiting for transfers between devices: 7.06 us -> 12.9 us  [the longest x1 12.9 us: shards(): west_cot = lax.ppermute(cot_east, 'lon', up)]
  transfers between devices with their start and end apart: 7 -> 6, of which waited for: 3 -> 2; matrix products, arithmetic and copies ran while one was open for 16% -> 0% of each run, Pallas kernels for 0% -> 12%
where the time goes in v1:
time: 84.3 us; the launch traced here: 83.9 us
  Pallas kernels  31.5 us (37%)
  waiting for transfers between devices  25.2 us (30%)
  starting transfers between devices  17.3 us (21%)
  local copies, waits for them, and re-layouts  8.47 us (10%)
  between operations  1.47 us (2%)
    pallas_call x1, Pallas kernels, shards(): call(rim_body, [((pixels, chans), bf16), ((lat_rows, lon_cols, chans), bf...  16.3 us
    ppermute x1, waiting for transfers between devices, shards(): west_cot = lax.ppermute(cot_east, 'lon', up)  12.9 us
    all_to_all x1, waiting for transfers between devices, shards(): lax.all_to_all(reply.reshape(devs, span, feats), ('lat', 'lon'), split_ax...  12.3 us
    unnamed x48, local copies, waits for them, and re-layouts  8.47 us
    pallas_call x1, Pallas kernels, shards(): call(own_body, [((pixels, chans), bf16), ((chans, pixels), bf16), ((pixel...  7.31 us
    all_to_all x1, starting transfers between devices, shards(): lax.all_to_all(payload.reshape(devs, span, feats), ('lat', 'lon'), split_...  7.3 us
    ppermute x1, starting transfers between devices, shards(): n_east = lax.ppermute(n0, 'lon', down)  3.53 us
    ppermute x1, starting transfers between devices, shards(): east_cot = lax.ppermute(cot_west, 'lon', down)  3.29 us
  transfers between devices with their start and end apart: 6, of which 2 were waited for; matrix products, arithmetic and copies ran while one was open for 0% of the time, Pallas kernels for 12%

profile of v1, /device:TPU:0, one launch (start us, length us, event | category | flops | bytes accessed | tf_op | source)
XLA Modules:
  0.0 83.9 jit_solution(7516679861597124574)
XLA Ops:
  1.3 0.0 copy-start.2
  1.3 1.0 %copy-done.2 = bf16[16,32,512]{2,1,0:T(8,128)(2,1)S(1)} copy-done((bf16[16,32,512]{2,1,0:T(8,128)(2,1)S(1)}, bf16[16,32,512]{2,1,0:T(8,128)(2,1)}, u32[]{:S(2)}) %copy-start.2) | copy-done | bytes 524312
  2.3 0.0 copy-start.5
  2.3 0.9 %copy-done.5 = bf16[512,256]{1,0:T(8,128)(2,1)S(1)} copy-done((bf16[512,256]{1,0:T(8,128)(2,1)S(1)}, bf16[512,256]{1,0:T(8,128)(2,1)}, u32[]{:S(2)}) %copy-start.5) | copy-done | bytes 262168
  3.3 0.0 copy-start.7
  3.3 0.7 copy-done.7
  4.0 0.0 copy-start.9
  4.0 0.7 copy-done.9
  4.6 0.0 copy-start.3
  4.6 0.0 copy-start.4
  4.6 2.3 %shard_map.112 = (bf16[768,256]{1,0:T(8,128)(2,1)}, s32[1,512]{1,0:T(1,128)S(1)}, bf16[272,512]{1,0:T(8,128)(2,1)S(1)}, bf16[272,512]{1,0:T(8,128)(2,1)S(1)}) custom-call(s32[1,512]{1,0:T(1,128)S(1)} %bitcast.8, s32[1]{0:T(128)S(6)} %copy.12.cnt_ref, s32[2,4,4]{2,1,0:T(4,128)S(1)} %copy-done.7, bf16[512,256]{1,0:T(8,128)(2,1)S(1)} %copy-done.5, ...), custom_call_target="tpu_custom_call" | custom-call | flops 419430400 | bytes 1048576 | tf_op jit(solution)/shard_map/pallas_call | solution.py:376
  6.9 7.3 %all-to-all-start = ((bf16[32,24,256]{2,1,0:T(8,128)(2,1)}), bf16[32,24,256]{2,1,0:T(8,128)(2,1)S(1)}, u32[]{:S(2)}, u32[]{:S(2)}) async-start(bf16[32,24,256]{2,1,0:T(8,128)(2,1)} %bitcast.1), calls=%async_computation | async-start | bytes 786432 | tf_op jit(solution)/shard_map/all_to_all | solution.py:388
  14.2 0.3 collective-permute-start.2
  14.5 0.0 copy-start.1
  14.5 0.0 copy-start.6
  14.5 3.3 %collective-permute-start.3 = (bf16[272,512]{1,0:T(8,128)(2,1)S(1)}, bf16[272,512]{1,0:T(8,128)(2,1)S(1)}, u32[]{:S(2)}, u32[]{:S(2)}) collective-permute-start(bf16[272,512]{1,0:T(8,128)(2,1)S(1)} %get-tuple-element.37), channel_id=1, source_target_pairs={{1,0},{2,1},{3,2},{4,3},{5,4},{6,5},{7,6},{0,7},{9,8},{10,9},{11,1... | collective-permute-start | bytes 835592 | tf_op jit(solution)/shard_map/ppermute | solution.py:392
  17.8 12.9 %collective-permute-done.2.west_ref = bf16[272,512]{1,0:T(8,128)(2,1)S(1)} collective-permute-done((bf16[272,512]{1,0:T(8,128)(2,1)S(1)}, bf16[272,512]{1,0:T(8,128)(2,1)S(1)}, u32[]{:S(2)}, u32[]{:S(2)}) %collective-permute-start.2) | collective-permute-done | bytes 278560 | tf_op jit(solution)/shard_map/ppermute | solution.py:391
  30.8 0.0 collective-permute-done.3.east_ref
  30.8 0.0 copy-done.3
  30.8 0.0 copy-done.4
  30.8 1.2 %shard_map.114 = (bf16[512,512]{1,0:T(8,128)(2,1)S(1)}, bf16[512,512]{1,0:T(8,128)(2,1)S(1)}, bf16[256,512]{1,0:T(8,128)(2,1)S(1)}, bf16[512,256]{1,0:T(8,128)(2...) custom-call(bf16[16,32,512]{2,1,0:T(8,128)(2,1)S(1)} %copy-done.3, ...), custom_call_target="tpu_custom_call" | custom-call | flops 1073741824 | bytes 1048576 | tf_op jit(solution)/shard_map/pallas_call | solution.py:393
  32.0 0.0 copy-start.10
  32.0 0.8 copy-done.10
  32.8 0.8 copy-done.12
  33.6 0.0 copy-start.14
  33.6 0.7 copy-done.14
  34.3 0.0 copy-start.16
  34.3 0.7 copy-done.16
  35.0 0.0 copy-start.18
  35.0 0.7 copy-done.18
  35.7 0.7 copy-done.20
  36.4 0.6 copy-done.22
  37.1 0.0 all-to-all-done
  37.1 0.0 copy-done.1
  37.1 0.0 copy-done.6
  37.1 0.0 copy-start
  37.1 0.0 copy-start.8
  37.1 0.0 copy-start.11
  37.1 0.0 copy-start.13
  37.1 2.0 %shard_map.113 = (bf16[512,512]{1,0:T(8,128)(2,1)S(1)}, bf16[512,512]{1,0:T(8,128)(2,1)S(1)}, bf16[256,512]{1,0:T(8,128)(2,1)S(1)}, bf16[256,512]{1,0:T(8,128)(2...) custom-call(bf16[768,256]{1,0:T(8,128)(2,1)S(1)} %bitcast.5, bf16[256,512]{1,0:T(8,128)(2,1)S(1)} %copy-done.6, ...), custom_call_target="tpu_custom_call" | custom-call | flops 1073741824 | bytes 1048576 | tf_op jit(solution)/shard_map/pallas_call | solution.py:408
  39.1 0.1 collective-permute-start
  39.2 3.5 %collective-permute-start.1 = (bf16[256,512]{1,0:T(8,128)(2,1)S(1)}, bf16[256,512]{1,0:T(8,128)(2,1)S(1)}, u32[]{:S(2)}, u32[]{:S(2)}) collective-permute-start(bf16[256,512]{1,0:T(8,128)(2,1)S(1)} %get-tuple-element.34), channel_id=1, source_target_pairs={{1,0},{2,1},{3,2},{4,3},{5,4},{6,5},{7,6},{0,7},{9,8},{10,9},{11,1... | collective-permute-start | bytes 786440 | tf_op jit(solution)/shard_map/ppermute | solution.py:422
  42.7 0.0 copy-done
  42.7 0.0 copy-done.8
  42.7 0.0 copy-done.11
  42.7 0.0 copy-done.13
  42.7 0.0 copy-start.15
  42.8 0.0 copy-start.17
  42.8 0.0 copy-start.19
  42.8 0.0 copy-start.21
  42.8 0.0 copy-start.23
  42.8 7.3 %shard_map.115 = (bf16[512,512]{1,0:T(8,128)(2,1)S(1)}, bf16[512,512]{1,0:T(8,128)(2,1)}, bf16[512,512]{1,0:T(8,128)(2,1)S(1)}, bf16[512,512]{1,0:T(8,128)(2,1)S...) custom-call(bf16[512,512]{1,0:T(8,128)(2,1)S(1)} %get-tuple-element., ...), custom_call_target="tpu_custom_call" | custom-call | flops 4294967296 | bytes 1048576 | tf_op jit(solution)/shard_map/pallas_call | solution.py:423
  50.1 0.0 collective-permute-done.nw_ref
  50.1 0.0 collective-permute-done.1.ne_ref
  50.1 0.0 copy-done.15
  50.1 0.0 copy-done.17
  50.1 0.0 copy-done.19
  50.1 0.0 copy-done.21
  50.1 0.0 copy-done.23
  50.2 16.3 %shard_map.116 = (bf16[512,512]{1,0:T(8,128)(2,1)S(1)}, bf16[16,32,512]{2,1,0:T(8,128)(2,1)}, bf16[768,256]{1,0:T(8,128)(2,1)}) custom-call(bf16[256,512]{1,0:T(8,128)(2,1)S(1)} %collective-permute-done.nw_ref, bf16[256,512]{1,0:T(8,128)(2,1)S(1)} %collective-permute-done.1.ne_ref, bf16[512,1536]{1,0:T(8,128)(2,1)S(1)} %copy-done, ...), custom_call_target="tpu_custom_call" | custom-call | flops 4294967296 | bytes 1048576 | tf_op jit(solution)/shard_map/pallas_call | solution.py:440
  66.5 2.8 %all-to-all-start.1 = ((bf16[32,24,256]{2,1,0:T(8,128)(2,1)}), bf16[32,24,256]{2,1,0:T(8,128)(2,1)S(1)}, u32[]{:S(2)}, u32[]{:S(2)}) async-start(bf16[32,24,256]{2,1,0:T(8,128)(2,1)} %bitcast.3), calls=%async_computation.1 | async-start | bytes 786432 | tf_op jit(solution)/shard_map/all_to_all | solution.py:463
  69.3 1.2 %shard_map.117 = bf16[16,32,512]{2,1,0:T(8,128)(2,1)} custom-call(bf16[512,512]{1,0:T(8,128)(2,1)S(1)} %get-tuple-element.57.mixed_ref, bf16[512,512]{1,0:T(8,128)(2,1)S(1)} %copy-done.4, bf16[512,512]{1,0:T(8,128)(2,1)S(1)} %get-tuple-element.53.state_ref), custom_call_target="tpu_custom_call" | custom-call | flops 1073741824 | bytes 1048576 | tf_op jit(solution)/shard_map/pallas_call | solution.py:466
  70.5 12.3 %all-to-all-done.1 = bf16[32,24,256]{2,1,0:T(8,128)(2,1)S(1)} async-done(((bf16[32,24,256]{2,1,0:T(8,128)(2,1)}), bf16[32,24,256]{2,1,0:T(8,128)(2,1)S(1)}, u32[]{:S(2)}, u32[]{:S(2)}) %all-to-all-start.1) | async-done | bytes 393248 | tf_op jit(solution)/shard_map/all_to_all | solution.py:463
  82.8 1.1 %shard_map.118 = bf16[512,256]{1,0:T(8,128)(2,1)} custom-call(bf16[768,256]{1,0:T(8,128)(2,1)S(1)} %bitcast.7, s32[1,512]{1,0:T(1,128)S(1)} %get-tuple-element.60.slot_ref), custom_call_target="tpu_custom_call" | custom-call | flops 268435456 | bytes 1048576 | tf_op jit(solution)/shard_map/pallas_call | solution.py:469
  (3 shorter events, 0.0 us)
Async XLA Ops:
  1.3 1.0 %copy-start.2 = (bf16[16,32,512]{2,1,0:T(8,128)(2,1)S(1)}, bf16[16,32,512]{2,1,0:T(8,128)(2,1)}, u32[]{:S(2)}) copy-start(bf16[16,32,512]{2,1,0:T(8,128)(2,1)} %cot_ref.5) | copy-start | bytes 1572868
  2.3 0.9 %copy-start.5 = (bf16[512,256]{1,0:T(8,128)(2,1)S(1)}, bf16[512,256]{1,0:T(8,128)(2,1)}, u32[]{:S(2)}) copy-start(bf16[512,256]{1,0:T(8,128)(2,1)} %rows_ref.1) | copy-start | bytes 786436
  3.3 0.7 copy-start.7
  4.0 0.7 copy-start.9
  4.6 26.1 %copy-start.3 = (bf16[16,32,512]{2,1,0:T(8,128)(2,1)S(1)}, bf16[16,32,512]{2,1,0:T(8,128)(2,1)}, u32[]{:S(2)}) copy-start(bf16[16,32,512]{2,1,0:T(8,128)(2,1)} %cot_ref.5) | copy-start | bytes 1572868
  4.6 26.1 %copy-start.4 = (bf16[512,512]{1,0:T(8,128)(2,1)S(1)}, bf16[512,512]{1,0:T(8,128)(2,1)}, u32[]{:S(2)}) copy-start(bf16[512,512]{1,0:T(8,128)(2,1)} %wout_ref.3) | copy-start | bytes 1572868
  6.9 30.1 %all-to-all-start = ((bf16[32,24,256]{2,1,0:T(8,128)(2,1)}), bf16[32,24,256]{2,1,0:T(8,128)(2,1)S(1)}, u32[]{:S(2)}, u32[]{:S(2)}) async-start(bf16[32,24,256]{2,1,0:T(8,128)(2,1)} %bitcast.1), calls=%async_computation | async-start | bytes 786432 | tf_op jit(solution)/shard_map/all_to_all | solution.py:388
  14.2 16.5 %collective-permute-start.2 = (bf16[272,512]{1,0:T(8,128)(2,1)S(1)}, bf16[272,512]{1,0:T(8,128)(2,1)S(1)}, u32[]{:S(2)}, u32[]{:S(2)}) collective-permute-start(bf16[272,512]{1,0:T(8,128)(2,1)S(1)} %get-tuple-element.36), channel_id=1, source_target_pairs={{0,1},{1,2},{2,3},{3,4},{4,5},{5,6},{6,7},{7,0},{8,9},{9,10},{10,1... | collective-permute-start | bytes 835592 | tf_op jit(solution)/shard_map/ppermute | solution.py:391
  14.5 22.5 %copy-start.1 = (bf16[16,32,512]{2,1,0:T(8,128)(2,1)S(1)}, bf16[16,32,512]{2,1,0:T(8,128)(2,1)}, u32[]{:S(2)}) copy-start(bf16[16,32,512]{2,1,0:T(8,128)(2,1)} %bg_ref.1) | copy-start | bytes 1572868
  14.5 22.5 %copy-start.6 = (bf16[256,512]{1,0:T(8,128)(2,1)S(1)}, bf16[256,512]{1,0:T(8,128)(2,1)}, u32[]{:S(2)}) copy-start(bf16[256,512]{1,0:T(8,128)(2,1)} %wenc_ref.5) | copy-start | bytes 786436
  14.5 16.2 %collective-permute-start.3 = (bf16[272,512]{1,0:T(8,128)(2,1)S(1)}, bf16[272,512]{1,0:T(8,128)(2,1)S(1)}, u32[]{:S(2)}, u32[]{:S(2)}) collective-permute-start(bf16[272,512]{1,0:T(8,128)(2,1)S(1)} %get-tuple-element.37), channel_id=1, source_target_pairs={{1,0},{2,1},{3,2},{4,3},{5,4},{6,5},{7,6},{0,7},{9,8},{10,9},{11,1... | collective-permute-start | bytes 835592 | tf_op jit(solution)/shard_map/ppermute | solution.py:392
  32.0 0.8 copy-start.10
  32.8 0.8 copy-start.12
  33.6 0.7 copy-start.14
  34.3 0.7 copy-start.16
  35.0 0.7 copy-start.18
  35.7 0.7 copy-start.20
  36.4 0.6 copy-start.22
  37.1 5.6 %copy-start = (bf16[512,1536]{1,0:T(8,128)(2,1)S(1)}, bf16[512,1536]{1,0:T(8,128)(2,1)}, u32[]{:S(2)}) copy-start(bf16[512,1536]{1,0:T(8,128)(2,1)} %wqkv_ref.3) | copy-start | bytes 4718596
  37.1 5.6 %copy-start.8 = (s32[2,4,4]{2,1,0:T(4,128)S(1)}, s32[2,4,4]{2,1,0:T(4,128)}, u32[]{:S(2)}) copy-start(s32[2,4,4]{2,1,0:T(4,128)} %pat_ref.5) | copy-start | bytes 388
  37.1 5.6 %copy-start.11 = (bf16[512,512]{1,0:T(8,128)(2,1)S(1)}, bf16[512,512]{1,0:T(8,128)(2,1)}, u32[]{:S(2)}) copy-start(bf16[512,512]{1,0:T(8,128)(2,1)} %copy-done.10) | copy-start | bytes 1572868
  37.1 5.6 %copy-start.13 = (bf16[512,512]{1,0:T(8,128)(2,1)S(1)}, bf16[512,512]{1,0:T(8,128)(2,1)}, u32[]{:S(2)}) copy-start(bf16[512,512]{1,0:T(8,128)(2,1)} %copy-done.12) | copy-start | bytes 1572868
  39.1 11.0 %collective-permute-start = (bf16[256,512]{1,0:T(8,128)(2,1)S(1)}, bf16[256,512]{1,0:T(8,128)(2,1)S(1)}, u32[]{:S(2)}, u32[]{:S(2)}) collective-permute-start(bf16[256,512]{1,0:T(8,128)(2,1)S(1)} %get-tuple-element.33), channel_id=1, source_target_pairs={{0,1},{1,2},{2,3},{3,4},{4,5},{5,6},{6,7},{7,0},{8,9},{9,10},{10,1... | collective-permute-start | bytes 786440 | tf_op jit(solution)/shard_map/ppermute | solution.py:421
  39.2 10.9 %collective-permute-start.1 = (bf16[256,512]{1,0:T(8,128)(2,1)S(1)}, bf16[256,512]{1,0:T(8,128)(2,1)S(1)}, u32[]{:S(2)}, u32[]{:S(2)}) collective-permute-start(bf16[256,512]{1,0:T(8,128)(2,1)S(1)} %get-tuple-element.34), channel_id=1, source_target_pairs={{1,0},{2,1},{3,2},{4,3},{5,4},{6,5},{7,6},{0,7},{9,8},{10,9},{11,1... | collective-permute-start | bytes 786440 | tf_op jit(solution)/shard_map/ppermute | solution.py:422
  42.7 7.4 %copy-start.15 = (bf16[256,512]{1,0:T(8,128)(2,1)S(1)}, bf16[256,512]{1,0:T(8,128)(2,1)}, u32[]{:S(2)}) copy-start(bf16[256,512]{1,0:T(8,128)(2,1)} %copy-done.14) | copy-start | bytes 786436
  42.8 7.4 %copy-start.17 = (bf16[512,256]{1,0:T(8,128)(2,1)S(1)}, bf16[512,256]{1,0:T(8,128)(2,1)}, u32[]{:S(2)}) copy-start(bf16[512,256]{1,0:T(8,128)(2,1)} %copy-done.16) | copy-start | bytes 786436
  42.8 7.4 %copy-start.19 = (bf16[256,512]{1,0:T(8,128)(2,1)S(1)}, bf16[256,512]{1,0:T(8,128)(2,1)}, u32[]{:S(2)}) copy-start(bf16[256,512]{1,0:T(8,128)(2,1)} %copy-done.18) | copy-start | bytes 786436
  42.8 7.4 %copy-start.21 = (bf16[512,256]{1,0:T(8,128)(2,1)S(1)}, bf16[512,256]{1,0:T(8,128)(2,1)}, u32[]{:S(2)}) copy-start(bf16[512,256]{1,0:T(8,128)(2,1)} %copy-done.20) | copy-start | bytes 786436
  42.8 7.4 %copy-start.23 = (f32[256,128]{1,0:T(8,128)S(1)}, f32[256,128]{1,0:T(8,128)}, u32[]{:S(2)}) copy-start(f32[256,128]{1,0:T(8,128)} %copy-done.22) | copy-start | bytes 393220
  66.5 16.3 %all-to-all-start.1 = ((bf16[32,24,256]{2,1,0:T(8,128)(2,1)}), bf16[32,24,256]{2,1,0:T(8,128)(2,1)S(1)}, u32[]{:S(2)}, u32[]{:S(2)}) async-start(bf16[32,24,256]{2,1,0:T(8,128)(2,1)} %bitcast.3), calls=%async_computation.1 | async-start | bytes 786432 | tf_op jit(solution)/shard_map/all_to_all | solution.py:463

commit v2 on v1

v2 whole, which is shorter than its diff:
```python
import functools
import math

import jax
import jax.numpy as jnp
from jax import lax
from jax.experimental import pallas as pl
from jax.experimental.pallas import tpu as pltpu
from jax.sharding import PartitionSpec as P

HEADS = 8
BLOCK = 8
HALF = 2 * BLOCK
TILE = BLOCK * HALF
SLAB = 128
MASKED = -1e30
GRAD_COST = 1 << 37

norm_eps = 1e-06
gelu_coef = 0.7978845608028654

bf16 = jnp.bfloat16
f32 = jnp.float32
i32 = jnp.int32


def iota(shape, dim):
    return lax.broadcasted_iota(i32, shape, dim)


def mm(lhs, rhs, lhs_dim=1, rhs_dim=0):
    return lax.dot_general(
        lhs, rhs, (((lhs_dim,), (rhs_dim,)), ((), ())), preferred_element_type=f32
    )


def one_hot(cond):
    return jnp.where(cond, 1.0, 0.0).astype(bf16)


def gelu_parts(inputs):
    square = inputs * inputs
    tangent = jnp.tanh(gelu_coef * inputs * (1.0 + 0.044715 * square))
    return square, tangent


def call(
    body, outs, scratch=(), flops=0, n_smem=(), n_hbm=(), out_hbm=(), n_in=0, size=1 << 20, vmem=16
):
    def spec(k, smem, hbm):
        if k in hbm:
            return pl.BlockSpec(memory_space=pltpu.HBM)
        return pl.BlockSpec(memory_space=pltpu.SMEM if k in smem else pltpu.VMEM)

    kernel = pl.pallas_call(
        body,
        out_shape=[
            pltpu.HBM(s, d) if k in out_hbm else jax.ShapeDtypeStruct(s, d)
            for k, (s, d) in enumerate(outs)
        ],
        in_specs=[spec(k, n_smem, n_hbm) for k in range(n_in)],
        out_specs=[spec(k, (), out_hbm) for k in range(len(outs))],
        scratch_shapes=list(scratch),
        compiler_params=pltpu.CompilerParams(vmem_limit_bytes=vmem << 20),
        cost_estimate=pl.CostEstimate(flops=flops, bytes_accessed=size, transcendentals=0),
    )

    def run(*args):
        return kernel(
            *[
                pltpu.with_memory_space_constraint(x, pltpu.HBM) if k in n_hbm else x
                for k, x in enumerate(args)
            ]
        )

    return run


def chunk(ref, row_block, half):
    part = ref[
        row_block * BLOCK : (row_block + 1) * BLOCK, half * HALF : (half + 1) * HALF, :
    ]
    return part.reshape(TILE, part.shape[-1])


def halves():
    return [(i, u) for i in range(2) for u in range(2)]


def rows_of(i, u):
    return slice((i * 2 + u) * TILE, (i * 2 + u + 1) * TILE)


def key_count(pat, i, b):
    return 1 + pat[i, b, 0] + pat[i, b, 1] + pat[i, b, 2] + pat[i, b, 3]


def mask_value(pat, i, b, shift):
    if abs(shift) > 2:
        return jnp.int32(0)
    if shift == 0:
        return jnp.int32(1)
    return pat[i, b, shift + 2 if shift < 0 else shift + 1]


def half_bias(count):
    bias = jnp.float32(-0.5 * math.log(64.0))
    for n in range(2, 6):
        bias = jnp.where(count == n, jnp.float32(-0.5 * math.log(64.0 * n)), bias)
    return bias


def own_bias(pat, i, u, turn):
    second_q = iota((TILE, TILE), 0) % HALF >= BLOCK
    second_k = iota((TILE, TILE), 1) % HALF >= BLOCK
    parts = []
    for qb in range(2):
        bias = half_bias(key_count(pat, i, 2 * u + qb))
        pair = [
            jnp.where(mask_value(pat, i, 2 * u + qb, 2 * turn + kb - qb) > 0, bias, MASKED)
            for kb in range(2)
        ]
        parts.append(jnp.where(second_k, pair[1], pair[0]))
    return jnp.where(second_q, parts[1], parts[0])


def start_copy(src, dst, sem):
    copy = pltpu.make_async_copy(src, dst, sem)
    copy.start()
    return copy


def halo_rows(pat_ref, u, turn, width):
    lane = iota((HALF, width), 1)
    line = iota((HALF, width), 0)
    second_k = lane % HALF >= BLOCK
    extra = jnp.zeros((HALF, width), f32)
    for i in range(2):
        for qb in range(2):
            pair = [
                mask_value(pat_ref, i, 2 * u + qb, 2 * turn + kb - qb).astype(f32)
                for kb in range(2)
            ]
            mask = jnp.where(second_k, pair[1], pair[0])
            count = key_count(pat_ref, i, 2 * u + qb).astype(f32)
            here = (line == i) & (lane >= qb * TILE) & (lane < (qb + 1) * TILE)
            there = (line == i) & (lane >= (qb + 2) * TILE) & (lane < (qb + 3) * TILE)
            extra = jnp.where(here, mask, jnp.where(there, count, extra))
    return extra.astype(bf16)


class Geometry:
    def __init__(self, slots, devs, lon_devs, lon_cols):
        self.devs, self.lon_devs = devs, lon_devs
        self.cap = (slots + devs - 1) // devs + 2
        self.full = self.cap // 8 * 8
        self.rest = self.cap - self.full
        self.shift = 4 if self.rest <= 3 else 8
        self.tail = 2 * self.shift
        self.mark = self.shift - 1
        self.rows = 2 * self.full + self.tail
        self.bulk = devs * self.full
        self.total = self.bulk + devs * self.tail
        self.lon_bits = (lon_cols * lon_devs).bit_length() - 1


def join_slots(geo, ref, feats):
    half = feats // 2
    tail = ref[:, 2 * geo.full : geo.rows, :].reshape(geo.devs * geo.tail, half)
    wide = tail.astype(f32)
    moved = pltpu.roll(wide, wide.shape[0] - geo.shift, 0)
    tail_rows = jnp.concatenate([wide, moved], axis=1).astype(bf16)
    if not geo.full:
        return tail, tail_rows
    first = ref[:, 0 : geo.full, :].reshape(geo.bulk, half)
    second = ref[:, geo.full : 2 * geo.full, :].reshape(geo.bulk, half)
    return tail, jnp.concatenate([jnp.concatenate([first, second], axis=1), tail_rows], axis=0)


def store_bulk(geo, ref, values):
    half = values.shape[1] // 2
    if geo.full:
        ref[:, 0 : geo.full, :] = values[:, 0:half].reshape(geo.devs, geo.full, half)
        ref[:, geo.full : 2 * geo.full, :] = values[:, half:].reshape(geo.devs, geo.full, half)


def slot_index(geo, owner, rank, live):
    place = jnp.where(
        rank < geo.full,
        owner * geo.full + rank,
        geo.bulk + owner * geo.tail + rank - geo.full,
    )
    return jnp.where(live, place, -1)


def pack_body(
    geo, pix_hbm, cnt_ref, rows_hbm, pat_hbm, cot_hbm,
    pay_hbm, slot_ref, east_hbm, west_hbm,
    pix_ref, rows_ref, pat_ref, pay_ref, east_ref, west_ref, sems,
):
    pix_copy = start_copy(pix_hbm, pix_ref, sems.at[0])
    rows_copy = start_copy(rows_hbm, rows_ref, sems.at[1])
    pat_copy = start_copy(pat_hbm, pat_ref, sems.at[2])
    lats = cot_hbm.shape[0]
    sides = ((east_ref, 1, 1), (west_ref, 0, -1))
    cot_copies = [
        start_copy(cot_hbm.at[:, u * HALF : (u + 1) * HALF, :], ref.at[0:lats], sems.at[3 + u])
        for ref, u, _ in sides
    ]
    slots = pix_ref.shape[1]
    upper = one_hot(iota((slots, slots), 0) <= iota((slots, slots), 1))
    pix_copy.wait()
    pix = pix_ref[...]
    lat = lax.shift_right_logical(pix, geo.lon_bits)
    lon = lax.bitwise_and(pix, (1 << geo.lon_bits) - 1)
    owner = lax.shift_right_logical(lat, 4) * geo.lon_devs + lax.shift_right_logical(lon, 5)
    row = lax.bitwise_and(lat, 15)
    col = lax.bitwise_and(lon, 31)
    code = (
        lax.shift_right_logical(row, 3) * (2 * TILE)
        + lax.shift_right_logical(col, 4) * TILE
        + lax.bitwise_and(row, 7) * HALF
        + lax.bitwise_and(col, 15)
        + 1
    )
    live = iota((1, slots), 1) < cnt_ref[0]
    table = (iota((geo.devs, slots), 0) == owner) & live
    table_f = jnp.where(table, 1.0, 0.0)
    table_b = table_f.astype(bf16)
    running = mm(table_b, upper)
    rank = (jnp.sum(running * table_f, axis=0, keepdims=True) - 1.0).astype(i32)
    slot = slot_index(geo, owner, rank, live)
    slot_ref[...] = slot
    high = lax.shift_right_logical(code, 5).astype(f32)
    low = lax.bitwise_and(code, 31).astype(f32)
    place = iota((128, slots), 0)
    codes = jnp.where(place == rank, high, 0.0) + jnp.where(place == rank + 64, low, 0.0)
    meta = mm(table_b, codes.astype(bf16), 1, 1)
    tails = geo.devs * geo.tail
    lift = one_hot(
        iota((tails, geo.devs), 0) == iota((tails, geo.devs), 1) * geo.tail + geo.mark
    )
    lifted = mm(lift, meta.astype(bf16))
    pat_copy.wait()
    for copy, (ref, u, turn) in zip(cot_copies, sides):
        ref[lats] = halo_rows(pat_ref, u, turn, cot_hbm.shape[2])
        copy.wait()
    outs = [
        start_copy(east_ref, east_hbm, sems.at[5]),
        start_copy(west_ref, west_hbm, sems.at[6]),
    ]
    place = iota((tails, slots), 0)
    first = one_hot(place == slot - geo.bulk)
    second = one_hot((place == slot - geo.bulk + geo.shift) & (slot >= geo.bulk))
    rows_copy.wait()
    half = rows_ref.shape[1] // 2
    if geo.full:
        spread = one_hot(iota((geo.bulk, slots), 0) == slot)
        store_bulk(geo, pay_ref, mm(spread, rows_ref[...]).astype(bf16))
    tail = mm(first, rows_ref[:, 0:half]) + mm(second, rows_ref[:, half:]) + lifted
    pay_ref[:, 2 * geo.full : geo.rows, :] = tail.astype(bf16).reshape(geo.devs, geo.tail, half)
    outs.append(start_copy(pay_ref, pay_hbm, sems.at[7]))
    for copy in outs:
        copy.wait()


def grad_body(
    cot_hbm, west_ref, east_ref, wout_hbm,
    gm_hbm, gmt_hbm, gw_hbm, gwt_hbm, ge_hbm, get_hbm, bw_hbm, be_hbm,
    cot_ref, wout_ref,
    gm_ref, gmt_ref, gw_ref, gwt_ref, ge_ref, get_ref, bw_ref, be_ref, in_sems, out_sems,
):
    wout_copy = start_copy(wout_hbm, wout_ref, in_sems.at[0])
    cot_copy = start_copy(cot_hbm, cot_ref, in_sems.at[1])
    wout_copy.wait()
    cot_copy.wait()
    wout = wout_ref[...]
    for i, u in halves():
        part = mm(chunk(cot_ref, i, u), wout, 1, 1)
        gm_ref[rows_of(i, u), :] = part.astype(bf16)
        gmt_ref[:, rows_of(i, u)] = part.T.astype(bf16)
    outs = [
        start_copy(gm_ref, gm_hbm, out_sems.at[0]),
        start_copy(gmt_ref, gmt_hbm, out_sems.at[1]),
    ]
    second_q = iota((TILE, TILE), 0) % HALF >= BLOCK
    for n, (src, dst, dst_t, bias_ref, dst_hbm, dst_t_hbm, bias_hbm) in enumerate(
        (
            (west_ref, gw_ref, gwt_ref, bw_ref, gw_hbm, gwt_hbm, bw_hbm),
            (east_ref, ge_ref, get_ref, be_ref, ge_hbm, get_hbm, be_hbm),
        )
    ):
        rows = src.shape[0] - 1
        part = mm(src[0:rows].reshape(2 * TILE, wout.shape[0]), wout, 1, 1)
        dst[...] = part.astype(bf16)
        dst_t[...] = part.T.astype(bf16)
        extra = src[rows].astype(f32)
        for i in range(2):
            line = extra[i : i + 1, :]
            mask = jnp.where(second_q, line[:, TILE : 2 * TILE], line[:, 0:TILE])
            count = jnp.where(second_q, line[:, 3 * TILE : 4 * TILE], line[:, 2 * TILE : 3 * TILE])
            bias = -0.5 * jnp.log(count * 64.0)
            bias_ref[i * TILE : (i + 1) * TILE, :] = jnp.where(mask > 0.5, bias, MASKED)
        outs += [
            start_copy(dst, dst_hbm, out_sems.at[2 + 3 * n]),
            start_copy(dst_t, dst_t_hbm, out_sems.at[3 + 3 * n]),
            start_copy(bias_ref, bias_hbm, out_sems.at[4 + 3 * n]),
        ]
    for copy in outs:
        copy.wait()


def state_body(geo, arr_ref, wenc_ref, bg_ref, state_ref, n_ref, n0_ref, n1_ref, inv_ref, oht_ref):
    devs, feats = geo.devs, wenc_ref.shape[0]
    tails, arr = join_slots(geo, arr_ref, feats)
    pick = one_hot(
        iota((devs, devs * geo.tail), 1) == iota((devs, devs * geo.tail), 0) * geo.tail + geo.mark
    )
    meta = mm(pick, tails).astype(bf16)
    codes = []
    for base, count in ((0, geo.full), (geo.full, geo.tail)):
        if count:
            owner = one_hot(
                iota((devs, count, devs), 0) == iota((devs, count, devs), 2)
            ).reshape(devs * count, devs)
            wide = mm(owner, meta)
            place = iota((devs, count, 128), 1).reshape(devs * count, 128) + base
            lane = iota((devs * count, 128), 1)
            scale = jnp.where(lane == place, 32.0, 0.0) + jnp.where(lane == place + 64, 1.0, 0.0)
            codes.append(jnp.sum(wide * scale, axis=1, keepdims=True))
    code = jnp.concatenate(codes, axis=0).astype(i32)
    pixels = n_ref.shape[0]
    oht = one_hot(code == iota((geo.total, pixels), 1) + 1)
    oht_ref[...] = oht
    pre = mm(arr, wenc_ref[...])
    _, tangent = gelu_parts(pre)
    encoded = (0.5 * pre * (1.0 + tangent)).astype(bf16)
    obs_sum = mm(oht, encoded, 0, 0)
    number = mm(oht, jnp.ones((geo.total, 128), bf16), 0, 0)
    inverse = 1.0 / (1.0 + number)
    inv_ref[...] = inverse
    for i, u in halves():
        rows = rows_of(i, u)
        fresh = obs_sum[rows] * inverse[rows, 0:1]
        state = (chunk(bg_ref, i, u).astype(f32) + fresh).astype(bf16)
        state_ref[rows, :] = state
        wide_state = state.astype(f32)
        inv_rms = lax.rsqrt(jnp.mean(wide_state * wide_state, axis=1, keepdims=True) + norm_eps)
        normed = (wide_state * inv_rms).astype(bf16)
        n_ref[rows, :] = normed
        side = n1_ref if u else n0_ref
        side[i * TILE : (i + 1) * TILE, :] = normed


def head_lanes(shape, head, dim=1):
    return lax.shift_right_logical(iota(shape, dim), 6) == head


def split_heads(slab):
    return [jnp.where(head_lanes(slab.shape, h), slab, jnp.zeros((), slab.dtype)) for h in range(2)]


def weigh(q2, g2, km, vm, bias):
    tangent = jnp.tanh(mm(q2, km, 1, 1) + bias)
    weight = tangent + 1.0
    slope = mm(g2, vm, 1, 1) * weight * (2.0 - weight)
    return weight.astype(bf16), slope.astype(bf16)


def stack_heads(slab):
    return jnp.concatenate(split_heads(slab), axis=0)


def project(src, wqkv_ref, q_ref, qt_ref, k_ref, v_ref, rows):
    chans = src.shape[1]
    queries = mm(src, wqkv_ref[:, 0:chans]).astype(bf16).astype(f32) * 0.0625
    q_ref[rows, :] = queries.astype(bf16)
    qt_ref[:, rows] = queries.T.astype(bf16)
    k_ref[rows, :] = mm(src, wqkv_ref[:, chans : 2 * chans]).astype(bf16)
    v_ref[rows, :] = mm(src, wqkv_ref[:, 2 * chans : 3 * chans]).astype(bf16)


def own_body(
    geo, n_ref, wqkv_ref, gm_ref, gmt_ref, pat_hbm, arr_ref, wenc_ref, state_ref,
    q_ref, k_ref, v_ref, dq_ref, dkt_ref, dvt_ref, slope_ref, weight_hbm, v_hbm, state_hbm,
    pat_ref, qt_ref, weight_ref, sems,
):
    chans = n_ref.shape[1]
    pat_copy = start_copy(pat_hbm, pat_ref, sems.at[0])
    state_copy = start_copy(state_ref, state_hbm, sems.at[1])
    project(n_ref[...], wqkv_ref, q_ref, qt_ref, k_ref, v_ref, slice(0, n_ref.shape[0]))
    v_copy = start_copy(v_ref, v_hbm, sems.at[2])
    pat_copy.wait()
    for i in range(2):
        keys = slice(i * 2 * TILE, (i + 1) * 2 * TILE)
        bias = [
            jnp.concatenate([own_bias(pat_ref, i, u, -u), own_bias(pat_ref, i, u, 1 - u)], axis=1)
            for u in range(2)
        ]
        bias = jnp.concatenate(bias, axis=0)
        for s in range(chans // SLAB):
            lanes = slice(s * SLAB, (s + 1) * SLAB)
            km = split_heads(k_ref[keys, lanes])
            vm = split_heads(v_ref[keys, lanes])
            grad_q = jnp.zeros((2 * TILE, SLAB), f32)
            for h in range(2):
                weight, slope = weigh(q_ref[keys, lanes], gm_ref[keys, lanes], km[h], vm[h], bias)
                weight_ref[i, 2 * s + h] = weight
                grad_q = grad_q + mm(slope, km[h])
                chan = slice(s * SLAB + h * 64, s * SLAB + (h + 1) * 64)
                dkt_ref[chan, keys] = mm(qt_ref[chan, keys], slope)
                dvt_ref[chan, keys] = mm(gmt_ref[chan, keys], weight)
            dq_ref[keys, lanes] = grad_q
    weight_copy = start_copy(weight_ref, weight_hbm, sems.at[3])
    pre = mm(join_slots(geo, arr_ref, wenc_ref.shape[0])[1], wenc_ref[...])
    square, tangent = gelu_parts(pre)
    slope_ref[...] = 0.5 * (1.0 + tangent) + 0.5 * pre * (1.0 - tangent * tangent) * gelu_coef * (
        1.0 + 3.0 * 0.044715 * square
    )
    for copy in (state_copy, v_copy, weight_copy):
        copy.wait()


def rim_body(
    geo, nw_ref, ne_ref, wqkv_ref, q_ref, k_ref, v_ref, gm_ref, gw_ref, gwt_ref, ge_ref, get_ref,
    bw_ref, be_ref, pat_hbm, dq_ref, dkt_ref, dvt_ref, state_ref, cot_ref, inv_ref,
    oht_ref, slope_ref, wenc_ref,
    v_hbm, weight_hbm, gback_hbm, reply_ref,
    pat_ref, rim_q, rim_qt, rim_k, rim_v, weight_ref, gback_ref, gq, gkt, gvt, sems,
):
    chans = q_ref.shape[1]
    pat_copy = start_copy(pat_hbm, pat_ref, sems.at[0])
    for side, src in enumerate((nw_ref, ne_ref)):
        rows = slice(side * 2 * TILE, (side + 1) * 2 * TILE)
        project(src[...], wqkv_ref, rim_q, rim_qt, rim_k, rim_v, rows)
    v_copy = start_copy(rim_v, v_hbm, sems.at[1])
    pat_copy.wait()
    for i in range(2):
        for side, (gh_ref, ght_ref, bias_ref) in enumerate(
            ((gw_ref, gwt_ref, bw_ref), (ge_ref, get_ref, be_ref))
        ):
            own = rows_of(i, side)
            far = slice((side * 2 + i) * TILE, (side * 2 + i + 1) * TILE)
            near = slice(i * TILE, (i + 1) * TILE)
            out_bias = own_bias(pat_ref, i, side, 2 * side - 1)
            out_bias = jnp.concatenate([out_bias, out_bias], axis=1)
            in_bias = bias_ref[near, :]
            in_bias = jnp.concatenate([in_bias, in_bias], axis=1)
            for s in range(chans // SLAB):
                lanes = slice(s * SLAB, (s + 1) * SLAB)
                km = stack_heads(rim_k[far, lanes])
                vm = stack_heads(rim_v[far, lanes])
                weight, slope = weigh(q_ref[own, lanes], gm_ref[own, lanes], km, vm, out_bias)
                weight_ref[i * 2 + side, s] = weight
                gq[own, lanes] = ((dq_ref[own, lanes] + mm(slope, km)) * 0.03125).astype(bf16)
                km = stack_heads(k_ref[own, lanes])
                vm = stack_heads(v_ref[own, lanes])
                weight, slope = weigh(rim_q[far, lanes], gh_ref[near, lanes], km, vm, in_bias)
                grad_k = mm(rim_qt[lanes, far], slope)
                grad_v = mm(ght_ref[lanes, near], weight)
                for h in range(2):
                    part = slice(h * 64, (h + 1) * 64)
                    cols = slice(h * TILE, (h + 1) * TILE)
                    chan = slice(s * SLAB + h * 64, s * SLAB + (h + 1) * 64)
                    gkt[chan, own] = ((dkt_ref[chan, own] + grad_k[part, cols]) * 0.5).astype(bf16)
                    gvt[chan, own] = ((dvt_ref[chan, own] + grad_v[part, cols]) * 0.5).astype(bf16)
    weight_copy = start_copy(weight_ref, weight_hbm, sems.at[2])
    grad_normed = (
        mm(gq[...], wqkv_ref[:, 0:chans], 1, 1)
        + mm(gkt[...], wqkv_ref[:, chans : 2 * chans], 0, 1)
        + mm(gvt[...], wqkv_ref[:, 2 * chans : 3 * chans], 0, 1)
    )
    scaled = []
    for i, u in halves():
        rows = rows_of(i, u)
        state = state_ref[rows, :].astype(f32)
        inv_rms = lax.rsqrt(jnp.mean(state * state, axis=1, keepdims=True) + norm_eps)
        normed = state * inv_rms
        grad = grad_normed[rows]
        grad_state = chunk(cot_ref, i, u).astype(f32) + inv_rms * (
            grad - normed * jnp.mean(grad * normed, axis=1, keepdims=True)
        )
        gback_ref[rows, :] = grad_state.astype(bf16)
        scaled.append((grad_state * inv_ref[rows, 0:1]).astype(bf16))
    gback_copy = start_copy(gback_ref, gback_hbm, sems.at[3])
    grad_enc = mm(oht_ref[...], jnp.concatenate(scaled, axis=0))
    grad_pre = (grad_enc * slope_ref[...]).astype(bf16)
    reply = mm(grad_pre, wenc_ref[...], 1, 1)
    store_bulk(geo, reply_ref, reply[0 : geo.bulk].astype(bf16))
    tail = reply[geo.bulk :]
    half = tail.shape[1] // 2
    moved = pltpu.roll(tail[:, half:], geo.shift, 0)
    lower = iota((geo.devs * geo.tail, half), 0) % geo.tail < geo.shift
    tail = jnp.where(lower, tail[:, 0:half], moved)
    reply_ref[:, 2 * geo.full : geo.rows, :] = tail.astype(bf16).reshape(geo.devs, geo.tail, half)
    for copy in (v_copy, weight_copy, gback_copy):
        copy.wait()


def out_body(*refs):
    hbm, (out_ref, back_ref), local, (mixed_ref, sems) = refs[:7], refs[7:9], refs[9:16], refs[16:]
    copies = [start_copy(src, dst, sems.at[n]) for n, (src, dst) in enumerate(zip(hbm, local))]
    for copy in copies:
        copy.wait()
    weight_ref, far_ref, v_ref, rim_v, wout_ref, state_ref, gback_ref = local
    chans = wout_ref.shape[0]
    for i in range(2):
        keys = slice(i * 2 * TILE, (i + 1) * 2 * TILE)
        for s in range(chans // SLAB):
            lanes = slice(s * SLAB, (s + 1) * SLAB)
            vm = split_heads(v_ref[keys, lanes])
            mixed = mm(weight_ref[i, 2 * s], vm[0]) + mm(weight_ref[i, 2 * s + 1], vm[1])
            for side in range(2):
                far = slice((side * 2 + i) * TILE, (side * 2 + i + 1) * TILE)
                total = mixed[side * TILE : (side + 1) * TILE] + mm(
                    far_ref[i * 2 + side, s], stack_heads(rim_v[far, lanes])
                )
                mixed_ref[rows_of(i, side), lanes] = (total * 0.5).astype(bf16)
    for i, u in halves():
        rows = rows_of(i, u)
        place = (slice(i * BLOCK, (i + 1) * BLOCK), slice(u * HALF, (u + 1) * HALF))
        total = state_ref[rows, :].astype(f32) + mm(mixed_ref[rows, :], wout_ref[...])
        out_ref[place[0], place[1], :] = total.astype(bf16).reshape(BLOCK, HALF, chans)
        back_ref[place[0], place[1], :] = gback_ref[rows, :].reshape(BLOCK, HALF, chans)


def unpack_body(geo, back_ref, slot_ref, out_ref):
    feats = out_ref.shape[1]
    slots = slot_ref.shape[1]
    spread = one_hot(iota((geo.total, slots), 0) == slot_ref[...])
    out_ref[...] = mm(spread, join_slots(geo, back_ref, feats)[1], 0, 0).astype(bf16)


def shards(
    background, obs_rows, obs_pixel, obs_count, block_pattern, w_enc, w_qkv, w_out, cotangent
):
    lat_rows, lon_cols, chans = background.shape
    pixels = lat_rows * lon_cols
    slots, feats = obs_rows.shape
    lon_devs = lax.axis_size("lon")
    geo = Geometry(slots, lax.axis_size("lat") * lon_devs, lon_devs, lon_cols)
    side = pixels // 2
    half = feats // 2
    up = [(i, (i + 1) % lon_devs) for i in range(lon_devs)]
    down = [(j, i) for i, j in up]

    rim = (lat_rows + 1, HALF, chans)
    wide, tall, edge, edge_t = (pixels, chans), (chans, pixels), (side, chans), (chans, side)
    weights_own = (2, HEADS, 2 * TILE, 2 * TILE)
    weights_far = (4, chans // SLAB, TILE, 2 * TILE)
    dma = pltpu.SemaphoreType.DMA
    pattern = pltpu.SMEM(block_pattern.shape, i32)

    def vmem(*shapes):
        return [pltpu.VMEM(shape, bf16) for shape in shapes]

    payload, slot, cot_east, cot_west = call(
        functools.partial(pack_body, geo),
        [((geo.devs, geo.rows, half), bf16), ((1, slots), i32), (rim, bf16), (rim, bf16)],
        scratch=[pltpu.VMEM((1, slots), i32), pltpu.VMEM((slots, feats), bf16), pattern]
        + vmem((geo.devs, geo.rows, half), rim, rim)
        + [dma((8,))],
        n_in=5,
        n_smem=(1,),
        n_hbm=(0, 2, 3, 4),
        out_hbm=(0, 2, 3),
        flops=400 << 20,
    )(obs_pixel.reshape(1, slots), obs_count, obs_rows, block_pattern, cotangent)
    west_cot = lax.ppermute(cot_east, "lon", up)
    east_cot = lax.ppermute(cot_west, "lon", down)
    arrived = lax.all_to_all(payload, ("lat", "lon"), split_axis=0, concat_axis=0, tiled=True)
    gm, gmt, gw, gwt, ge, get, bias_w, bias_e = call(
        grad_body,
        [
            (wide, bf16),
            (tall, bf16),
            (edge, bf16),
            (edge_t, bf16),
            (edge, bf16),
            (edge_t, bf16),
            ((side, TILE), f32),
            ((side, TILE), f32),
        ],
        scratch=vmem((lat_rows, lon_cols, chans), (chans, chans))
        + vmem(wide, tall, edge, edge_t, edge, edge_t)
        + [pltpu.VMEM((side, TILE), f32)] * 2
        + [dma((2,)), dma((8,))],
        n_in=4,
        n_hbm=(0, 3),
        out_hbm=range(8),
        flops=GRAD_COST,
    )(cotangent, west_cot, east_cot, w_out)
    state, normed, n0, n1, inverse, oht = call(
        functools.partial(state_body, geo),
        [
            (wide, bf16),
            (wide, bf16),
            (edge, bf16),
            (edge, bf16),
            ((pixels, 128), f32),
            ((geo.total, pixels), bf16),
        ],
        n_in=3,
        flops=1 << 30,
    )(arrived, w_enc, background)
    n_west = lax.ppermute(n1, "lon", up)
    n_east = lax.ppermute(n0, "lon", down)
    q, k, v, dq, dkt, dvt, slope, weight, v_far, state_far = call(
        functools.partial(own_body, geo),
        [
            (wide, bf16),
            (wide, bf16),
            (wide, bf16),
            (wide, f32),
            (tall, f32),
            (tall, f32),
            ((geo.total, chans), f32),
            (weights_own, bf16),
            (wide, bf16),
            (wide, bf16),
        ],
        scratch=[pattern] + vmem(tall, weights_own) + [dma((4,))],
        n_in=8,
        n_hbm=(4,),
        out_hbm=(7, 8, 9),
        flops=4 << 30,
    )(normed, w_qkv, gm, gmt, block_pattern, arrived, w_enc, state)
    rim_v, far, gback, reply = call(
        functools.partial(rim_body, geo),
        [
            (wide, bf16),
            (weights_far, bf16),
            (wide, bf16),
            ((geo.devs, geo.rows, half), bf16),
        ],
        scratch=[pattern] + vmem(wide, tall, wide, wide, weights_far, wide, wide, tall, tall) + [dma((4,))],
        n_in=23,
        n_hbm=(13,),
        out_hbm=(0, 1, 2),
        flops=4 << 30,
    )(
        n_west, n_east, w_qkv, q, k, v, gm, gw, gwt, ge, get, bias_w, bias_e, block_pattern,
        dq, dkt, dvt, state, cotangent, inverse, oht, slope, w_enc,
    )
    returned = lax.all_to_all(reply, ("lat", "lon"), split_axis=0, concat_axis=0, tiled=True)
    updated, grad_background = call(
        out_body,
        [((lat_rows, lon_cols, chans), bf16), ((lat_rows, lon_cols, chans), bf16)],
        scratch=vmem(weights_own, weights_far, wide, wide, (chans, chans), wide, wide, wide)
        + [dma((7,))],
        n_in=7,
        n_hbm=range(7),
        flops=1 << 30,
    )(weight, far, v_far, rim_v, w_out, state_far, gback)
    (grad_obs,) = call(
        functools.partial(unpack_body, geo), [((slots, feats), bf16)], n_in=2, flops=1 << 28
    )(returned, slot)
    return (updated, grad_background, grad_obs)


def solution(mesh):
    return jax.shard_map(
        shards,
        mesh=mesh,
        in_specs=(
            P("lat", "lon", None),
            P(("lat", "lon"), None),
            P(("lat", "lon")),
            P(("lat", "lon")),
            P("lat", "lon", None),
            P(),
            P(),
            P(),
            P("lat", "lon", None),
        ),
        out_specs=(P("lat", "lon", None), P("lat", "lon", None), P(("lat", "lon"), None)),
        check_vma=False,
    )
```

time: 84.3 us -> 65.7 us (0.78)
  waiting for transfers between devices: 25.2 us -> 15.8 us
  local copies, waits for them, and re-layouts: 8.47 us -> 0.06 us
  starting transfers between devices: 17.3 us -> 15.3 us
  Pallas kernels: 31.5 us -> 32.6 us
    ppermute x1, waiting for transfers between devices: 12.9 us -> 0.17 us  [shards(): west_cot = lax.ppermute(cot_east, 'lon', up)]
    unnamed x48 -> x24, local copies, waits for them, and re-layouts: 8.47 us -> 0.06 us
    all_to_all x2, starting transfers between devices: 10.1 us -> 7.1 us  [the longest x1 4.49 us: shards(): lax.all_to_all(payload, ('lat', 'lon'), split_axis=0, concat_axis=0, tile...]
    all_to_all x2, waiting for transfers between devices: 12.3 us -> 15 us  [the longest x1 7.77 us: shards(): lax.all_to_all(payload, ('lat', 'lon'), split_axis=0, concat_axis=0, tile...]
    pallas_call x7, Pallas kernels: 31.5 us -> 32.6 us  [run(): kernel(*[pltpu.with_memory_space_constraint(x, pltpu.HBM) if k in n_hbm e...]
  transfers between devices with their start and end apart: 6 -> 6, of which waited for: 2 -> 4; matrix products, arithmetic and copies ran while one was open for 0% -> 0% of each run, Pallas kernels for 12% -> 24%
where the time goes in v2:
time: 65.7 us; the launch traced here: 65.3 us
  Pallas kernels  32.6 us (50%)
  waiting for transfers between devices  15.8 us (24%)
  starting transfers between devices  15.3 us (23%)
  between operations  1.5 us (2%)
    pallas_call x7, Pallas kernels, run(): kernel(*[pltpu.with_memory_space_constraint(x, pltpu.HBM) if k in n_hbm e...  32.6 us
    all_to_all x1, waiting for transfers between devices, shards(): lax.all_to_all(payload, ('lat', 'lon'), split_axis=0, concat_axis=0, tile...  7.77 us
    all_to_all x1, waiting for transfers between devices, shards(): lax.all_to_all(reply, ('lat', 'lon'), split_axis=0, concat_axis=0, tiled=...  7.27 us
    all_to_all x1, starting transfers between devices, shards(): lax.all_to_all(payload, ('lat', 'lon'), split_axis=0, concat_axis=0, tile...  4.49 us
    ppermute x1, starting transfers between devices, shards(): east_cot = lax.ppermute(cot_west, 'lon', down)  4.1 us
    ppermute x1, starting transfers between devices, shards(): n_east = lax.ppermute(n0, 'lon', down)  3.43 us
    all_to_all x1, starting transfers between devices, shards(): lax.all_to_all(reply, ('lat', 'lon'), split_axis=0, concat_axis=0, tiled=...  2.61 us
  transfers between devices with their start and end apart: 6, of which 4 were waited for; matrix products, arithmetic and copies ran while one was open for 0% of the time, Pallas kernels for 24%

profile of v2, /device:TPU:0, one launch (start us, length us, event | category | flops | bytes accessed | tf_op | source)
XLA Modules:
  0.0 65.3 jit_solution(17964076471225088335)
XLA Ops:
  1.3 2.6 %shard_map.112 = (bf16[32,40,128]{2,1,0:T(8,128)(2,1)}, s32[1,512]{1,0:T(1,128)S(1)}, bf16[17,16,512]{2,1,0:T(8,128)(2,1)}, bf16[17,16,512]{2,1,0:T(8,128)(2,1)}) custom-call(s32[1,512]{1,0:T(1,128)} %bitcast.1, s32[1]{0:T(128)S(6)} %copy.12.cnt_ref, bf16[512,256]{1,0:T(8,128)(2,1)} %rows_hbm.1, s32[2,4,4]{2,1,0:T(4,128)} %pat_hbm.5, ...), custom_call_target="tpu_custom_call" | custom-call | flops 419430400 | bytes 1048576 | tf_op jit(solution)/shard_map/pallas_call | solution.py:69
  3.9 0.5 collective-permute-start
  4.4 4.1 %collective-permute-start.1 = (bf16[17,16,512]{2,1,0:T(8,128)(2,1)}, bf16[17,16,512]{2,1,0:T(8,128)(2,1)S(1)}, u32[]{:S(2)}, u32[]{:S(2)}) collective-permute-start(bf16[17,16,512]{2,1,0:T(8,128)(2,1)} %get-tuple-element.40), channel_id=1, source_target_pairs={{1,0},{2,1},{3,2},{4,3},{5,4},{6,5},{7,6},{0,7},{9,8},{10,9},{11,1... | collective-permute-start | bytes 835592 | tf_op jit(solution)/shard_map/ppermute | solution.py:570
  8.5 4.5 %all-to-all-start = ((bf16[32,40,128]{2,1,0:T(8,128)(2,1)}), bf16[32,40,128]{2,1,0:T(8,128)(2,1)S(1)}, u32[]{:S(2)}, u32[]{:S(2)}) async-start(bf16[32,40,128]{2,1,0:T(8,128)(2,1)} %get-tuple-element.37), calls=%async_computation | async-start | bytes 655360 | tf_op jit(solution)/shard_map/all_to_all | solution.py:571
  13.0 0.0 copy-start.1
  13.0 0.0 copy-start.3
  13.0 0.2 collective-permute-done.west_ref
  13.2 0.6 collective-permute-done.1.east_ref
  13.8 3.5 %shard_map.114 = (bf16[512,512]{1,0:T(8,128)(2,1)}, bf16[512,512]{1,0:T(8,128)(2,1)}, bf16[256,512]{1,0:T(8,128)(2,1)}, bf16[512,256]{1,0:T(8,128)(2,1)}, bf16[2...) custom-call(bf16[16,32,512]{2,1,0:T(8,128)(2,1)} %cot_ref.1, ...), custom_call_target="tpu_custom_call" | custom-call | flops 137438953472 | bytes 1048576 | tf_op jit(solution)/shard_map/pallas_call | solution.py:69
  17.3 0.0 copy-start
  17.4 0.0 copy-start.4
  17.4 7.8 %all-to-all-done.arr_ref = bf16[32,40,128]{2,1,0:T(8,128)(2,1)S(1)} async-done(((bf16[32,40,128]{2,1,0:T(8,128)(2,1)}), bf16[32,40,128]{2,1,0:T(8,128)(2,1)S(1)}, u32[]{:S(2)}, u32[]{:S(2)}) %all-to-all-start) | async-done | bytes 327712 | tf_op jit(solution)/shard_map/all_to_all | solution.py:571
  25.1 0.0 copy-done.1
  25.1 0.0 copy-done.3
  25.1 0.0 copy-start.11
  25.1 2.1 %shard_map.113 = (bf16[512,512]{1,0:T(8,128)(2,1)S(1)}, bf16[512,512]{1,0:T(8,128)(2,1)S(1)}, bf16[256,512]{1,0:T(8,128)(2,1)S(1)}, bf16[256,512]{1,0:T(8,128)(2...) custom-call(bf16[32,40,128]{2,1,0:T(8,128)(2,1)S(1)} %all-to-all-done.arr_ref, ...), custom_call_target="tpu_custom_call" | custom-call | flops 1073741824 | bytes 1048576 | tf_op jit(solution)/shard_map/pallas_call | solution.py:69
  27.3 0.2 collective-permute-start.2
  27.4 3.4 %collective-permute-start.3 = (bf16[256,512]{1,0:T(8,128)(2,1)S(1)}, bf16[256,512]{1,0:T(8,128)(2,1)S(1)}, u32[]{:S(2)}, u32[]{:S(2)}) collective-permute-start(bf16[256,512]{1,0:T(8,128)(2,1)S(1)} %get-tuple-element.46), channel_id=1, source_target_pairs={{1,0},{2,1},{3,2},{4,3},{5,4},{6,5},{7,6},{0,7},{9,8},{10,9},{11,1... | collective-permute-start | bytes 786440 | tf_op jit(solution)/shard_map/ppermute | solution.py:607
  30.9 0.0 copy-done
  30.9 0.0 copy-done.4
  30.9 0.0 copy-done.11
  30.9 0.0 copy-start.2
  30.9 0.0 copy-start.5
  30.9 0.0 copy-start.6
  30.9 0.0 copy-start.7
  30.9 0.0 copy-start.8
  30.9 0.0 copy-start.9
  30.9 0.0 copy-start.10
  30.9 7.1 %shard_map.115 = (bf16[512,512]{1,0:T(8,128)(2,1)S(1)}, bf16[512,512]{1,0:T(8,128)(2,1)S(1)}, bf16[512,512]{1,0:T(8,128)(2,1)S(1)}, f32[512,512]{1,0:T(8,128)S(1...) custom-call(bf16[512,512]{1,0:T(8,128)(2,1)S(1)} %get-tuple-element., ...), custom_call_target="tpu_custom_call" | custom-call | flops 4294967296 | bytes 1048576 | tf_op jit(solution)/shard_map/pallas_call | solution.py:69
  38.0 0.0 collective-permute-done.2.nw_ref
  38.0 0.0 collective-permute-done.3.ne_ref
  38.0 0.0 copy-done.2
  38.1 0.0 copy-done.5
  38.1 0.0 copy-done.6
  38.1 0.0 copy-done.7
  38.1 0.0 copy-done.8
  38.1 0.0 copy-done.9
  38.1 0.0 copy-done.10
  38.1 11.3 %shard_map.116 = (bf16[512,512]{1,0:T(8,128)(2,1)}, bf16[4,4,128,256]{3,2,1,0:T(8,128)(2,1)}, bf16[512,512]{1,0:T(8,128)(2,1)}, bf16[32,40,128]{2,1,0:T(8,128)(2,1)}) custom-call(bf16[256,512]{1,0:T(8,128)(2,1)S(1)} %collective-permute-done.2.nw_ref, bf16[256,512]{1,0:T(8,128)(2,1)S(1)} %collective-permute-done.3.ne_ref, bf16[512,1536]{1,0:T(8,128)(2,1)S(1)} %copy-done, ...), custom_call_target="tpu_custom_call" | custom-call | flops 4294967296 | bytes 1048576 | tf_op jit(solution)/shard_map/pallas_call | solution.py:69
  49.4 2.6 %all-to-all-start.1 = ((bf16[32,40,128]{2,1,0:T(8,128)(2,1)}), bf16[32,40,128]{2,1,0:T(8,128)(2,1)S(1)}, u32[]{:S(2)}, u32[]{:S(2)}) async-start(bf16[32,40,128]{2,1,0:T(8,128)(2,1)} %get-tuple-element.69), calls=%async_computation.1 | async-start | bytes 655360 | tf_op jit(solution)/shard_map/all_to_all | solution.py:645
  52.0 4.9 %shard_map.117 = (bf16[16,32,512]{2,1,0:T(8,128)(2,1)}, bf16[16,32,512]{2,1,0:T(8,128)(2,1)}) custom-call(bf16[2,8,256,256]{3,2,1,0:T(8,128)(2,1)} %get-tuple-element.44.refs_0_, bf16[4,4,128,256]{3,2,1,0:T(8,128)(2,1)} %get-tuple-element.62.refs_1_, bf16[512,512]{1,0:T(8,128)(2,1)} %get-tuple-element.63.refs_2_, ...), custom_call_target="tpu_custom_call" | custom-call | flops 1073741824 | bytes 1048576 | tf_op jit(solution)/shard_map/pallas_call | solution.py:69
  56.9 7.3 %all-to-all-done.1.back_ref = bf16[32,40,128]{2,1,0:T(8,128)(2,1)S(1)} async-done(((bf16[32,40,128]{2,1,0:T(8,128)(2,1)}), bf16[32,40,128]{2,1,0:T(8,128)(2,1)S(1)}, u32[]{:S(2)}, u32[]{:S(2)}) %all-to-all-start.1) | async-done | bytes 327712 | tf_op jit(solution)/shard_map/all_to_all | solution.py:645
  64.2 1.1 %shard_map.118 = bf16[512,256]{1,0:T(8,128)(2,1)} custom-call(bf16[32,40,128]{2,1,0:T(8,128)(2,1)S(1)} %all-to-all-done.1.back_ref, s32[1,512]{1,0:T(1,128)S(1)} %get-tuple-element.70.slot_ref), custom_call_target="tpu_custom_call" | custom-call | flops 268435456 | bytes 1048576 | tf_op jit(solution)/shard_map/pallas_call | solution.py:69
Async XLA Ops:
  3.9 9.3 %collective-permute-start = (bf16[17,16,512]{2,1,0:T(8,128)(2,1)}, bf16[17,16,512]{2,1,0:T(8,128)(2,1)S(1)}, u32[]{:S(2)}, u32[]{:S(2)}) collective-permute-start(bf16[17,16,512]{2,1,0:T(8,128)(2,1)} %get-tuple-element.39), channel_id=1, source_target_pairs={{0,1},{1,2},{2,3},{3,4},{4,5},{5,6},{6,7},{7,0},{8,9},{9,10},{10,1... | collective-permute-start | bytes 835592 | tf_op jit(solution)/shard_map/ppermute | solution.py:569
  4.4 9.4 %collective-permute-start.1 = (bf16[17,16,512]{2,1,0:T(8,128)(2,1)}, bf16[17,16,512]{2,1,0:T(8,128)(2,1)S(1)}, u32[]{:S(2)}, u32[]{:S(2)}) collective-permute-start(bf16[17,16,512]{2,1,0:T(8,128)(2,1)} %get-tuple-element.40), channel_id=1, source_target_pairs={{1,0},{2,1},{3,2},{4,3},{5,4},{6,5},{7,6},{0,7},{9,8},{10,9},{11,1... | collective-permute-start | bytes 835592 | tf_op jit(solution)/shard_map/ppermute | solution.py:570
  8.5 16.6 %all-to-all-start = ((bf16[32,40,128]{2,1,0:T(8,128)(2,1)}), bf16[32,40,128]{2,1,0:T(8,128)(2,1)S(1)}, u32[]{:S(2)}, u32[]{:S(2)}) async-start(bf16[32,40,128]{2,1,0:T(8,128)(2,1)} %get-tuple-element.37), calls=%async_computation | async-start | bytes 655360 | tf_op jit(solution)/shard_map/all_to_all | solution.py:571
  13.0 12.1 %copy-start.1 = (bf16[16,32,512]{2,1,0:T(8,128)(2,1)S(1)}, bf16[16,32,512]{2,1,0:T(8,128)(2,1)}, u32[]{:S(2)}) copy-start(bf16[16,32,512]{2,1,0:T(8,128)(2,1)} %bg_ref.1) | copy-start | bytes 1572868
  13.0 12.1 %copy-start.3 = (bf16[256,512]{1,0:T(8,128)(2,1)S(1)}, bf16[256,512]{1,0:T(8,128)(2,1)}, u32[]{:S(2)}) copy-start(bf16[256,512]{1,0:T(8,128)(2,1)} %wenc_ref.5) | copy-start | bytes 786436
  17.3 13.5 %copy-start = (bf16[512,1536]{1,0:T(8,128)(2,1)S(1)}, bf16[512,1536]{1,0:T(8,128)(2,1)}, u32[]{:S(2)}) copy-start(bf16[512,1536]{1,0:T(8,128)(2,1)} %wqkv_ref.3) | copy-start | bytes 4718596
  17.4 13.5 %copy-start.4 = (bf16[512,512]{1,0:T(8,128)(2,1)S(1)}, bf16[512,512]{1,0:T(8,128)(2,1)}, u32[]{:S(2)}) copy-start(bf16[512,512]{1,0:T(8,128)(2,1)} %get-tuple-element.41.gm_ref) | copy-start | bytes 1572868
  25.1 5.7 %copy-start.11 = (bf16[512,512]{1,0:T(8,128)(2,1)S(1)}, bf16[512,512]{1,0:T(8,128)(2,1)}, u32[]{:S(2)}) copy-start(bf16[512,512]{1,0:T(8,128)(2,1)} %get-tuple-element.42.gmt_ref) | copy-start | bytes 1572868
  27.3 10.8 %collective-permute-start.2 = (bf16[256,512]{1,0:T(8,128)(2,1)S(1)}, bf16[256,512]{1,0:T(8,128)(2,1)S(1)}, u32[]{:S(2)}, u32[]{:S(2)}) collective-permute-start(bf16[256,512]{1,0:T(8,128)(2,1)S(1)} %get-tuple-element.45), channel_id=1, source_target_pairs={{0,1},{1,2},{2,3},{3,4},{4,5},{5,6},{6,7},{7,0},{8,9},{9,10},{10,1... | collective-permute-start | bytes 786440 | tf_op jit(solution)/shard_map/ppermute | solution.py:606
  27.4 10.6 %collective-permute-start.3 = (bf16[256,512]{1,0:T(8,128)(2,1)S(1)}, bf16[256,512]{1,0:T(8,128)(2,1)S(1)}, u32[]{:S(2)}, u32[]{:S(2)}) collective-permute-start(bf16[256,512]{1,0:T(8,128)(2,1)S(1)} %get-tuple-element.46), channel_id=1, source_target_pairs={{1,0},{2,1},{3,2},{4,3},{5,4},{6,5},{7,6},{0,7},{9,8},{10,9},{11,1... | collective-permute-start | bytes 786440 | tf_op jit(solution)/shard_map/ppermute | solution.py:607
  30.9 7.2 %copy-start.2 = (bf16[16,32,512]{2,1,0:T(8,128)(2,1)S(1)}, bf16[16,32,512]{2,1,0:T(8,128)(2,1)}, u32[]{:S(2)}) copy-start(bf16[16,32,512]{2,1,0:T(8,128)(2,1)} %cot_ref.1) | copy-start | bytes 1572868
  30.9 7.2 %copy-start.5 = (bf16[256,512]{1,0:T(8,128)(2,1)S(1)}, bf16[256,512]{1,0:T(8,128)(2,1)}, u32[]{:S(2)}) copy-start(bf16[256,512]{1,0:T(8,128)(2,1)} %get-tuple-element.50.gw_ref) | copy-start | bytes 786436
  30.9 7.2 %copy-start.6 = (bf16[512,256]{1,0:T(8,128)(2,1)S(1)}, bf16[512,256]{1,0:T(8,128)(2,1)}, u32[]{:S(2)}) copy-start(bf16[512,256]{1,0:T(8,128)(2,1)} %get-tuple-element.51.gwt_ref) | copy-start | bytes 786436
  30.9 7.2 %copy-start.7 = (bf16[256,512]{1,0:T(8,128)(2,1)S(1)}, bf16[256,512]{1,0:T(8,128)(2,1)}, u32[]{:S(2)}) copy-start(bf16[256,512]{1,0:T(8,128)(2,1)} %get-tuple-element.52.ge_ref) | copy-start | bytes 786436
  30.9 7.2 %copy-start.8 = (bf16[512,256]{1,0:T(8,128)(2,1)S(1)}, bf16[512,256]{1,0:T(8,128)(2,1)}, u32[]{:S(2)}) copy-start(bf16[512,256]{1,0:T(8,128)(2,1)} %get-tuple-element.53.get_ref) | copy-start | bytes 786436
  30.9 7.2 %copy-start.9 = (f32[256,128]{1,0:T(8,128)S(1)}, f32[256,128]{1,0:T(8,128)}, u32[]{:S(2)}) copy-start(f32[256,128]{1,0:T(8,128)} %get-tuple-element.54.bw_ref) | copy-start | bytes 393220
  30.9 7.2 %copy-start.10 = (f32[256,128]{1,0:T(8,128)S(1)}, f32[256,128]{1,0:T(8,128)}, u32[]{:S(2)}) copy-start(f32[256,128]{1,0:T(8,128)} %get-tuple-element.55.be_ref) | copy-start | bytes 393220
  49.4 14.8 %all-to-all-start.1 = ((bf16[32,40,128]{2,1,0:T(8,128)(2,1)}), bf16[32,40,128]{2,1,0:T(8,128)(2,1)S(1)}, u32[]{:S(2)}, u32[]{:S(2)}) async-start(bf16[32,40,128]{2,1,0:T(8,128)(2,1)} %get-tuple-element.69), calls=%async_computation.1 | async-start | bytes 655360 | tf_op jit(solution)/shard_map/all_to_all | solution.py:645

commit v3 on v2

--- a/solution.py
+++ b/solution.py
@@ -160,21 +160,28 @@
         self.mark = self.shift - 1
         self.rows = 2 * self.full + self.tail
         self.bulk = devs * self.full
-        self.total = self.bulk + devs * self.tail
+        self.total = self.bulk + devs * self.rest
         self.lon_bits = (lon_cols * lon_devs).bit_length() - 1
+
+
+def tail_picks(geo, offset):
+    shape = (geo.devs, geo.devs * geo.tail)
+    base = iota(shape, 1) - iota(shape, 0) * geo.tail
+    return jnp.concatenate([one_hot(base == offset + r) for r in range(geo.rest)], axis=0)
 
 
 def join_slots(geo, ref, feats):
     half = feats // 2
     tail = ref[:, 2 * geo.full : geo.rows, :].reshape(geo.devs * geo.tail, half)
-    wide = tail.astype(f32)
-    moved = pltpu.roll(wide, wide.shape[0] - geo.shift, 0)
-    tail_rows = jnp.concatenate([wide, moved], axis=1).astype(bf16)
-    if not geo.full:
-        return tail, tail_rows
-    first = ref[:, 0 : geo.full, :].reshape(geo.bulk, half)
-    second = ref[:, geo.full : 2 * geo.full, :].reshape(geo.bulk, half)
-    return tail, jnp.concatenate([jnp.concatenate([first, second], axis=1), tail_rows], axis=0)
+    parts = []
+    if geo.full:
+        first = ref[:, 0 : geo.full, :].reshape(geo.bulk, half)
+        second = ref[:, geo.full : 2 * geo.full, :].reshape(geo.bulk, half)
+        parts.append(jnp.concatenate([first, second], axis=1))
+    if geo.rest:
+        rows = [mm(tail_picks(geo, n * geo.shift), tail) for n in range(2)]
+        parts.append(jnp.concatenate(rows, axis=1).astype(bf16))
+    return tail, jnp.concatenate(parts, axis=0)
 
 
 def store_bulk(geo, ref, values):
@@ -188,7 +195,7 @@
     place = jnp.where(
         rank < geo.full,
         owner * geo.full + rank,
-        geo.bulk + owner * geo.tail + rank - geo.full,
+        geo.bulk + (rank - geo.full) * geo.devs + owner,
     )
     return jnp.where(live, place, -1)
 
@@ -250,8 +257,9 @@
         start_copy(west_ref, west_hbm, sems.at[6]),
     ]
     place = iota((tails, slots), 0)
-    first = one_hot(place == slot - geo.bulk)
-    second = one_hot((place == slot - geo.bulk + geo.shift) & (slot >= geo.bulk))
+    line = jnp.where(live & (rank >= geo.full), owner * geo.tail + rank - geo.full, -geo.tail)
+    first = one_hot(place == line)
+    second = one_hot(place == line + geo.shift)
     rows_copy.wait()
     half = rows_ref.shape[1] // 2
     if geo.full:
@@ -266,9 +274,9 @@
 
 def grad_body(
     cot_hbm, west_ref, east_ref, wout_hbm,
-    gm_hbm, gmt_hbm, gw_hbm, gwt_hbm, ge_hbm, get_hbm, bw_hbm, be_hbm,
+    gm_hbm, gw_hbm, ge_hbm, bw_hbm, be_hbm,
     cot_ref, wout_ref,
-    gm_ref, gmt_ref, gw_ref, gwt_ref, ge_ref, get_ref, bw_ref, be_ref, in_sems, out_sems,
+    gm_ref, gw_ref, ge_ref, bw_ref, be_ref, in_sems, out_sems,
 ):
     wout_copy = start_copy(wout_hbm, wout_ref, in_sems.at[0])
     cot_copy = start_copy(cot_hbm, cot_ref, in_sems.at[1])
@@ -278,22 +286,17 @@
     for i, u in halves():
         part = mm(chunk(cot_ref, i, u), wout, 1, 1)
         gm_ref[rows_of(i, u), :] = part.astype(bf16)
-        gmt_ref[:, rows_of(i, u)] = part.T.astype(bf16)
-    outs = [
-        start_copy(gm_ref, gm_hbm, out_sems.at[0]),
-        start_copy(gmt_ref, gmt_hbm, out_sems.at[1]),
-    ]
+    outs = [start_copy(gm_ref, gm_hbm, out_sems.at[0])]
     second_q = iota((TILE, TILE), 0) % HALF >= BLOCK
-    for n, (src, dst, dst_t, bias_ref, dst_hbm, dst_t_hbm, bias_hbm) in enumerate(
+    for n, (src, dst, bias_ref, dst_hbm, bias_hbm) in enumerate(
         (
-            (west_ref, gw_ref, gwt_ref, bw_ref, gw_hbm, gwt_hbm, bw_hbm),
-            (east_ref, ge_ref, get_ref, be_ref, ge_hbm, get_hbm, be_hbm),
+            (west_ref, gw_ref, bw_ref, gw_hbm, bw_hbm),
+            (east_ref, ge_ref, be_ref, ge_hbm, be_hbm),
         )
     ):
         rows = src.shape[0] - 1
         part = mm(src[0:rows].reshape(2 * TILE, wout.shape[0]), wout, 1, 1)
         dst[...] = part.astype(bf16)
-        dst_t[...] = part.T.astype(bf16)
         extra = src[rows].astype(f32)
         for i in range(2):
             line = extra[i : i + 1, :]
@@ -302,9 +305,8 @@
             bias = -0.5 * jnp.log(count * 64.0)
             bias_ref[i * TILE : (i + 1) * TILE, :] = jnp.where(mask > 0.5, bias, MASKED)
         outs += [
-            start_copy(dst, dst_hbm, out_sems.at[2 + 3 * n]),
-            start_copy(dst_t, dst_t_hbm, out_sems.at[3 + 3 * n]),
-            start_copy(bias_ref, bias_hbm, out_sems.at[4 + 3 * n]),
+            start_copy(dst, dst_hbm, out_sems.at[1 + 2 * n]),
+            start_copy(bias_ref, bias_hbm, out_sems.at[2 + 2 * n]),
         ]
     for copy in outs:
         copy.wait()
@@ -318,16 +320,16 @@
     )
     meta = mm(pick, tails).astype(bf16)
     codes = []
-    for base, count in ((0, geo.full), (geo.full, geo.tail)):
-        if count:
-            owner = one_hot(
-                iota((devs, count, devs), 0) == iota((devs, count, devs), 2)
-            ).reshape(devs * count, devs)
-            wide = mm(owner, meta)
-            place = iota((devs, count, 128), 1).reshape(devs * count, 128) + base
-            lane = iota((devs * count, 128), 1)
-            scale = jnp.where(lane == place, 32.0, 0.0) + jnp.where(lane == place + 64, 1.0, 0.0)
-            codes.append(jnp.sum(wide * scale, axis=1, keepdims=True))
+    if geo.full:
+        shape = (devs, geo.full, devs)
+        owner = one_hot(iota(shape, 0) == iota(shape, 2)).reshape(geo.bulk, devs)
+        place = iota((devs, geo.full, 128), 1).reshape(geo.bulk, 128)
+        lane = iota((geo.bulk, 128), 1)
+        scale = jnp.where(lane == place, 32.0, 0.0) + jnp.where(lane == place + 64, 1.0, 0.0)
+        codes.append(jnp.sum(mm(owner, meta) * scale, axis=1, keepdims=True))
+    spare = meta.astype(f32)
+    for r in range(geo.full, geo.cap):
+        codes.append(spare[:, r : r + 1] * 32.0 + spare[:, 64 + r : 65 + r])
     code = jnp.concatenate(codes, axis=0).astype(i32)
     pixels = n_ref.shape[0]
     oht = one_hot(code == iota((geo.total, pixels), 1) + 1)
@@ -360,57 +362,94 @@
     return [jnp.where(head_lanes(slab.shape, h), slab, jnp.zeros((), slab.dtype)) for h in range(2)]
 
 
-def weigh(q2, g2, km, vm, bias):
-    tangent = jnp.tanh(mm(q2, km, 1, 1) + bias)
-    weight = tangent + 1.0
-    slope = mm(g2, vm, 1, 1) * weight * (2.0 - weight)
-    return weight.astype(bf16), slope.astype(bf16)
-
-
 def stack_heads(slab):
     return jnp.concatenate(split_heads(slab), axis=0)
 
 
-def project(src, wqkv_ref, q_ref, qt_ref, k_ref, v_ref, rows):
+def weigh(score, grad, bias):
+    weight = jnp.tanh(score + bias) + 1.0
+    slope = grad * weight * (2.0 - weight)
+    return weight.astype(bf16), slope.astype(bf16)
+
+
+def pipeline(items, stages):
+    states = [None] * len(items)
+    for step in range(len(items) + len(stages) - 1):
+        for lag, stage in enumerate(stages):
+            n = step - lag
+            if 0 <= n < len(items):
+                states[n] = stage(items[n], states[n])
+
+
+def project(src, wqkv_ref, q_ref, k_ref, v_ref, rows):
     chans = src.shape[1]
     queries = mm(src, wqkv_ref[:, 0:chans]).astype(bf16).astype(f32) * 0.0625
     q_ref[rows, :] = queries.astype(bf16)
-    qt_ref[:, rows] = queries.T.astype(bf16)
     k_ref[rows, :] = mm(src, wqkv_ref[:, chans : 2 * chans]).astype(bf16)
     v_ref[rows, :] = mm(src, wqkv_ref[:, 2 * chans : 3 * chans]).astype(bf16)
 
 
+def slab_lanes(s):
+    return slice(s * SLAB, (s + 1) * SLAB)
+
+
 def own_body(
-    geo, n_ref, wqkv_ref, gm_ref, gmt_ref, pat_hbm, arr_ref, wenc_ref, state_ref,
-    q_ref, k_ref, v_ref, dq_ref, dkt_ref, dvt_ref, slope_ref, weight_hbm, v_hbm, state_hbm,
-    pat_ref, qt_ref, weight_ref, sems,
+    geo, n_ref, wqkv_ref, gm_ref, pat_hbm, arr_ref, wenc_ref, state_ref,
+    q_ref, k_ref, v_ref, dq_ref, dk_ref, dv_ref, slope_ref, weight_hbm, v_hbm, state_hbm,
+    pat_ref, weight_ref, sems,
 ):
     chans = n_ref.shape[1]
     pat_copy = start_copy(pat_hbm, pat_ref, sems.at[0])
     state_copy = start_copy(state_ref, state_hbm, sems.at[1])
-    project(n_ref[...], wqkv_ref, q_ref, qt_ref, k_ref, v_ref, slice(0, n_ref.shape[0]))
+    project(n_ref[...], wqkv_ref, q_ref, k_ref, v_ref, slice(0, n_ref.shape[0]))
     v_copy = start_copy(v_ref, v_hbm, sems.at[2])
     pat_copy.wait()
+    biases = []
     for i in range(2):
-        keys = slice(i * 2 * TILE, (i + 1) * 2 * TILE)
         bias = [
             jnp.concatenate([own_bias(pat_ref, i, u, -u), own_bias(pat_ref, i, u, 1 - u)], axis=1)
             for u in range(2)
         ]
-        bias = jnp.concatenate(bias, axis=0)
-        for s in range(chans // SLAB):
-            lanes = slice(s * SLAB, (s + 1) * SLAB)
-            km = split_heads(k_ref[keys, lanes])
-            vm = split_heads(v_ref[keys, lanes])
-            grad_q = jnp.zeros((2 * TILE, SLAB), f32)
-            for h in range(2):
-                weight, slope = weigh(q_ref[keys, lanes], gm_ref[keys, lanes], km[h], vm[h], bias)
-                weight_ref[i, 2 * s + h] = weight
-                grad_q = grad_q + mm(slope, km[h])
-                chan = slice(s * SLAB + h * 64, s * SLAB + (h + 1) * 64)
-                dkt_ref[chan, keys] = mm(qt_ref[chan, keys], slope)
-                dvt_ref[chan, keys] = mm(gmt_ref[chan, keys], weight)
-            dq_ref[keys, lanes] = grad_q
+        biases.append(jnp.concatenate(bias, axis=0))
+
+    def first(item, _):
+        i, s, h = item
+        keys, lanes = slice(i * 2 * TILE, (i + 1) * 2 * TILE), slab_lanes(s)
+        km = split_heads(k_ref[keys, lanes])[h]
+        vm = split_heads(v_ref[keys, lanes])[h]
+        return km, mm(q_ref[keys, lanes], km, 1, 1), mm(gm_ref[keys, lanes], vm, 1, 1)
+
+    def second(item, state):
+        i, s, h = item
+        km, score, grad = state
+        weight, slope = weigh(score, grad, biases[i])
+        weight_ref[i, 2 * s + h] = weight
+        return km, weight, slope
+
+    held = {}
+
+    def third(item, state):
+        i, s, h = item
+        keys, lanes = slice(i * 2 * TILE, (i + 1) * 2 * TILE), slab_lanes(s)
+        km, weight, slope = state
+        parts = (
+            mm(slope, km),
+            mm(slope, q_ref[keys, lanes], 0, 0),
+            mm(weight, gm_ref[keys, lanes], 0, 0),
+        )
+        if h == 0:
+            held[i, s] = parts
+            return
+        before = held.pop((i, s))
+        lower = iota((2 * TILE, SLAB), 1) < SLAB // 2
+        dq_ref[keys, lanes] = before[0] + parts[0]
+        dk_ref[keys, lanes] = jnp.where(lower, before[1], parts[1])
+        dv_ref[keys, lanes] = jnp.where(lower, before[2], parts[2])
+
+    pipeline(
+        [(i, s, h) for i in range(2) for s in range(chans // SLAB) for h in range(2)],
+        (first, second, third),
+    )
     weight_copy = start_copy(weight_ref, weight_hbm, sems.at[3])
     pre = mm(join_slots(geo, arr_ref, wenc_ref.shape[0])[1], wenc_ref[...])
     square, tangent = gelu_parts(pre)
@@ -422,78 +461,104 @@
 
 
 def rim_body(
-    geo, nw_ref, ne_ref, wqkv_ref, q_ref, k_ref, v_ref, gm_ref, gw_ref, gwt_ref, ge_ref, get_ref,
-    bw_ref, be_ref, pat_hbm, dq_ref, dkt_ref, dvt_ref, state_ref, cot_ref, inv_ref,
+    geo, nw_ref, ne_ref, wqkv_ref, q_ref, k_ref, v_ref, gm_ref, gw_ref, ge_ref,
+    bw_ref, be_ref, pat_hbm, dq_ref, dk_ref, dv_ref, state_ref, cot_ref, inv_ref,
     oht_ref, slope_ref, wenc_ref,
-    v_hbm, weight_hbm, gback_hbm, reply_ref,
-    pat_ref, rim_q, rim_qt, rim_k, rim_v, weight_ref, gback_ref, gq, gkt, gvt, sems,
+    v_hbm, weight_hbm, gback_hbm, reply_hbm,
+    pat_ref, rim_q, rim_k, rim_v, weight_ref, gback_ref, grad_ref, reply_ref, sems,
 ):
     chans = q_ref.shape[1]
     pat_copy = start_copy(pat_hbm, pat_ref, sems.at[0])
     for side, src in enumerate((nw_ref, ne_ref)):
         rows = slice(side * 2 * TILE, (side + 1) * 2 * TILE)
-        project(src[...], wqkv_ref, rim_q, rim_qt, rim_k, rim_v, rows)
+        project(src[...], wqkv_ref, rim_q, rim_k, rim_v, rows)
     v_copy = start_copy(rim_v, v_hbm, sems.at[1])
     pat_copy.wait()
+    out_bias, in_bias = {}, {}
     for i in range(2):
-        for side, (gh_ref, ght_ref, bias_ref) in enumerate(
-            ((gw_ref, gwt_ref, bw_ref), (ge_ref, get_ref, be_ref))
+        for side, bias_ref in enumerate((bw_ref, be_ref)):
+            bias = own_bias(pat_ref, i, side, 2 * side - 1)
+            out_bias[i, side] = jnp.concatenate([bias, bias], axis=1)
+            bias = bias_ref[i * TILE : (i + 1) * TILE, :]
+            in_bias[i, side] = jnp.concatenate([bias, bias], axis=1)
+
+    def where(item):
+        i, side, s = item
+        far = slice((side * 2 + i) * TILE, (side * 2 + i + 1) * TILE)
+        near = slice(i * TILE, (i + 1) * TILE)
+        return rows_of(i, side), far, near, (gw_ref, ge_ref)[side], slab_lanes(s)
+
+    def first(item, _):
+        own, far, near, gh_ref, lanes = where(item)
+        km = stack_heads(rim_k[far, lanes])
+        return (
+            km,
+            mm(q_ref[own, lanes], km, 1, 1),
+            mm(gm_ref[own, lanes], stack_heads(rim_v[far, lanes]), 1, 1),
+            mm(rim_q[far, lanes], stack_heads(k_ref[own, lanes]), 1, 1),
+            mm(gh_ref[near, lanes], stack_heads(v_ref[own, lanes]), 1, 1),
+        )
+
+    def second(item, state):
+        i, side, s = item
+        km, score_out, grad_out, score_in, grad_in = state
+        weight, slope_out = weigh(score_out, grad_out, out_bias[i, side])
+        weight_ref[i * 2 + side, s] = weight
+        weight_in, slope_in = weigh(score_in, grad_in, in_bias[i, side])
+        return km, slope_out, weight_in, slope_in
+
+    def third(item, state):
+        own, far, near, gh_ref, lanes = where(item)
+        km, slope_out, weight_in, slope_in = state
+        grad_q = mm(slope_out, km)
+        grad_k = mm(slope_in, rim_q[far, lanes], 0, 0)
+        grad_v = mm(weight_in, gh_ref[near, lanes], 0, 0)
+        lower = iota((TILE, SLAB), 1) < SLAB // 2
+        grad_k = jnp.where(lower, grad_k[0:TILE], grad_k[TILE:])
+        grad_v = jnp.where(lower, grad_v[0:TILE], grad_v[TILE:])
+        for n, total in enumerate(
+            (
+                (dq_ref[own, lanes] + grad_q) * 0.03125,
+                (dk_ref[own, lanes] + grad_k) * 0.5,
+                (dv_ref[own, lanes] + grad_v) * 0.5,
+            )
         ):
-            own = rows_of(i, side)
-            far = slice((side * 2 + i) * TILE, (side * 2 + i + 1) * TILE)
-            near = slice(i * TILE, (i + 1) * TILE)
-            out_bias = own_bias(pat_ref, i, side, 2 * side - 1)
-            out_bias = jnp.concatenate([out_bias, out_bias], axis=1)
-            in_bias = bias_ref[near, :]
-            in_bias = jnp.concatenate([in_bias, in_bias], axis=1)
-            for s in range(chans // SLAB):
-                lanes = slice(s * SLAB, (s + 1) * SLAB)
-                km = stack_heads(rim_k[far, lanes])
-                vm = stack_heads(rim_v[far, lanes])
-                weight, slope = weigh(q_ref[own, lanes], gm_ref[own, lanes], km, vm, out_bias)
-                weight_ref[i * 2 + side, s] = weight
-                gq[own, lanes] = ((dq_ref[own, lanes] + mm(slope, km)) * 0.03125).astype(bf16)
-                km = stack_heads(k_ref[own, lanes])
-                vm = stack_heads(v_ref[own, lanes])
-                weight, slope = weigh(rim_q[far, lanes], gh_ref[near, lanes], km, vm, in_bias)
-                grad_k = mm(rim_qt[lanes, far], slope)
-                grad_v = mm(ght_ref[lanes, near], weight)
-                for h in range(2):
-                    part = slice(h * 64, (h + 1) * 64)
-                    cols = slice(h * TILE, (h + 1) * TILE)
-                    chan = slice(s * SLAB + h * 64, s * SLAB + (h + 1) * 64)
-                    gkt[chan, own] = ((dkt_ref[chan, own] + grad_k[part, cols]) * 0.5).astype(bf16)
-                    gvt[chan, own] = ((dvt_ref[chan, own] + grad_v[part, cols]) * 0.5).astype(bf16)
+            spot = slice(n * chans + lanes.start, n * chans + lanes.stop)
+            grad_ref[own, spot] = total.astype(bf16)
+
+    pipeline(
+        [(i, side, s) for i in range(2) for side in range(2) for s in range(chans // SLAB)],
+        (first, second, third),
+    )
     weight_copy = start_copy(weight_ref, weight_hbm, sems.at[2])
-    grad_normed = (
-        mm(gq[...], wqkv_ref[:, 0:chans], 1, 1)
-        + mm(gkt[...], wqkv_ref[:, chans : 2 * chans], 0, 1)
-        + mm(gvt[...], wqkv_ref[:, 2 * chans : 3 * chans], 0, 1)
-    )
     scaled = []
     for i, u in halves():
         rows = rows_of(i, u)
+        grad = mm(grad_ref[rows, :], wqkv_ref[...], 1, 1)
         state = state_ref[rows, :].astype(f32)
         inv_rms = lax.rsqrt(jnp.mean(state * state, axis=1, keepdims=True) + norm_eps)
         normed = state * inv_rms
-        grad = grad_normed[rows]
         grad_state = chunk(cot_ref, i, u).astype(f32) + inv_rms * (
             grad - normed * jnp.mean(grad * normed, axis=1, keepdims=True)
         )
         gback_ref[rows, :] = grad_state.astype(bf16)
         scaled.append((grad_state * inv_ref[rows, 0:1]).astype(bf16))
     gback_copy = start_copy(gback_ref, gback_hbm, sems.at[3])
-    grad_enc = mm(oht_ref[...], jnp.concatenate(scaled, axis=0))
+    scaled = jnp.concatenate(scaled, axis=0)
+    grad_enc = mm(oht_ref[...], scaled)
     grad_pre = (grad_enc * slope_ref[...]).astype(bf16)
-    reply = mm(grad_pre, wenc_ref[...], 1, 1)
-    store_bulk(geo, reply_ref, reply[0 : geo.bulk].astype(bf16))
-    tail = reply[geo.bulk :]
-    half = tail.shape[1] // 2
-    moved = pltpu.roll(tail[:, half:], geo.shift, 0)
-    lower = iota((geo.devs * geo.tail, half), 0) % geo.tail < geo.shift
-    tail = jnp.where(lower, tail[:, 0:half], moved)
+    reply = mm(grad_pre, wenc_ref[...], 1, 1).astype(bf16)
+    store_bulk(geo, reply_ref, reply[0 : geo.bulk])
+    half = reply.shape[1] // 2
+    tail = jnp.zeros((geo.devs * geo.tail, half), f32)
+    if geo.rest:
+        for n in range(2):
+            tail = tail + mm(
+                tail_picks(geo, n * geo.shift), reply[geo.bulk :, n * half : (n + 1) * half], 0, 0
+            )
     reply_ref[:, 2 * geo.full : geo.rows, :] = tail.astype(bf16).reshape(geo.devs, geo.tail, half)
-    for copy in (v_copy, weight_copy, gback_copy):
+    reply_copy = start_copy(reply_ref, reply_hbm, sems.at[4])
+    for copy in (v_copy, weight_copy, gback_copy, reply_copy):
         copy.wait()
 
 
@@ -545,7 +610,7 @@
     down = [(j, i) for i, j in up]
 
     rim = (lat_rows + 1, HALF, chans)
-    wide, tall, edge, edge_t = (pixels, chans), (chans, pixels), (side, chans), (chans, side)
+    wide, edge = (pixels, chans), (side, chans)
     weights_own = (2, HEADS, 2 * TILE, 2 * TILE)
     weights_far = (4, chans // SLAB, TILE, 2 * TILE)
     dma = pltpu.SemaphoreType.DMA
@@ -569,25 +634,22 @@
     west_cot = lax.ppermute(cot_east, "lon", up)
     east_cot = lax.ppermute(cot_west, "lon", down)
     arrived = lax.all_to_all(payload, ("lat", "lon"), split_axis=0, concat_axis=0, tiled=True)
-    gm, gmt, gw, gwt, ge, get, bias_w, bias_e = call(
+    gm, gw, ge, bias_w, bias_e = call(
         grad_body,
         [
             (wide, bf16),
-            (tall, bf16),
             (edge, bf16),
-            (edge_t, bf16),
             (edge, bf16),
-            (edge_t, bf16),
             ((side, TILE), f32),
             ((side, TILE), f32),
         ],
         scratch=vmem((lat_rows, lon_cols, chans), (chans, chans))
-        + vmem(wide, tall, edge, edge_t, edge, edge_t)
+        + vmem(wide, edge, edge)
         + [pltpu.VMEM((side, TILE), f32)] * 2
-        + [dma((2,)), dma((8,))],
+        + [dma((2,)), dma((5,))],
         n_in=4,
         n_hbm=(0, 3),
-        out_hbm=range(8),
+        out_hbm=range(5),
         flops=GRAD_COST,
     )(cotangent, west_cot, east_cot, w_out)
     state, normed, n0, n1, inverse, oht = call(
@@ -605,42 +667,30 @@
     )(arrived, w_enc, background)
     n_west = lax.ppermute(n1, "lon", up)
     n_east = lax.ppermute(n0, "lon", down)
-    q, k, v, dq, dkt, dvt, slope, weight, v_far, state_far = call(
+    q, k, v, dq, dk, dv, slope, weight, v_far, state_far = call(
         functools.partial(own_body, geo),
-        [
-            (wide, bf16),
-            (wide, bf16),
-            (wide, bf16),
-            (wide, f32),
-            (tall, f32),
-            (tall, f32),
-            ((geo.total, chans), f32),
-            (weights_own, bf16),
-            (wide, bf16),
-            (wide, bf16),
-        ],
-        scratch=[pattern] + vmem(tall, weights_own) + [dma((4,))],
-        n_in=8,
-        n_hbm=(4,),
+        [(wide, bf16)] * 3
+        + [(wide, f32)] * 3
+        + [((geo.total, chans), f32), (weights_own, bf16), (wide, bf16), (wide, bf16)],
+        scratch=[pattern] + vmem(weights_own) + [dma((4,))],
+        n_in=7,
+        n_hbm=(3,),
         out_hbm=(7, 8, 9),
         flops=4 << 30,
-    )(normed, w_qkv, gm, gmt, block_pattern, arrived, w_enc, state)
+    )(normed, w_qkv, gm, block_pattern, arrived, w_enc, state)
     rim_v, far, gback, reply = call(
         functools.partial(rim_body, geo),
-        [
-            (wide, bf16),
-            (weights_far, bf16),
-            (wide, bf16),
-            ((geo.devs, geo.rows, half), bf16),
-        ],
-        scratch=[pattern] + vmem(wide, tall, wide, wide, weights_far, wide, wide, tall, tall) + [dma((4,))],
-        n_in=23,
-        n_hbm=(13,),
-        out_hbm=(0, 1, 2),
+        [(wide, bf16), (weights_far, bf16), (wide, bf16), ((geo.devs, geo.rows, half), bf16)],
+        scratch=[pattern]
+        + vmem(wide, wide, wide, weights_far, wide, (pixels, 3 * chans), (geo.devs, geo.rows, half))
+        + [dma((5,))],
+        n_in=21,
+        n_hbm=(11,),
+        out_hbm=(0, 1, 2, 3),
         flops=4 << 30,
     )(
-        n_west, n_east, w_qkv, q, k, v, gm, gw, gwt, ge, get, bias_w, bias_e, block_pattern,
-        dq, dkt, dvt, state, cotangent, inverse, oht, slope, w_enc,
+        n_west, n_east, w_qkv, q, k, v, gm, gw, ge, bias_w, bias_e, block_pattern,
+        dq, dk, dv, state, cotangent, inverse, oht, slope, w_enc,
     )
     returned = lax.all_to_all(reply, ("lat", "lon"), split_axis=0, concat_axis=0, tiled=True)
     updated, grad_background = call(

time: 65.7 us -> 61.7 us (0.939)
  Pallas kernels: 32.6 us -> 28.3 us
    pallas_call x7, Pallas kernels: 32.6 us -> 28.3 us  [run(): kernel(*[pltpu.with_memory_space_constraint(x, pltpu.HBM) if k in n_hbm e...]
  transfers between devices with their start and end apart: 6 -> 6, of which waited for: 4 -> 4; matrix products, arithmetic and copies ran while one was open for 0% -> 0% of each run, Pallas kernels for 24% -> 23%
where the time goes in v3:
time: 61.7 us; the launch traced here: 61.4 us
  Pallas kernels  28.3 us (46%)
  waiting for transfers between devices  16.2 us (26%)
  starting transfers between devices  15.3 us (25%)
  between operations  1.46 us (2%)
    pallas_call x7, Pallas kernels, run(): kernel(*[pltpu.with_memory_space_constraint(x, pltpu.HBM) if k in n_hbm e...  28.3 us
    all_to_all x1, waiting for transfers between devices, shards(): lax.all_to_all(payload, ('lat', 'lon'), split_axis=0, concat_axis=0, tile...  8.17 us
    all_to_all x1, waiting for transfers between devices, shards(): lax.all_to_all(reply, ('lat', 'lon'), split_axis=0, concat_axis=0, tiled=...  7.28 us
    all_to_all x1, starting transfers between devices, shards(): lax.all_to_all(payload, ('lat', 'lon'), split_axis=0, concat_axis=0, tile...  4.49 us
    ppermute x1, starting transfers between devices, shards(): east_cot = lax.ppermute(cot_west, 'lon', down)  4.1 us
    ppermute x1, starting transfers between devices, shards(): n_east = lax.ppermute(n0, 'lon', down)  3.43 us
    all_to_all x1, starting transfers between devices, shards(): lax.all_to_all(reply, ('lat', 'lon'), split_axis=0, concat_axis=0, tiled=...  2.61 us
  transfers between devices with their start and end apart: 6, of which 4 were waited for; matrix products, arithmetic and copies ran while one was open for 0% of the time, Pallas kernels for 23%

profile of v3, /device:TPU:0, one launch (start us, length us, event | category | flops | bytes accessed | tf_op | source)
XLA Modules:
  0.0 61.4 jit_solution(4916488038004954387)
XLA Ops:
  1.3 2.6 %shard_map.112 = (bf16[32,40,128]{2,1,0:T(8,128)(2,1)}, s32[1,512]{1,0:T(1,128)S(1)}, bf16[17,16,512]{2,1,0:T(8,128)(2,1)}, bf16[17,16,512]{2,1,0:T(8,128)(2,1)}) custom-call(s32[1,512]{1,0:T(1,128)} %bitcast.1, s32[1]{0:T(128)S(6)} %copy.12.cnt_ref, bf16[512,256]{1,0:T(8,128)(2,1)} %rows_hbm.1, s32[2,4,4]{2,1,0:T(4,128)} %pat_hbm.5, ...), custom_call_target="tpu_custom_call" | custom-call | flops 419430400 | bytes 1048576 | tf_op jit(solution)/shard_map/pallas_call | solution.py:69
  3.9 0.5 collective-permute-start
  4.4 4.1 %collective-permute-start.1 = (bf16[17,16,512]{2,1,0:T(8,128)(2,1)}, bf16[17,16,512]{2,1,0:T(8,128)(2,1)S(1)}, u32[]{:S(2)}, u32[]{:S(2)}) collective-permute-start(bf16[17,16,512]{2,1,0:T(8,128)(2,1)} %get-tuple-element.37), channel_id=1, source_target_pairs={{1,0},{2,1},{3,2},{4,3},{5,4},{6,5},{7,6},{0,7},{9,8},{10,9},{11,1... | collective-permute-start | bytes 835592 | tf_op jit(solution)/shard_map/ppermute | solution.py:635
  8.5 4.5 %all-to-all-start = ((bf16[32,40,128]{2,1,0:T(8,128)(2,1)}), bf16[32,40,128]{2,1,0:T(8,128)(2,1)S(1)}, u32[]{:S(2)}, u32[]{:S(2)}) async-start(bf16[32,40,128]{2,1,0:T(8,128)(2,1)} %get-tuple-element.34), calls=%async_computation | async-start | bytes 655360 | tf_op jit(solution)/shard_map/all_to_all | solution.py:636
  13.0 0.0 copy-start.1
  13.0 0.0 copy-start.3
  13.0 0.2 collective-permute-done.west_ref
  13.2 0.6 collective-permute-done.1.east_ref
  13.8 3.1 %shard_map.114 = (bf16[512,512]{1,0:T(8,128)(2,1)}, bf16[256,512]{1,0:T(8,128)(2,1)}, bf16[256,512]{1,0:T(8,128)(2,1)}, f32[256,128]{1,0:T(8,128)}, f32[256,128]{1,0:T(8,128)}) custom-call(bf16[16,32,512]{2,1,0:T(8,128)(2,1)} %cot_ref.1, bf16[17,16,512]{2,1,0:T(8,128)(2,1)S(1)} %collective-permute-done.west_ref, ...), custom_call_target="tpu_custom_call" | custom-call | flops 137438953472 | bytes 1048576 | tf_op jit(solution)/shard_map/pallas_call | solution.py:69
  16.9 0.0 copy-start
  17.0 0.0 copy-start.4
  17.0 8.2 %all-to-all-done.arr_ref = bf16[32,40,128]{2,1,0:T(8,128)(2,1)S(1)} async-done(((bf16[32,40,128]{2,1,0:T(8,128)(2,1)}), bf16[32,40,128]{2,1,0:T(8,128)(2,1)S(1)}, u32[]{:S(2)}, u32[]{:S(2)}) %all-to-all-start) | async-done | bytes 327712 | tf_op jit(solution)/shard_map/all_to_all | solution.py:636
  25.1 0.0 copy-done.1
  25.1 0.0 copy-done.3
  25.1 2.2 %shard_map.113 = (bf16[512,512]{1,0:T(8,128)(2,1)S(1)}, bf16[512,512]{1,0:T(8,128)(2,1)S(1)}, bf16[256,512]{1,0:T(8,128)(2,1)S(1)}, bf16[256,512]{1,0:T(8,128)(2...) custom-call(bf16[32,40,128]{2,1,0:T(8,128)(2,1)S(1)} %all-to-all-done.arr_ref, ...), custom_call_target="tpu_custom_call" | custom-call | flops 1073741824 | bytes 1048576 | tf_op jit(solution)/shard_map/pallas_call | solution.py:69
  27.3 0.2 collective-permute-start.2
  27.5 3.4 %collective-permute-start.3 = (bf16[256,512]{1,0:T(8,128)(2,1)S(1)}, bf16[256,512]{1,0:T(8,128)(2,1)S(1)}, u32[]{:S(2)}, u32[]{:S(2)}) collective-permute-start(bf16[256,512]{1,0:T(8,128)(2,1)S(1)} %get-tuple-element.42), channel_id=1, source_target_pairs={{1,0},{2,1},{3,2},{4,3},{5,4},{6,5},{7,6},{0,7},{9,8},{10,9},{11,1... | collective-permute-start | bytes 786440 | tf_op jit(solution)/shard_map/ppermute | solution.py:669
  30.9 0.0 copy-done
  30.9 0.0 copy-done.4
  30.9 0.0 copy-start.2
  30.9 0.0 copy-start.5
  31.0 0.0 copy-start.6
  31.0 0.0 copy-start.7
  31.0 0.0 copy-start.8
  31.0 6.0 %shard_map.115 = (bf16[512,512]{1,0:T(8,128)(2,1)S(1)}, bf16[512,512]{1,0:T(8,128)(2,1)S(1)}, bf16[512,512]{1,0:T(8,128)(2,1)S(1)}, f32[512,512]{1,0:T(8,128)S(1...) custom-call(bf16[512,512]{1,0:T(8,128)(2,1)S(1)} %get-tuple-element., ...), custom_call_target="tpu_custom_call" | custom-call | flops 4294967296 | bytes 1048576 | tf_op jit(solution)/shard_map/pallas_call | solution.py:69
  37.0 0.0 collective-permute-done.2.nw_ref
  37.0 0.0 collective-permute-done.3.ne_ref
  37.0 0.0 copy-done.2
  37.0 0.0 copy-done.5
  37.0 0.0 copy-done.6
  37.0 0.0 copy-done.7
  37.0 0.0 copy-done.8
  37.0 8.4 %shard_map.116 = (bf16[512,512]{1,0:T(8,128)(2,1)}, bf16[4,4,128,256]{3,2,1,0:T(8,128)(2,1)}, bf16[512,512]{1,0:T(8,128)(2,1)}, bf16[32,40,128]{2,1,0:T(8,128)(2,1)}) custom-call(bf16[256,512]{1,0:T(8,128)(2,1)S(1)} %collective-permute-done.2.nw_ref, bf16[256,512]{1,0:T(8,128)(2,1)S(1)} %collective-permute-done.3.ne_ref, bf16[512,1536]{1,0:T(8,128)(2,1)S(1)} %copy-done, ...), custom_call_target="tpu_custom_call" | custom-call | flops 4294967296 | bytes 1048576 | tf_op jit(solution)/shard_map/pallas_call | solution.py:69
  45.5 2.6 %all-to-all-start.1 = ((bf16[32,40,128]{2,1,0:T(8,128)(2,1)}), bf16[32,40,128]{2,1,0:T(8,128)(2,1)S(1)}, u32[]{:S(2)}, u32[]{:S(2)}) async-start(bf16[32,40,128]{2,1,0:T(8,128)(2,1)} %get-tuple-element.63), calls=%async_computation.1 | async-start | bytes 655360 | tf_op jit(solution)/shard_map/all_to_all | solution.py:695
  48.1 4.9 %shard_map.117 = (bf16[16,32,512]{2,1,0:T(8,128)(2,1)}, bf16[16,32,512]{2,1,0:T(8,128)(2,1)}) custom-call(bf16[2,8,256,256]{3,2,1,0:T(8,128)(2,1)} %get-tuple-element.40.refs_0_, bf16[4,4,128,256]{3,2,1,0:T(8,128)(2,1)} %get-tuple-element.56.refs_1_, bf16[512,512]{1,0:T(8,128)(2,1)} %get-tuple-element.57.refs_2_, ...), custom_call_target="tpu_custom_call" | custom-call | flops 1073741824 | bytes 1048576 | tf_op jit(solution)/shard_map/pallas_call | solution.py:69
  53.0 7.3 %all-to-all-done.1.back_ref = bf16[32,40,128]{2,1,0:T(8,128)(2,1)S(1)} async-done(((bf16[32,40,128]{2,1,0:T(8,128)(2,1)}), bf16[32,40,128]{2,1,0:T(8,128)(2,1)S(1)}, u32[]{:S(2)}, u32[]{:S(2)}) %all-to-all-start.1) | async-done | bytes 327712 | tf_op jit(solution)/shard_map/all_to_all | solution.py:695
  60.2 1.1 %shard_map.118 = bf16[512,256]{1,0:T(8,128)(2,1)} custom-call(bf16[32,40,128]{2,1,0:T(8,128)(2,1)S(1)} %all-to-all-done.1.back_ref, s32[1,512]{1,0:T(1,128)S(1)} %get-tuple-element.64.slot_ref), custom_call_target="tpu_custom_call" | custom-call | flops 268435456 | bytes 1048576 | tf_op jit(solution)/shard_map/pallas_call | solution.py:69
Async XLA Ops:
  3.9 9.3 %collective-permute-start = (bf16[17,16,512]{2,1,0:T(8,128)(2,1)}, bf16[17,16,512]{2,1,0:T(8,128)(2,1)S(1)}, u32[]{:S(2)}, u32[]{:S(2)}) collective-permute-start(bf16[17,16,512]{2,1,0:T(8,128)(2,1)} %get-tuple-element.36), channel_id=1, source_target_pairs={{0,1},{1,2},{2,3},{3,4},{4,5},{5,6},{6,7},{7,0},{8,9},{9,10},{10,1... | collective-permute-start | bytes 835592 | tf_op jit(solution)/shard_map/ppermute | solution.py:634
  4.4 9.4 %collective-permute-start.1 = (bf16[17,16,512]{2,1,0:T(8,128)(2,1)}, bf16[17,16,512]{2,1,0:T(8,128)(2,1)S(1)}, u32[]{:S(2)}, u32[]{:S(2)}) collective-permute-start(bf16[17,16,512]{2,1,0:T(8,128)(2,1)} %get-tuple-element.37), channel_id=1, source_target_pairs={{1,0},{2,1},{3,2},{4,3},{5,4},{6,5},{7,6},{0,7},{9,8},{10,9},{11,1... | collective-permute-start | bytes 835592 | tf_op jit(solution)/shard_map/ppermute | solution.py:635
  8.5 16.6 %all-to-all-start = ((bf16[32,40,128]{2,1,0:T(8,128)(2,1)}), bf16[32,40,128]{2,1,0:T(8,128)(2,1)S(1)}, u32[]{:S(2)}, u32[]{:S(2)}) async-start(bf16[32,40,128]{2,1,0:T(8,128)(2,1)} %get-tuple-element.34), calls=%async_computation | async-start | bytes 655360 | tf_op jit(solution)/shard_map/all_to_all | solution.py:636
  13.0 12.1 %copy-start.1 = (bf16[16,32,512]{2,1,0:T(8,128)(2,1)S(1)}, bf16[16,32,512]{2,1,0:T(8,128)(2,1)}, u32[]{:S(2)}) copy-start(bf16[16,32,512]{2,1,0:T(8,128)(2,1)} %bg_ref.1) | copy-start | bytes 1572868
  13.0 12.1 %copy-start.3 = (bf16[256,512]{1,0:T(8,128)(2,1)S(1)}, bf16[256,512]{1,0:T(8,128)(2,1)}, u32[]{:S(2)}) copy-start(bf16[256,512]{1,0:T(8,128)(2,1)} %wenc_ref.5) | copy-start | bytes 786436
  16.9 14.0 %copy-start = (bf16[512,1536]{1,0:T(8,128)(2,1)S(1)}, bf16[512,1536]{1,0:T(8,128)(2,1)}, u32[]{:S(2)}) copy-start(bf16[512,1536]{1,0:T(8,128)(2,1)} %wqkv_ref.3) | copy-start | bytes 4718596
  17.0 14.0 %copy-start.4 = (bf16[512,512]{1,0:T(8,128)(2,1)S(1)}, bf16[512,512]{1,0:T(8,128)(2,1)}, u32[]{:S(2)}) copy-start(bf16[512,512]{1,0:T(8,128)(2,1)} %get-tuple-element.38.gm_ref) | copy-start | bytes 1572868
  27.3 9.6 %collective-permute-start.2 = (bf16[256,512]{1,0:T(8,128)(2,1)S(1)}, bf16[256,512]{1,0:T(8,128)(2,1)S(1)}, u32[]{:S(2)}, u32[]{:S(2)}) collective-permute-start(bf16[256,512]{1,0:T(8,128)(2,1)S(1)} %get-tuple-element.41), channel_id=1, source_target_pairs={{0,1},{1,2},{2,3},{3,4},{4,5},{5,6},{6,7},{7,0},{8,9},{9,10},{10,1... | collective-permute-start | bytes 786440 | tf_op jit(solution)/shard_map/ppermute | solution.py:668
  27.5 9.5 %collective-permute-start.3 = (bf16[256,512]{1,0:T(8,128)(2,1)S(1)}, bf16[256,512]{1,0:T(8,128)(2,1)S(1)}, u32[]{:S(2)}, u32[]{:S(2)}) collective-permute-start(bf16[256,512]{1,0:T(8,128)(2,1)S(1)} %get-tuple-element.42), channel_id=1, source_target_pairs={{1,0},{2,1},{3,2},{4,3},{5,4},{6,5},{7,6},{0,7},{9,8},{10,9},{11,1... | collective-permute-start | bytes 786440 | tf_op jit(solution)/shard_map/ppermute | solution.py:669
  30.9 6.0 %copy-start.2 = (bf16[16,32,512]{2,1,0:T(8,128)(2,1)S(1)}, bf16[16,32,512]{2,1,0:T(8,128)(2,1)}, u32[]{:S(2)}) copy-start(bf16[16,32,512]{2,1,0:T(8,128)(2,1)} %cot_ref.1) | copy-start | bytes 1572868
  30.9 6.1 %copy-start.5 = (bf16[256,512]{1,0:T(8,128)(2,1)S(1)}, bf16[256,512]{1,0:T(8,128)(2,1)}, u32[]{:S(2)}) copy-start(bf16[256,512]{1,0:T(8,128)(2,1)} %get-tuple-element.46.gw_ref) | copy-start | bytes 786436
  31.0 6.1 %copy-start.6 = (bf16[256,512]{1,0:T(8,128)(2,1)S(1)}, bf16[256,512]{1,0:T(8,128)(2,1)}, u32[]{:S(2)}) copy-start(bf16[256,512]{1,0:T(8,128)(2,1)} %get-tuple-element.47.ge_ref) | copy-start | bytes 786436
  31.0 6.1 %copy-start.7 = (f32[256,128]{1,0:T(8,128)S(1)}, f32[256,128]{1,0:T(8,128)}, u32[]{:S(2)}) copy-start(f32[256,128]{1,0:T(8,128)} %get-tuple-element.48.bw_ref) | copy-start | bytes 393220
  31.0 6.1 %copy-start.8 = (f32[256,128]{1,0:T(8,128)S(1)}, f32[256,128]{1,0:T(8,128)}, u32[]{:S(2)}) copy-start(f32[256,128]{1,0:T(8,128)} %get-tuple-element.49.be_ref) | copy-start | bytes 393220
  45.5 14.8 %all-to-all-start.1 = ((bf16[32,40,128]{2,1,0:T(8,128)(2,1)}), bf16[32,40,128]{2,1,0:T(8,128)(2,1)S(1)}, u32[]{:S(2)}, u32[]{:S(2)}) async-start(bf16[32,40,128]{2,1,0:T(8,128)(2,1)} %get-tuple-element.63), calls=%async_computation.1 | async-start | bytes 655360 | tf_op jit(solution)/shard_map/all_to_all | solution.py:695

commit v4 on v3

--- a/solution.py
+++ b/solution.py
@@ -15,6 +15,9 @@
 SLAB = 128
 MASKED = -1e30
 GRAD_COST = 1 << 37
+GROUPS = 4
+BATCH = 2
+STRIP = 32
 
 norm_eps = 1e-06
 gelu_coef = 0.7978845608028654
@@ -149,6 +152,29 @@
     return extra.astype(bf16)
 
 
+def pipeline(items, stages, extra=None):
+    states = [None] * len(items)
+    extra = extra or {}
+    for step in range(max([len(items) + len(stages) - 1] + [n + 1 for n in extra])):
+        for lag, stage in enumerate(stages):
+            n = step - lag
+            if 0 <= n < len(items):
+                states[n] = stage(items[n], states[n])
+        for task in extra.get(step, ()):
+            task()
+
+
+def batch(items, stages, size):
+    groups = [items[n : n + size] for n in range(0, len(items), size)]
+
+    def lift(stage):
+        return lambda group, states: [
+            stage(item, state) for item, state in zip(group, states or [None] * len(group))
+        ]
+
+    return groups, tuple(lift(stage) for stage in stages)
+
+
 class Geometry:
     def __init__(self, slots, devs, lon_devs, lon_cols):
         self.devs, self.lon_devs = devs, lon_devs
@@ -184,11 +210,23 @@
     return tail, jnp.concatenate(parts, axis=0)
 
 
-def store_bulk(geo, ref, values):
-    half = values.shape[1] // 2
-    if geo.full:
-        ref[:, 0 : geo.full, :] = values[:, 0:half].reshape(geo.devs, geo.full, half)
-        ref[:, geo.full : 2 * geo.full, :] = values[:, half:].reshape(geo.devs, geo.full, half)
+def send_groups(geo, ref, hbm, sems, base, stages):
+    copies = []
+    if not geo.full:
+        copies.append(start_copy(ref, hbm, sems.at[base]))
+        return copies
+    step = geo.devs // GROUPS
+
+    def store(item, values):
+        n, lo, hi = item
+        half = values.shape[1] // 2
+        values = values.astype(bf16)
+        ref[lo:hi, 0 : geo.full, :] = values[:, 0:half].reshape(hi - lo, geo.full, half)
+        ref[lo:hi, geo.full : 2 * geo.full, :] = values[:, half:].reshape(hi - lo, geo.full, half)
+        copies.append(start_copy(ref.at[lo:hi], hbm.at[lo:hi], sems.at[base + n]))
+
+    pipeline([(n, n * step, (n + 1) * step) for n in range(GROUPS)], tuple(stages) + (store,))
+    return copies
 
 
 def slot_index(geo, owner, rank, live):
@@ -262,12 +300,15 @@
     second = one_hot(place == line + geo.shift)
     rows_copy.wait()
     half = rows_ref.shape[1] // 2
-    if geo.full:
-        spread = one_hot(iota((geo.bulk, slots), 0) == slot)
-        store_bulk(geo, pay_ref, mm(spread, rows_ref[...]).astype(bf16))
     tail = mm(first, rows_ref[:, 0:half]) + mm(second, rows_ref[:, half:]) + lifted
     pay_ref[:, 2 * geo.full : geo.rows, :] = tail.astype(bf16).reshape(geo.devs, geo.tail, half)
-    outs.append(start_copy(pay_ref, pay_hbm, sems.at[7]))
+
+    def spread(item, _):
+        base = item[1] * geo.full
+        hot = one_hot(iota(((item[2] - item[1]) * geo.full, slots), 0) + base == slot)
+        return mm(hot, rows_ref[...])
+
+    outs += send_groups(geo, pay_ref, pay_hbm, sems, 7, (spread,))
     for copy in outs:
         copy.wait()
 
@@ -312,18 +353,16 @@
         copy.wait()
 
 
-def state_body(geo, arr_ref, wenc_ref, bg_ref, state_ref, n_ref, n0_ref, n1_ref, inv_ref, oht_ref):
-    devs, feats = geo.devs, wenc_ref.shape[0]
-    tails, arr = join_slots(geo, arr_ref, feats)
+def slot_table(geo, tails, pixels):
     pick = one_hot(
-        iota((devs, devs * geo.tail), 1) == iota((devs, devs * geo.tail), 0) * geo.tail + geo.mark
+        iota((geo.devs, geo.devs * geo.tail), 1) == iota((geo.devs, geo.devs * geo.tail), 0) * geo.tail + geo.mark
     )
     meta = mm(pick, tails).astype(bf16)
     codes = []
     if geo.full:
-        shape = (devs, geo.full, devs)
-        owner = one_hot(iota(shape, 0) == iota(shape, 2)).reshape(geo.bulk, devs)
-        place = iota((devs, geo.full, 128), 1).reshape(geo.bulk, 128)
+        shape = (geo.devs, geo.full, geo.devs)
+        owner = one_hot(iota(shape, 0) == iota(shape, 2)).reshape(geo.bulk, geo.devs)
+        place = iota((geo.devs, geo.full, 128), 1).reshape(geo.bulk, 128)
         lane = iota((geo.bulk, 128), 1)
         scale = jnp.where(lane == place, 32.0, 0.0) + jnp.where(lane == place + 64, 1.0, 0.0)
         codes.append(jnp.sum(mm(owner, meta) * scale, axis=1, keepdims=True))
@@ -331,8 +370,13 @@
     for r in range(geo.full, geo.cap):
         codes.append(spare[:, r : r + 1] * 32.0 + spare[:, 64 + r : 65 + r])
     code = jnp.concatenate(codes, axis=0).astype(i32)
-    pixels = n_ref.shape[0]
-    oht = one_hot(code == iota((geo.total, pixels), 1) + 1)
+    return one_hot(code == iota((geo.total, pixels), 1) + 1)
+
+
+def state_body(geo, arr_ref, wenc_ref, bg_ref, state_ref, n_ref, n0_ref, n1_ref, inv_ref, rms_ref, oht_ref):
+    feats = wenc_ref.shape[0]
+    tails, arr = join_slots(geo, arr_ref, feats)
+    oht = slot_table(geo, tails, n_ref.shape[0])
     oht_ref[...] = oht
     pre = mm(arr, wenc_ref[...])
     _, tangent = gelu_parts(pre)
@@ -348,6 +392,7 @@
         state_ref[rows, :] = state
         wide_state = state.astype(f32)
         inv_rms = lax.rsqrt(jnp.mean(wide_state * wide_state, axis=1, keepdims=True) + norm_eps)
+        rms_ref[rows, :] = jnp.broadcast_to(inv_rms, (TILE, 128))
         normed = (wide_state * inv_rms).astype(bf16)
         n_ref[rows, :] = normed
         side = n1_ref if u else n0_ref
@@ -362,6 +407,10 @@
     return [jnp.where(head_lanes(slab.shape, h), slab, jnp.zeros((), slab.dtype)) for h in range(2)]
 
 
+def across(lanes, width):
+    return jnp.concatenate([lanes] * (width // lanes.shape[1]), axis=1)
+
+
 def stack_heads(slab):
     return jnp.concatenate(split_heads(slab), axis=0)
 
@@ -372,19 +421,9 @@
     return weight.astype(bf16), slope.astype(bf16)
 
 
-def pipeline(items, stages):
-    states = [None] * len(items)
-    for step in range(len(items) + len(stages) - 1):
-        for lag, stage in enumerate(stages):
-            n = step - lag
-            if 0 <= n < len(items):
-                states[n] = stage(items[n], states[n])
-
-
 def project(src, wqkv_ref, q_ref, k_ref, v_ref, rows):
     chans = src.shape[1]
-    queries = mm(src, wqkv_ref[:, 0:chans]).astype(bf16).astype(f32) * 0.0625
-    q_ref[rows, :] = queries.astype(bf16)
+    q_ref[rows, :] = (mm(src, wqkv_ref[:, 0:chans]) * 0.0625).astype(bf16)
     k_ref[rows, :] = mm(src, wqkv_ref[:, chans : 2 * chans]).astype(bf16)
     v_ref[rows, :] = mm(src, wqkv_ref[:, 2 * chans : 3 * chans]).astype(bf16)
 
@@ -426,7 +465,7 @@
         weight_ref[i, 2 * s + h] = weight
         return km, weight, slope
 
-    held = {}
+    held, weight_copies = {}, []
 
     def third(item, state):
         i, s, h = item
@@ -445,34 +484,35 @@
         dq_ref[keys, lanes] = before[0] + parts[0]
         dk_ref[keys, lanes] = jnp.where(lower, before[1], parts[1])
         dv_ref[keys, lanes] = jnp.where(lower, before[2], parts[2])
+        pair = (i, slice(2 * s, 2 * s + 2))
+        sem = sems.at[3 + i * (chans // SLAB) + s]
+        weight_copies.append(start_copy(weight_ref.at[pair], weight_hbm.at[pair], sem))
 
     pipeline(
         [(i, s, h) for i in range(2) for s in range(chans // SLAB) for h in range(2)],
         (first, second, third),
     )
-    weight_copy = start_copy(weight_ref, weight_hbm, sems.at[3])
-    pre = mm(join_slots(geo, arr_ref, wenc_ref.shape[0])[1], wenc_ref[...])
+    arr = join_slots(geo, arr_ref, wenc_ref.shape[0])[1]
+    pre = mm(arr, wenc_ref[...])
     square, tangent = gelu_parts(pre)
     slope_ref[...] = 0.5 * (1.0 + tangent) + 0.5 * pre * (1.0 - tangent * tangent) * gelu_coef * (
         1.0 + 3.0 * 0.044715 * square
     )
-    for copy in (state_copy, v_copy, weight_copy):
+    for copy in [state_copy, v_copy] + weight_copies:
         copy.wait()
 
 
 def rim_body(
     geo, nw_ref, ne_ref, wqkv_ref, q_ref, k_ref, v_ref, gm_ref, gw_ref, ge_ref,
-    bw_ref, be_ref, pat_hbm, dq_ref, dk_ref, dv_ref, state_ref, cot_ref, inv_ref,
+    bw_ref, be_ref, pat_hbm, dq_ref, dk_ref, dv_ref, state_ref, rms_ref, cot_ref, inv_ref,
     oht_ref, slope_ref, wenc_ref,
     v_hbm, weight_hbm, gback_hbm, reply_hbm,
-    pat_ref, rim_q, rim_k, rim_v, weight_ref, gback_ref, grad_ref, reply_ref, sems,
+    pat_ref, rim_q, rim_k, rim_v, weight_ref, gback_ref, scaled_ref, grad_ref, reply_ref, tail_ref, sems,
 ):
     chans = q_ref.shape[1]
     pat_copy = start_copy(pat_hbm, pat_ref, sems.at[0])
-    for side, src in enumerate((nw_ref, ne_ref)):
-        rows = slice(side * 2 * TILE, (side + 1) * 2 * TILE)
-        project(src[...], wqkv_ref, rim_q, rim_k, rim_v, rows)
-    v_copy = start_copy(rim_v, v_hbm, sems.at[1])
+    far_rows = [slice(side * 2 * TILE, (side + 1) * 2 * TILE) for side in range(2)]
+    project(nw_ref[...], wqkv_ref, rim_q, rim_k, rim_v, far_rows[0])
     pat_copy.wait()
     out_bias, in_bias = {}, {}
     for i in range(2):
@@ -526,39 +566,62 @@
             spot = slice(n * chans + lanes.start, n * chans + lanes.stop)
             grad_ref[own, spot] = total.astype(bf16)
 
-    pipeline(
-        [(i, side, s) for i in range(2) for side in range(2) for s in range(chans // SLAB)],
-        (first, second, third),
-    )
+    back = {}
+
+    def project_back(group):
+        back[group] = mm(grad_ref[rows_of(*group), :], wqkv_ref[...], 1, 1)
+
+    def norm_back(item):
+        i, u = item
+        total = back.pop(item)
+        cot = chunk(cot_ref, i, u)
+        for n in range(0, TILE, STRIP):
+            base = rows_of(i, u).start + n
+            rows = slice(base, base + STRIP)
+            inv_rms = across(rms_ref[rows, :], chans)
+            normed = state_ref[rows, :].astype(f32) * inv_rms
+            grad = total[n : n + STRIP]
+            grad_state = cot[n : n + STRIP].astype(f32) + inv_rms * (
+                grad - normed * jnp.mean(grad * normed, axis=1, keepdims=True)
+            )
+            gback_ref[rows, :] = grad_state.astype(bf16)
+            scaled_ref[rows, :] = (grad_state * across(inv_ref[rows, :], chans)).astype(bf16)
+
+    slabs = chans // SLAB
+    groups = [(i, side) for side in range(2) for i in range(2)]
+    extra = {
+        1: [lambda: project(ne_ref[...], wqkv_ref, rim_q, rim_k, rim_v, far_rows[1])],
+    }
+    for n, group in enumerate(groups):
+        ready = slabs * (n + 1) // BATCH + 1
+        extra.setdefault(ready, []).append(functools.partial(project_back, group))
+        extra.setdefault(ready + 1, []).append(functools.partial(norm_back, group))
+    items = [(i, side, s) for i, side in groups for s in range(slabs)]
+    pipeline(*batch(items, (first, second, third), BATCH), extra)
+    v_copy = start_copy(rim_v, v_hbm, sems.at[1])
     weight_copy = start_copy(weight_ref, weight_hbm, sems.at[2])
-    scaled = []
-    for i, u in halves():
-        rows = rows_of(i, u)
-        grad = mm(grad_ref[rows, :], wqkv_ref[...], 1, 1)
-        state = state_ref[rows, :].astype(f32)
-        inv_rms = lax.rsqrt(jnp.mean(state * state, axis=1, keepdims=True) + norm_eps)
-        normed = state * inv_rms
-        grad_state = chunk(cot_ref, i, u).astype(f32) + inv_rms * (
-            grad - normed * jnp.mean(grad * normed, axis=1, keepdims=True)
-        )
-        gback_ref[rows, :] = grad_state.astype(bf16)
-        scaled.append((grad_state * inv_ref[rows, 0:1]).astype(bf16))
     gback_copy = start_copy(gback_ref, gback_hbm, sems.at[3])
-    scaled = jnp.concatenate(scaled, axis=0)
-    grad_enc = mm(oht_ref[...], scaled)
-    grad_pre = (grad_enc * slope_ref[...]).astype(bf16)
-    reply = mm(grad_pre, wenc_ref[...], 1, 1).astype(bf16)
-    store_bulk(geo, reply_ref, reply[0 : geo.bulk])
-    half = reply.shape[1] // 2
-    tail = jnp.zeros((geo.devs * geo.tail, half), f32)
+
+    def pre_grad(lo, hi):
+        return (mm(oht_ref[lo:hi, :], scaled_ref[...]) * slope_ref[lo:hi, :]).astype(bf16)
+
+    half = wenc_ref.shape[0] // 2
+    tail_ref[...] = jnp.zeros(tail_ref.shape, f32)
     if geo.rest:
+        spare = mm(pre_grad(geo.bulk, geo.total), wenc_ref[...], 1, 1)
         for n in range(2):
-            tail = tail + mm(
-                tail_picks(geo, n * geo.shift), reply[geo.bulk :, n * half : (n + 1) * half], 0, 0
-            )
-    reply_ref[:, 2 * geo.full : geo.rows, :] = tail.astype(bf16).reshape(geo.devs, geo.tail, half)
-    reply_copy = start_copy(reply_ref, reply_hbm, sems.at[4])
-    for copy in (v_copy, weight_copy, gback_copy, reply_copy):
+            for r in range(geo.rest):
+                part = spare[r * geo.devs : (r + 1) * geo.devs, n * half : (n + 1) * half]
+                tail_ref[:, n * geo.shift + r, :] = part
+    reply_ref[:, 2 * geo.full : geo.rows, :] = tail_ref[...].astype(bf16)
+    replies = send_groups(
+        geo, reply_ref, reply_hbm, sems, 4,
+        (
+            lambda item, _: pre_grad(item[1] * geo.full, item[2] * geo.full),
+            lambda item, rows: mm(rows, wenc_ref[...], 1, 1),
+        ),
+    )
+    for copy in [v_copy, weight_copy, gback_copy] + replies:
         copy.wait()
 
 
@@ -589,11 +652,18 @@
         back_ref[place[0], place[1], :] = gback_ref[rows, :].reshape(BLOCK, HALF, chans)
 
 
-def unpack_body(geo, back_ref, slot_ref, out_ref):
-    feats = out_ref.shape[1]
-    slots = slot_ref.shape[1]
-    spread = one_hot(iota((geo.total, slots), 0) == slot_ref[...])
-    out_ref[...] = mm(spread, join_slots(geo, back_ref, feats)[1], 0, 0).astype(bf16)
+def unpack_body(geo, back_ref, slot_ref, out_hbm, out_ref, sems):
+    slots, feats = out_ref.shape
+    rows = join_slots(geo, back_ref, feats)[1]
+    step = slots // GROUPS
+    copies = []
+    for n in range(GROUPS):
+        part = slice(n * step, (n + 1) * step)
+        spread = one_hot(iota((geo.total, step), 0) == slot_ref[:, part])
+        out_ref[part, :] = mm(spread, rows, 0, 0).astype(bf16)
+        copies.append(start_copy(out_ref.at[part], out_hbm.at[part], sems.at[n]))
+    for copy in copies:
+        copy.wait()
 
 
 def shards(
@@ -624,7 +694,7 @@
         [((geo.devs, geo.rows, half), bf16), ((1, slots), i32), (rim, bf16), (rim, bf16)],
         scratch=[pltpu.VMEM((1, slots), i32), pltpu.VMEM((slots, feats), bf16), pattern]
         + vmem((geo.devs, geo.rows, half), rim, rim)
-        + [dma((8,))],
+        + [dma((7 + GROUPS,))],
         n_in=5,
         n_smem=(1,),
         n_hbm=(0, 2, 3, 4),
@@ -652,13 +722,14 @@
         out_hbm=range(5),
         flops=GRAD_COST,
     )(cotangent, west_cot, east_cot, w_out)
-    state, normed, n0, n1, inverse, oht = call(
+    state, normed, n0, n1, inverse, inv_rms, oht = call(
         functools.partial(state_body, geo),
         [
             (wide, bf16),
             (wide, bf16),
             (edge, bf16),
             (edge, bf16),
+            ((pixels, 128), f32),
             ((pixels, 128), f32),
             ((geo.total, pixels), bf16),
         ],
@@ -672,7 +743,7 @@
         [(wide, bf16)] * 3
         + [(wide, f32)] * 3
         + [((geo.total, chans), f32), (weights_own, bf16), (wide, bf16), (wide, bf16)],
-        scratch=[pattern] + vmem(weights_own) + [dma((4,))],
+        scratch=[pattern] + vmem(weights_own) + [dma((3 + HEADS,))],
         n_in=7,
         n_hbm=(3,),
         out_hbm=(7, 8, 9),
@@ -682,15 +753,15 @@
         functools.partial(rim_body, geo),
         [(wide, bf16), (weights_far, bf16), (wide, bf16), ((geo.devs, geo.rows, half), bf16)],
         scratch=[pattern]
-        + vmem(wide, wide, wide, weights_far, wide, (pixels, 3 * chans), (geo.devs, geo.rows, half))
-        + [dma((5,))],
-        n_in=21,
+        + vmem(wide, wide, wide, weights_far, wide, wide, (pixels, 3 * chans), (geo.devs, geo.rows, half))
+        + [pltpu.VMEM((geo.devs, geo.tail, half), f32), dma((4 + GROUPS,))],
+        n_in=22,
         n_hbm=(11,),
         out_hbm=(0, 1, 2, 3),
         flops=4 << 30,
     )(
         n_west, n_east, w_qkv, q, k, v, gm, gw, ge, bias_w, bias_e, block_pattern,
-        dq, dk, dv, state, cotangent, inverse, oht, slope, w_enc,
+        dq, dk, dv, state, inv_rms, cotangent, inverse, oht, slope, w_enc,
     )
     returned = lax.all_to_all(reply, ("lat", "lon"), split_axis=0, concat_axis=0, tiled=True)
     updated, grad_background = call(
@@ -703,7 +774,12 @@
         flops=1 << 30,
     )(weight, far, v_far, rim_v, w_out, state_far, gback)
     (grad_obs,) = call(
-        functools.partial(unpack_body, geo), [((slots, feats), bf16)], n_in=2, flops=1 << 28
+        functools.partial(unpack_body, geo),
+        [((slots, feats), bf16)],
+        scratch=vmem((slots, feats)) + [dma((GROUPS,))],
+        n_in=2,
+        out_hbm=(0,),
+        flops=1 << 28,
     )(returned, slot)
     return (updated, grad_background, grad_obs)
 

time: 61.7 us -> 60.9 us (0.987)
  Pallas kernels: 28.3 us -> 27.3 us
    pallas_call x7, Pallas kernels: 28.3 us -> 27.3 us  [run(): kernel(*[pltpu.with_memory_space_constraint(x, pltpu.HBM) if k in n_hbm e...]
  transfers between devices with their start and end apart: 6 -> 6, of which waited for: 4 -> 4; matrix products, arithmetic and copies ran while one was open for 0% -> 0% of each run, Pallas kernels for 23% -> 22%
where the time goes in v4:
time: 60.9 us; the launch traced here: 60.5 us
  Pallas kernels  27.3 us (45%)
  waiting for transfers between devices  16.2 us (27%)
  starting transfers between devices  15.3 us (25%)
  between operations  1.62 us (3%)
    pallas_call x7, Pallas kernels, run(): kernel(*[pltpu.with_memory_space_constraint(x, pltpu.HBM) if k in n_hbm e...  27.3 us
    all_to_all x1, waiting for transfers between devices, shards(): lax.all_to_all(payload, ('lat', 'lon'), split_axis=0, concat_axis=0, tile...  8.17 us
    all_to_all x1, waiting for transfers between devices, shards(): lax.all_to_all(reply, ('lat', 'lon'), split_axis=0, concat_axis=0, tiled=...  7.27 us
    all_to_all x1, starting transfers between devices, shards(): lax.all_to_all(payload, ('lat', 'lon'), split_axis=0, concat_axis=0, tile...  4.49 us
    ppermute x1, starting transfers between devices, shards(): east_cot = lax.ppermute(cot_west, 'lon', down)  4.1 us
    ppermute x1, starting transfers between devices, shards(): n_east = lax.ppermute(n0, 'lon', down)  3.43 us
    all_to_all x1, starting transfers between devices, shards(): lax.all_to_all(reply, ('lat', 'lon'), split_axis=0, concat_axis=0, tiled=...  2.61 us
  transfers between devices with their start and end apart: 6, of which 4 were waited for; matrix products, arithmetic and copies ran while one was open for 0% of the time, Pallas kernels for 22%

profile of v4, /device:TPU:0, one launch (start us, length us, event | category | flops | bytes accessed | tf_op | source)
XLA Modules:
  0.0 60.5 jit_solution(3294877946311335876)
XLA Ops:
  1.3 2.6 %shard_map.112 = (bf16[32,40,128]{2,1,0:T(8,128)(2,1)}, s32[1,512]{1,0:T(1,128)S(1)}, bf16[17,16,512]{2,1,0:T(8,128)(2,1)}, bf16[17,16,512]{2,1,0:T(8,128)(2,1)}) custom-call(s32[1,512]{1,0:T(1,128)} %bitcast.1, s32[1]{0:T(128)S(6)} %copy.12.cnt_ref, bf16[512,256]{1,0:T(8,128)(2,1)} %rows_hbm.1, s32[2,4,4]{2,1,0:T(4,128)} %pat_hbm.5, ...), custom_call_target="tpu_custom_call" | custom-call | flops 419430400 | bytes 1048576 | tf_op jit(solution)/shard_map/pallas_call | solution.py:72
  3.8 0.5 collective-permute-start
  4.4 4.1 %collective-permute-start.1 = (bf16[17,16,512]{2,1,0:T(8,128)(2,1)}, bf16[17,16,512]{2,1,0:T(8,128)(2,1)S(1)}, u32[]{:S(2)}, u32[]{:S(2)}) collective-permute-start(bf16[17,16,512]{2,1,0:T(8,128)(2,1)} %get-tuple-element.38), channel_id=1, source_target_pairs={{1,0},{2,1},{3,2},{4,3},{5,4},{6,5},{7,6},{0,7},{9,8},{10,9},{11,1... | collective-permute-start | bytes 835592 | tf_op jit(solution)/shard_map/ppermute | solution.py:705
  8.5 4.5 %all-to-all-start = ((bf16[32,40,128]{2,1,0:T(8,128)(2,1)}), bf16[32,40,128]{2,1,0:T(8,128)(2,1)S(1)}, u32[]{:S(2)}, u32[]{:S(2)}) async-start(bf16[32,40,128]{2,1,0:T(8,128)(2,1)} %get-tuple-element.35), calls=%async_computation | async-start | bytes 655360 | tf_op jit(solution)/shard_map/all_to_all | solution.py:706
  13.0 0.0 copy-start.1
  13.0 0.0 copy-start.3
  13.0 0.2 collective-permute-done.west_ref
  13.1 0.6 %collective-permute-done.1.east_ref = bf16[17,16,512]{2,1,0:T(8,128)(2,1)S(1)} collective-permute-done((bf16[17,16,512]{2,1,0:T(8,128)(2,1)}, bf16[17,16,512]{2,1,0:T(8,128)(2,1)S(1)}, u32[]{:S(2)}, u32[]{:S(2)}) %collective-permute-start.1) | collective-permute-done | bytes 278560 | tf_op jit(solution)/shard_map/ppermute | solution.py:705
  13.8 3.1 %shard_map.114 = (bf16[512,512]{1,0:T(8,128)(2,1)}, bf16[256,512]{1,0:T(8,128)(2,1)}, bf16[256,512]{1,0:T(8,128)(2,1)}, f32[256,128]{1,0:T(8,128)}, f32[256,128]{1,0:T(8,128)}) custom-call(bf16[16,32,512]{2,1,0:T(8,128)(2,1)} %cot_ref.1, bf16[17,16,512]{2,1,0:T(8,128)(2,1)S(1)} %collective-permute-done.west_ref, ...), custom_call_target="tpu_custom_call" | custom-call | flops 137438953472 | bytes 1048576 | tf_op jit(solution)/shard_map/pallas_call | solution.py:72
  16.9 0.0 copy-start
  16.9 0.0 copy-start.4
  16.9 8.2 %all-to-all-done.arr_ref = bf16[32,40,128]{2,1,0:T(8,128)(2,1)S(1)} async-done(((bf16[32,40,128]{2,1,0:T(8,128)(2,1)}), bf16[32,40,128]{2,1,0:T(8,128)(2,1)S(1)}, u32[]{:S(2)}, u32[]{:S(2)}) %all-to-all-start) | async-done | bytes 327712 | tf_op jit(solution)/shard_map/all_to_all | solution.py:706
  25.1 0.0 copy-done.1
  25.1 0.0 copy-done.3
  25.1 2.2 %shard_map.113 = (bf16[512,512]{1,0:T(8,128)(2,1)S(1)}, bf16[512,512]{1,0:T(8,128)(2,1)S(1)}, bf16[256,512]{1,0:T(8,128)(2,1)S(1)}, bf16[256,512]{1,0:T(8,128)(2...) custom-call(bf16[32,40,128]{2,1,0:T(8,128)(2,1)S(1)} %all-to-all-done.arr_ref, ...), custom_call_target="tpu_custom_call" | custom-call | flops 1073741824 | bytes 1048576 | tf_op jit(solution)/shard_map/pallas_call | solution.py:72
  27.3 0.2 collective-permute-start.2
  27.5 3.4 %collective-permute-start.3 = (bf16[256,512]{1,0:T(8,128)(2,1)S(1)}, bf16[256,512]{1,0:T(8,128)(2,1)S(1)}, u32[]{:S(2)}, u32[]{:S(2)}) collective-permute-start(bf16[256,512]{1,0:T(8,128)(2,1)S(1)} %get-tuple-element.43), channel_id=1, source_target_pairs={{1,0},{2,1},{3,2},{4,3},{5,4},{6,5},{7,6},{0,7},{9,8},{10,9},{11,1... | collective-permute-start | bytes 786440 | tf_op jit(solution)/shard_map/ppermute | solution.py:740
  30.9 0.0 copy-done
  30.9 0.0 copy-done.4
  30.9 0.0 copy-start.2
  30.9 0.0 copy-start.5
  30.9 0.0 copy-start.6
  30.9 0.0 copy-start.7
  30.9 0.0 copy-start.8
  30.9 5.4 %shard_map.115 = (bf16[512,512]{1,0:T(8,128)(2,1)S(1)}, bf16[512,512]{1,0:T(8,128)(2,1)S(1)}, bf16[512,512]{1,0:T(8,128)(2,1)S(1)}, f32[512,512]{1,0:T(8,128)S(1...) custom-call(bf16[512,512]{1,0:T(8,128)(2,1)S(1)} %get-tuple-element., ...), custom_call_target="tpu_custom_call" | custom-call | flops 4294967296 | bytes 1048576 | tf_op jit(solution)/shard_map/pallas_call | solution.py:72
  36.3 0.0 collective-permute-done.2.nw_ref
  36.3 0.0 collective-permute-done.3.ne_ref
  36.3 0.0 copy-done.2
  36.3 0.0 copy-done.5
  36.3 0.0 copy-done.6
  36.4 0.0 copy-done.7
  36.4 0.0 copy-done.8
  36.4 8.1 %shard_map.116 = (bf16[512,512]{1,0:T(8,128)(2,1)}, bf16[4,4,128,256]{3,2,1,0:T(8,128)(2,1)}, bf16[512,512]{1,0:T(8,128)(2,1)}, bf16[32,40,128]{2,1,0:T(8,128)(2,1)}) custom-call(bf16[256,512]{1,0:T(8,128)(2,1)S(1)} %collective-permute-done.2.nw_ref, bf16[256,512]{1,0:T(8,128)(2,1)S(1)} %collective-permute-done.3.ne_ref, bf16[512,1536]{1,0:T(8,128)(2,1)S(1)} %copy-done, ...), custom_call_target="tpu_custom_call" | custom-call | flops 4294967296 | bytes 1048576 | tf_op jit(solution)/shard_map/pallas_call | solution.py:72
  44.5 2.6 %all-to-all-start.1 = ((bf16[32,40,128]{2,1,0:T(8,128)(2,1)}), bf16[32,40,128]{2,1,0:T(8,128)(2,1)S(1)}, u32[]{:S(2)}, u32[]{:S(2)}) async-start(bf16[32,40,128]{2,1,0:T(8,128)(2,1)} %get-tuple-element.65), calls=%async_computation.1 | async-start | bytes 655360 | tf_op jit(solution)/shard_map/all_to_all | solution.py:766
  47.1 4.9 %shard_map.117 = (bf16[16,32,512]{2,1,0:T(8,128)(2,1)}, bf16[16,32,512]{2,1,0:T(8,128)(2,1)}) custom-call(bf16[2,8,256,256]{3,2,1,0:T(8,128)(2,1)} %get-tuple-element.41.refs_0_, bf16[4,4,128,256]{3,2,1,0:T(8,128)(2,1)} %get-tuple-element.58.refs_1_, bf16[512,512]{1,0:T(8,128)(2,1)} %get-tuple-element.59.refs_2_, ...), custom_call_target="tpu_custom_call" | custom-call | flops 1073741824 | bytes 1048576 | tf_op jit(solution)/shard_map/pallas_call | solution.py:72
  52.0 7.3 %all-to-all-done.1.back_ref = bf16[32,40,128]{2,1,0:T(8,128)(2,1)S(1)} async-done(((bf16[32,40,128]{2,1,0:T(8,128)(2,1)}), bf16[32,40,128]{2,1,0:T(8,128)(2,1)S(1)}, u32[]{:S(2)}, u32[]{:S(2)}) %all-to-all-start.1) | async-done | bytes 327712 | tf_op jit(solution)/shard_map/all_to_all | solution.py:766
  59.3 1.1 %shard_map.118 = bf16[512,256]{1,0:T(8,128)(2,1)} custom-call(bf16[32,40,128]{2,1,0:T(8,128)(2,1)S(1)} %all-to-all-done.1.back_ref, s32[1,512]{1,0:T(1,128)S(1)} %get-tuple-element.66.slot_ref), custom_call_target="tpu_custom_call" | custom-call | flops 268435456 | bytes 1048576 | tf_op jit(solution)/shard_map/pallas_call | solution.py:72
Async XLA Ops:
  3.8 9.3 %collective-permute-start = (bf16[17,16,512]{2,1,0:T(8,128)(2,1)}, bf16[17,16,512]{2,1,0:T(8,128)(2,1)S(1)}, u32[]{:S(2)}, u32[]{:S(2)}) collective-permute-start(bf16[17,16,512]{2,1,0:T(8,128)(2,1)} %get-tuple-element.37), channel_id=1, source_target_pairs={{0,1},{1,2},{2,3},{3,4},{4,5},{5,6},{6,7},{7,0},{8,9},{9,10},{10,1... | collective-permute-start | bytes 835592 | tf_op jit(solution)/shard_map/ppermute | solution.py:704
  4.4 9.4 %collective-permute-start.1 = (bf16[17,16,512]{2,1,0:T(8,128)(2,1)}, bf16[17,16,512]{2,1,0:T(8,128)(2,1)S(1)}, u32[]{:S(2)}, u32[]{:S(2)}) collective-permute-start(bf16[17,16,512]{2,1,0:T(8,128)(2,1)} %get-tuple-element.38), channel_id=1, source_target_pairs={{1,0},{2,1},{3,2},{4,3},{5,4},{6,5},{7,6},{0,7},{9,8},{10,9},{11,1... | collective-permute-start | bytes 835592 | tf_op jit(solution)/shard_map/ppermute | solution.py:705
  8.5 16.6 %all-to-all-start = ((bf16[32,40,128]{2,1,0:T(8,128)(2,1)}), bf16[32,40,128]{2,1,0:T(8,128)(2,1)S(1)}, u32[]{:S(2)}, u32[]{:S(2)}) async-start(bf16[32,40,128]{2,1,0:T(8,128)(2,1)} %get-tuple-element.35), calls=%async_computation | async-start | bytes 655360 | tf_op jit(solution)/shard_map/all_to_all | solution.py:706
  13.0 12.1 %copy-start.1 = (bf16[16,32,512]{2,1,0:T(8,128)(2,1)S(1)}, bf16[16,32,512]{2,1,0:T(8,128)(2,1)}, u32[]{:S(2)}) copy-start(bf16[16,32,512]{2,1,0:T(8,128)(2,1)} %bg_ref.1) | copy-start | bytes 1572868
  13.0 12.1 %copy-start.3 = (bf16[256,512]{1,0:T(8,128)(2,1)S(1)}, bf16[256,512]{1,0:T(8,128)(2,1)}, u32[]{:S(2)}) copy-start(bf16[256,512]{1,0:T(8,128)(2,1)} %wenc_ref.5) | copy-start | bytes 786436
  16.9 14.0 %copy-start = (bf16[512,1536]{1,0:T(8,128)(2,1)S(1)}, bf16[512,1536]{1,0:T(8,128)(2,1)}, u32[]{:S(2)}) copy-start(bf16[512,1536]{1,0:T(8,128)(2,1)} %wqkv_ref.3) | copy-start | bytes 4718596
  16.9 14.0 %copy-start.4 = (bf16[512,512]{1,0:T(8,128)(2,1)S(1)}, bf16[512,512]{1,0:T(8,128)(2,1)}, u32[]{:S(2)}) copy-start(bf16[512,512]{1,0:T(8,128)(2,1)} %get-tuple-element.39.gm_ref) | copy-start | bytes 1572868
  27.3 9.0 %collective-permute-start.2 = (bf16[256,512]{1,0:T(8,128)(2,1)S(1)}, bf16[256,512]{1,0:T(8,128)(2,1)S(1)}, u32[]{:S(2)}, u32[]{:S(2)}) collective-permute-start(bf16[256,512]{1,0:T(8,128)(2,1)S(1)} %get-tuple-element.42), channel_id=1, source_target_pairs={{0,1},{1,2},{2,3},{3,4},{4,5},{5,6},{6,7},{7,0},{8,9},{9,10},{10,1... | collective-permute-start | bytes 786440 | tf_op jit(solution)/shard_map/ppermute | solution.py:739
  27.5 8.9 %collective-permute-start.3 = (bf16[256,512]{1,0:T(8,128)(2,1)S(1)}, bf16[256,512]{1,0:T(8,128)(2,1)S(1)}, u32[]{:S(2)}, u32[]{:S(2)}) collective-permute-start(bf16[256,512]{1,0:T(8,128)(2,1)S(1)} %get-tuple-element.43), channel_id=1, source_target_pairs={{1,0},{2,1},{3,2},{4,3},{5,4},{6,5},{7,6},{0,7},{9,8},{10,9},{11,1... | collective-permute-start | bytes 786440 | tf_op jit(solution)/shard_map/ppermute | solution.py:740
  30.9 5.4 %copy-start.2 = (bf16[16,32,512]{2,1,0:T(8,128)(2,1)S(1)}, bf16[16,32,512]{2,1,0:T(8,128)(2,1)}, u32[]{:S(2)}) copy-start(bf16[16,32,512]{2,1,0:T(8,128)(2,1)} %cot_ref.1) | copy-start | bytes 1572868
  30.9 5.4 %copy-start.5 = (bf16[256,512]{1,0:T(8,128)(2,1)S(1)}, bf16[256,512]{1,0:T(8,128)(2,1)}, u32[]{:S(2)}) copy-start(bf16[256,512]{1,0:T(8,128)(2,1)} %get-tuple-element.47.gw_ref) | copy-start | bytes 786436
  30.9 5.4 %copy-start.6 = (bf16[256,512]{1,0:T(8,128)(2,1)S(1)}, bf16[256,512]{1,0:T(8,128)(2,1)}, u32[]{:S(2)}) copy-start(bf16[256,512]{1,0:T(8,128)(2,1)} %get-tuple-element.48.ge_ref) | copy-start | bytes 786436
  30.9 5.4 %copy-start.7 = (f32[256,128]{1,0:T(8,128)S(1)}, f32[256,128]{1,0:T(8,128)}, u32[]{:S(2)}) copy-start(f32[256,128]{1,0:T(8,128)} %get-tuple-element.49.bw_ref) | copy-start | bytes 393220
  30.9 5.4 %copy-start.8 = (f32[256,128]{1,0:T(8,128)S(1)}, f32[256,128]{1,0:T(8,128)}, u32[]{:S(2)}) copy-start(f32[256,128]{1,0:T(8,128)} %get-tuple-element.50.be_ref) | copy-start | bytes 393220
  44.5 14.8 %all-to-all-start.1 = ((bf16[32,40,128]{2,1,0:T(8,128)(2,1)}), bf16[32,40,128]{2,1,0:T(8,128)(2,1)S(1)}, u32[]{:S(2)}, u32[]{:S(2)}) async-start(bf16[32,40,128]{2,1,0:T(8,128)(2,1)} %get-tuple-element.65), calls=%async_computation.1 | async-start | bytes 655360 | tf_op jit(solution)/shard_map/all_to_all | solution.py:766

commit v5 on v4

--- a/solution.py
+++ b/solution.py
@@ -16,7 +16,8 @@
 MASKED = -1e30
 GRAD_COST = 1 << 37
 GROUPS = 4
-BATCH = 2
+BATCH = 4
+ORDER = {1: (0,), 2: (1, 0), 3: (1, 0, 2)}
 STRIP = 32
 
 norm_eps = 1e-06
@@ -156,7 +157,8 @@
     states = [None] * len(items)
     extra = extra or {}
     for step in range(max([len(items) + len(stages) - 1] + [n + 1 for n in extra])):
-        for lag, stage in enumerate(stages):
+        for lag in ORDER[len(stages)]:
+            stage = stages[lag]
             n = step - lag
             if 0 <= n < len(items):
                 states[n] = stage(items[n], states[n])

time: 60.9 us -> 60.9 us (level)
  no operation moved by 1% of the time
where the time goes in v5:
time: 60.9 us; the launch traced here: 60.5 us
  Pallas kernels  27.2 us (45%)
  waiting for transfers between devices  16.3 us (27%)
  starting transfers between devices  15.4 us (25%)
  between operations  1.6 us (3%)
    pallas_call x7, Pallas kernels, run(): kernel(*[pltpu.with_memory_space_constraint(x, pltpu.HBM) if k in n_hbm e...  27.2 us
    all_to_all x1, waiting for transfers between devices, shards(): lax.all_to_all(payload, ('lat', 'lon'), split_axis=0, concat_axis=0, tile...  8.17 us
    all_to_all x1, waiting for transfers between devices, shards(): lax.all_to_all(reply, ('lat', 'lon'), split_axis=0, concat_axis=0, tiled=...  7.28 us
    all_to_all x1, starting transfers between devices, shards(): lax.all_to_all(payload, ('lat', 'lon'), split_axis=0, concat_axis=0, tile...  4.49 us
    ppermute x1, starting transfers between devices, shards(): east_cot = lax.ppermute(cot_west, 'lon', down)  4.1 us
    ppermute x1, starting transfers between devices, shards(): n_east = lax.ppermute(n0, 'lon', down)  3.43 us
    all_to_all x1, starting transfers between devices, shards(): lax.all_to_all(reply, ('lat', 'lon'), split_axis=0, concat_axis=0, tiled=...  2.73 us
  transfers between devices with their start and end apart: 6, of which 4 were waited for; matrix products, arithmetic and copies ran while one was open for 0% of the time, Pallas kernels for 22%

profile of v5, /device:TPU:0, one launch (start us, length us, event | category | flops | bytes accessed | tf_op | source)
XLA Modules:
  0.0 60.5 jit_solution(5270302579079555573)
XLA Ops:
  1.3 2.6 %shard_map.112 = (bf16[32,40,128]{2,1,0:T(8,128)(2,1)}, s32[1,512]{1,0:T(1,128)S(1)}, bf16[17,16,512]{2,1,0:T(8,128)(2,1)}, bf16[17,16,512]{2,1,0:T(8,128)(2,1)}) custom-call(s32[1,512]{1,0:T(1,128)} %bitcast.1, s32[1]{0:T(128)S(6)} %copy.12.cnt_ref, bf16[512,256]{1,0:T(8,128)(2,1)} %rows_hbm.1, s32[2,4,4]{2,1,0:T(4,128)} %pat_hbm.5, ...), custom_call_target="tpu_custom_call" | custom-call | flops 419430400 | bytes 1048576 | tf_op jit(solution)/shard_map/pallas_call | solution.py:73
  3.8 0.5 collective-permute-start
  4.4 4.1 %collective-permute-start.1 = (bf16[17,16,512]{2,1,0:T(8,128)(2,1)}, bf16[17,16,512]{2,1,0:T(8,128)(2,1)S(1)}, u32[]{:S(2)}, u32[]{:S(2)}) collective-permute-start(bf16[17,16,512]{2,1,0:T(8,128)(2,1)} %get-tuple-element.38), channel_id=1, source_target_pairs={{1,0},{2,1},{3,2},{4,3},{5,4},{6,5},{7,6},{0,7},{9,8},{10,9},{11,1... | collective-permute-start | bytes 835592 | tf_op jit(solution)/shard_map/ppermute | solution.py:707
  8.5 4.5 %all-to-all-start = ((bf16[32,40,128]{2,1,0:T(8,128)(2,1)}), bf16[32,40,128]{2,1,0:T(8,128)(2,1)S(1)}, u32[]{:S(2)}, u32[]{:S(2)}) async-start(bf16[32,40,128]{2,1,0:T(8,128)(2,1)} %get-tuple-element.35), calls=%async_computation | async-start | bytes 655360 | tf_op jit(solution)/shard_map/all_to_all | solution.py:708
  13.0 0.0 copy-start.1
  13.0 0.0 copy-start.3
  13.0 0.2 collective-permute-done.west_ref
  13.1 0.6 %collective-permute-done.1.east_ref = bf16[17,16,512]{2,1,0:T(8,128)(2,1)S(1)} collective-permute-done((bf16[17,16,512]{2,1,0:T(8,128)(2,1)}, bf16[17,16,512]{2,1,0:T(8,128)(2,1)S(1)}, u32[]{:S(2)}, u32[]{:S(2)}) %collective-permute-start.1) | collective-permute-done | bytes 278560 | tf_op jit(solution)/shard_map/ppermute | solution.py:707
  13.8 3.1 %shard_map.114 = (bf16[512,512]{1,0:T(8,128)(2,1)}, bf16[256,512]{1,0:T(8,128)(2,1)}, bf16[256,512]{1,0:T(8,128)(2,1)}, f32[256,128]{1,0:T(8,128)}, f32[256,128]{1,0:T(8,128)}) custom-call(bf16[16,32,512]{2,1,0:T(8,128)(2,1)} %cot_ref.1, bf16[17,16,512]{2,1,0:T(8,128)(2,1)S(1)} %collective-permute-done.west_ref, ...), custom_call_target="tpu_custom_call" | custom-call | flops 137438953472 | bytes 1048576 | tf_op jit(solution)/shard_map/pallas_call | solution.py:73
  16.9 0.0 copy-start
  16.9 0.0 copy-start.4
  16.9 8.2 %all-to-all-done.arr_ref = bf16[32,40,128]{2,1,0:T(8,128)(2,1)S(1)} async-done(((bf16[32,40,128]{2,1,0:T(8,128)(2,1)}), bf16[32,40,128]{2,1,0:T(8,128)(2,1)S(1)}, u32[]{:S(2)}, u32[]{:S(2)}) %all-to-all-start) | async-done | bytes 327712 | tf_op jit(solution)/shard_map/all_to_all | solution.py:708
  25.1 0.0 copy-done.1
  25.1 0.0 copy-done.3
  25.1 2.2 %shard_map.113 = (bf16[512,512]{1,0:T(8,128)(2,1)S(1)}, bf16[512,512]{1,0:T(8,128)(2,1)S(1)}, bf16[256,512]{1,0:T(8,128)(2,1)S(1)}, bf16[256,512]{1,0:T(8,128)(2...) custom-call(bf16[32,40,128]{2,1,0:T(8,128)(2,1)S(1)} %all-to-all-done.arr_ref, ...), custom_call_target="tpu_custom_call" | custom-call | flops 1073741824 | bytes 1048576 | tf_op jit(solution)/shard_map/pallas_call | solution.py:73
  27.3 0.2 collective-permute-start.2
  27.5 3.4 %collective-permute-start.3 = (bf16[256,512]{1,0:T(8,128)(2,1)S(1)}, bf16[256,512]{1,0:T(8,128)(2,1)S(1)}, u32[]{:S(2)}, u32[]{:S(2)}) collective-permute-start(bf16[256,512]{1,0:T(8,128)(2,1)S(1)} %get-tuple-element.43), channel_id=1, source_target_pairs={{1,0},{2,1},{3,2},{4,3},{5,4},{6,5},{7,6},{0,7},{9,8},{10,9},{11,1... | collective-permute-start | bytes 786440 | tf_op jit(solution)/shard_map/ppermute | solution.py:742
  30.9 0.0 copy-done
  30.9 0.0 copy-done.4
  30.9 0.0 copy-start.2
  30.9 0.0 copy-start.5
  30.9 0.0 copy-start.6
  30.9 0.0 copy-start.7
  30.9 0.0 copy-start.8
  30.9 5.1 %shard_map.115 = (bf16[512,512]{1,0:T(8,128)(2,1)S(1)}, bf16[512,512]{1,0:T(8,128)(2,1)S(1)}, bf16[512,512]{1,0:T(8,128)(2,1)S(1)}, f32[512,512]{1,0:T(8,128)S(1...) custom-call(bf16[512,512]{1,0:T(8,128)(2,1)S(1)} %get-tuple-element., ...), custom_call_target="tpu_custom_call" | custom-call | flops 4294967296 | bytes 1048576 | tf_op jit(solution)/shard_map/pallas_call | solution.py:73
  36.1 0.0 collective-permute-done.2.nw_ref
  36.1 0.0 collective-permute-done.3.ne_ref
  36.1 0.0 copy-done.2
  36.1 0.0 copy-done.5
  36.1 0.0 copy-done.6
  36.1 0.0 copy-done.7
  36.2 0.0 copy-done.8
  36.2 8.2 %shard_map.116 = (bf16[512,512]{1,0:T(8,128)(2,1)}, bf16[4,4,128,256]{3,2,1,0:T(8,128)(2,1)}, bf16[512,512]{1,0:T(8,128)(2,1)}, bf16[32,40,128]{2,1,0:T(8,128)(2,1)}) custom-call(bf16[256,512]{1,0:T(8,128)(2,1)S(1)} %collective-permute-done.2.nw_ref, bf16[256,512]{1,0:T(8,128)(2,1)S(1)} %collective-permute-done.3.ne_ref, bf16[512,1536]{1,0:T(8,128)(2,1)S(1)} %copy-done, ...), custom_call_target="tpu_custom_call" | custom-call | flops 4294967296 | bytes 1048576 | tf_op jit(solution)/shard_map/pallas_call | solution.py:73
  44.4 2.7 %all-to-all-start.1 = ((bf16[32,40,128]{2,1,0:T(8,128)(2,1)}), bf16[32,40,128]{2,1,0:T(8,128)(2,1)S(1)}, u32[]{:S(2)}, u32[]{:S(2)}) async-start(bf16[32,40,128]{2,1,0:T(8,128)(2,1)} %get-tuple-element.65), calls=%async_computation.1 | async-start | bytes 655360 | tf_op jit(solution)/shard_map/all_to_all | solution.py:768
  47.1 4.9 %shard_map.117 = (bf16[16,32,512]{2,1,0:T(8,128)(2,1)}, bf16[16,32,512]{2,1,0:T(8,128)(2,1)}) custom-call(bf16[2,8,256,256]{3,2,1,0:T(8,128)(2,1)} %get-tuple-element.41.refs_0_, bf16[4,4,128,256]{3,2,1,0:T(8,128)(2,1)} %get-tuple-element.58.refs_1_, bf16[512,512]{1,0:T(8,128)(2,1)} %get-tuple-element.59.refs_2_, ...), custom_call_target="tpu_custom_call" | custom-call | flops 1073741824 | bytes 1048576 | tf_op jit(solution)/shard_map/pallas_call | solution.py:73
  52.0 7.3 %all-to-all-done.1.back_ref = bf16[32,40,128]{2,1,0:T(8,128)(2,1)S(1)} async-done(((bf16[32,40,128]{2,1,0:T(8,128)(2,1)}), bf16[32,40,128]{2,1,0:T(8,128)(2,1)S(1)}, u32[]{:S(2)}, u32[]{:S(2)}) %all-to-all-start.1) | async-done | bytes 327712 | tf_op jit(solution)/shard_map/all_to_all | solution.py:768
  59.2 1.1 %shard_map.118 = bf16[512,256]{1,0:T(8,128)(2,1)} custom-call(bf16[32,40,128]{2,1,0:T(8,128)(2,1)S(1)} %all-to-all-done.1.back_ref, s32[1,512]{1,0:T(1,128)S(1)} %get-tuple-element.66.slot_ref), custom_call_target="tpu_custom_call" | custom-call | flops 268435456 | bytes 1048576 | tf_op jit(solution)/shard_map/pallas_call | solution.py:73
Async XLA Ops:
  3.8 9.3 %collective-permute-start = (bf16[17,16,512]{2,1,0:T(8,128)(2,1)}, bf16[17,16,512]{2,1,0:T(8,128)(2,1)S(1)}, u32[]{:S(2)}, u32[]{:S(2)}) collective-permute-start(bf16[17,16,512]{2,1,0:T(8,128)(2,1)} %get-tuple-element.37), channel_id=1, source_target_pairs={{0,1},{1,2},{2,3},{3,4},{4,5},{5,6},{6,7},{7,0},{8,9},{9,10},{10,1... | collective-permute-start | bytes 835592 | tf_op jit(solution)/shard_map/ppermute | solution.py:706
  4.4 9.4 %collective-permute-start.1 = (bf16[17,16,512]{2,1,0:T(8,128)(2,1)}, bf16[17,16,512]{2,1,0:T(8,128)(2,1)S(1)}, u32[]{:S(2)}, u32[]{:S(2)}) collective-permute-start(bf16[17,16,512]{2,1,0:T(8,128)(2,1)} %get-tuple-element.38), channel_id=1, source_target_pairs={{1,0},{2,1},{3,2},{4,3},{5,4},{6,5},{7,6},{0,7},{9,8},{10,9},{11,1... | collective-permute-start | bytes 835592 | tf_op jit(solution)/shard_map/ppermute | solution.py:707
  8.5 16.6 %all-to-all-start = ((bf16[32,40,128]{2,1,0:T(8,128)(2,1)}), bf16[32,40,128]{2,1,0:T(8,128)(2,1)S(1)}, u32[]{:S(2)}, u32[]{:S(2)}) async-start(bf16[32,40,128]{2,1,0:T(8,128)(2,1)} %get-tuple-element.35), calls=%async_computation | async-start | bytes 655360 | tf_op jit(solution)/shard_map/all_to_all | solution.py:708
  13.0 12.1 %copy-start.1 = (bf16[16,32,512]{2,1,0:T(8,128)(2,1)S(1)}, bf16[16,32,512]{2,1,0:T(8,128)(2,1)}, u32[]{:S(2)}) copy-start(bf16[16,32,512]{2,1,0:T(8,128)(2,1)} %bg_ref.1) | copy-start | bytes 1572868
  13.0 12.1 %copy-start.3 = (bf16[256,512]{1,0:T(8,128)(2,1)S(1)}, bf16[256,512]{1,0:T(8,128)(2,1)}, u32[]{:S(2)}) copy-start(bf16[256,512]{1,0:T(8,128)(2,1)} %wenc_ref.5) | copy-start | bytes 786436
  16.9 14.0 %copy-start = (bf16[512,1536]{1,0:T(8,128)(2,1)S(1)}, bf16[512,1536]{1,0:T(8,128)(2,1)}, u32[]{:S(2)}) copy-start(bf16[512,1536]{1,0:T(8,128)(2,1)} %wqkv_ref.3) | copy-start | bytes 4718596
  16.9 14.0 %copy-start.4 = (bf16[512,512]{1,0:T(8,128)(2,1)S(1)}, bf16[512,512]{1,0:T(8,128)(2,1)}, u32[]{:S(2)}) copy-start(bf16[512,512]{1,0:T(8,128)(2,1)} %get-tuple-element.39.gm_ref) | copy-start | bytes 1572868
  27.3 8.8 %collective-permute-start.2 = (bf16[256,512]{1,0:T(8,128)(2,1)S(1)}, bf16[256,512]{1,0:T(8,128)(2,1)S(1)}, u32[]{:S(2)}, u32[]{:S(2)}) collective-permute-start(bf16[256,512]{1,0:T(8,128)(2,1)S(1)} %get-tuple-element.42), channel_id=1, source_target_pairs={{0,1},{1,2},{2,3},{3,4},{4,5},{5,6},{6,7},{7,0},{8,9},{9,10},{10,1... | collective-permute-start | bytes 786440 | tf_op jit(solution)/shard_map/ppermute | solution.py:741
  27.5 8.7 %collective-permute-start.3 = (bf16[256,512]{1,0:T(8,128)(2,1)S(1)}, bf16[256,512]{1,0:T(8,128)(2,1)S(1)}, u32[]{:S(2)}, u32[]{:S(2)}) collective-permute-start(bf16[256,512]{1,0:T(8,128)(2,1)S(1)} %get-tuple-element.43), channel_id=1, source_target_pairs={{1,0},{2,1},{3,2},{4,3},{5,4},{6,5},{7,6},{0,7},{9,8},{10,9},{11,1... | collective-permute-start | bytes 786440 | tf_op jit(solution)/shard_map/ppermute | solution.py:742
  30.9 5.2 %copy-start.2 = (bf16[16,32,512]{2,1,0:T(8,128)(2,1)S(1)}, bf16[16,32,512]{2,1,0:T(8,128)(2,1)}, u32[]{:S(2)}) copy-start(bf16[16,32,512]{2,1,0:T(8,128)(2,1)} %cot_ref.1) | copy-start | bytes 1572868
  30.9 5.2 %copy-start.5 = (bf16[256,512]{1,0:T(8,128)(2,1)S(1)}, bf16[256,512]{1,0:T(8,128)(2,1)}, u32[]{:S(2)}) copy-start(bf16[256,512]{1,0:T(8,128)(2,1)} %get-tuple-element.47.gw_ref) | copy-start | bytes 786436
  30.9 5.2 %copy-start.6 = (bf16[256,512]{1,0:T(8,128)(2,1)S(1)}, bf16[256,512]{1,0:T(8,128)(2,1)}, u32[]{:S(2)}) copy-start(bf16[256,512]{1,0:T(8,128)(2,1)} %get-tuple-element.48.ge_ref) | copy-start | bytes 786436
  30.9 5.2 %copy-start.7 = (f32[256,128]{1,0:T(8,128)S(1)}, f32[256,128]{1,0:T(8,128)}, u32[]{:S(2)}) copy-start(f32[256,128]{1,0:T(8,128)} %get-tuple-element.49.bw_ref) | copy-start | bytes 393220
  30.9 5.2 %copy-start.8 = (f32[256,128]{1,0:T(8,128)S(1)}, f32[256,128]{1,0:T(8,128)}, u32[]{:S(2)}) copy-start(f32[256,128]{1,0:T(8,128)} %get-tuple-element.50.be_ref) | copy-start | bytes 393220
  44.4 14.9 %all-to-all-start.1 = ((bf16[32,40,128]{2,1,0:T(8,128)(2,1)}), bf16[32,40,128]{2,1,0:T(8,128)(2,1)S(1)}, u32[]{:S(2)}, u32[]{:S(2)}) async-start(bf16[32,40,128]{2,1,0:T(8,128)(2,1)} %get-tuple-element.65), calls=%async_computation.1 | async-start | bytes 655360 | tf_op jit(solution)/shard_map/all_to_all | solution.py:768

commit v6 on v4

--- a/solution.py
+++ b/solution.py
@@ -16,7 +16,7 @@
 MASKED = -1e30
 GRAD_COST = 1 << 37
 GROUPS = 4
-BATCH = 2
+BATCH = 4
 STRIP = 32
 
 norm_eps = 1e-06

time: 60.9 us -> 60.8 us (level)
  no operation moved by 1% of the time
where the time goes in v6:
time: 60.8 us; the launch traced here: 60.4 us
  Pallas kernels  27.2 us (45%)
  waiting for transfers between devices  16.2 us (27%)
  starting transfers between devices  15.3 us (25%)
  between operations  1.62 us (3%)
    pallas_call x7, Pallas kernels, run(): kernel(*[pltpu.with_memory_space_constraint(x, pltpu.HBM) if k in n_hbm e...  27.2 us
    all_to_all x1, waiting for transfers between devices, shards(): lax.all_to_all(payload, ('lat', 'lon'), split_axis=0, concat_axis=0, tile...  8.17 us
    all_to_all x1, waiting for transfers between devices, shards(): lax.all_to_all(reply, ('lat', 'lon'), split_axis=0, concat_axis=0, tiled=...  7.27 us
    all_to_all x1, starting transfers between devices, shards(): lax.all_to_all(payload, ('lat', 'lon'), split_axis=0, concat_axis=0, tile...  4.49 us
    ppermute x1, starting transfers between devices, shards(): east_cot = lax.ppermute(cot_west, 'lon', down)  4.1 us
    ppermute x1, starting transfers between devices, shards(): n_east = lax.ppermute(n0, 'lon', down)  3.43 us
    all_to_all x1, starting transfers between devices, shards(): lax.all_to_all(reply, ('lat', 'lon'), split_axis=0, concat_axis=0, tiled=...  2.61 us
  transfers between devices with their start and end apart: 6, of which 4 were waited for; matrix products, arithmetic and copies ran while one was open for 0% of the time, Pallas kernels for 22%

profile of v6, /device:TPU:0, one launch (start us, length us, event | category | flops | bytes accessed | tf_op | source)
XLA Modules:
  0.0 60.4 jit_solution(7950713804902041801)
XLA Ops:
  1.3 2.6 %shard_map.112 = (bf16[32,40,128]{2,1,0:T(8,128)(2,1)}, s32[1,512]{1,0:T(1,128)S(1)}, bf16[17,16,512]{2,1,0:T(8,128)(2,1)}, bf16[17,16,512]{2,1,0:T(8,128)(2,1)}) custom-call(s32[1,512]{1,0:T(1,128)} %bitcast.1, s32[1]{0:T(128)S(6)} %copy.12.cnt_ref, bf16[512,256]{1,0:T(8,128)(2,1)} %rows_hbm.1, s32[2,4,4]{2,1,0:T(4,128)} %pat_hbm.5, ...), custom_call_target="tpu_custom_call" | custom-call | flops 419430400 | bytes 1048576 | tf_op jit(solution)/shard_map/pallas_call | solution.py:72
  3.8 0.5 collective-permute-start
  4.4 4.1 %collective-permute-start.1 = (bf16[17,16,512]{2,1,0:T(8,128)(2,1)}, bf16[17,16,512]{2,1,0:T(8,128)(2,1)S(1)}, u32[]{:S(2)}, u32[]{:S(2)}) collective-permute-start(bf16[17,16,512]{2,1,0:T(8,128)(2,1)} %get-tuple-element.38), channel_id=1, source_target_pairs={{1,0},{2,1},{3,2},{4,3},{5,4},{6,5},{7,6},{0,7},{9,8},{10,9},{11,1... | collective-permute-start | bytes 835592 | tf_op jit(solution)/shard_map/ppermute | solution.py:705
  8.5 4.5 %all-to-all-start = ((bf16[32,40,128]{2,1,0:T(8,128)(2,1)}), bf16[32,40,128]{2,1,0:T(8,128)(2,1)S(1)}, u32[]{:S(2)}, u32[]{:S(2)}) async-start(bf16[32,40,128]{2,1,0:T(8,128)(2,1)} %get-tuple-element.35), calls=%async_computation | async-start | bytes 655360 | tf_op jit(solution)/shard_map/all_to_all | solution.py:706
  13.0 0.0 copy-start.1
  13.0 0.0 copy-start.3
  13.0 0.2 collective-permute-done.west_ref
  13.1 0.6 %collective-permute-done.1.east_ref = bf16[17,16,512]{2,1,0:T(8,128)(2,1)S(1)} collective-permute-done((bf16[17,16,512]{2,1,0:T(8,128)(2,1)}, bf16[17,16,512]{2,1,0:T(8,128)(2,1)S(1)}, u32[]{:S(2)}, u32[]{:S(2)}) %collective-permute-start.1) | collective-permute-done | bytes 278560 | tf_op jit(solution)/shard_map/ppermute | solution.py:705
  13.8 3.1 %shard_map.114 = (bf16[512,512]{1,0:T(8,128)(2,1)}, bf16[256,512]{1,0:T(8,128)(2,1)}, bf16[256,512]{1,0:T(8,128)(2,1)}, f32[256,128]{1,0:T(8,128)}, f32[256,128]{1,0:T(8,128)}) custom-call(bf16[16,32,512]{2,1,0:T(8,128)(2,1)} %cot_ref.1, bf16[17,16,512]{2,1,0:T(8,128)(2,1)S(1)} %collective-permute-done.west_ref, ...), custom_call_target="tpu_custom_call" | custom-call | flops 137438953472 | bytes 1048576 | tf_op jit(solution)/shard_map/pallas_call | solution.py:72
  16.9 0.0 copy-start
  16.9 0.0 copy-start.4
  16.9 8.2 %all-to-all-done.arr_ref = bf16[32,40,128]{2,1,0:T(8,128)(2,1)S(1)} async-done(((bf16[32,40,128]{2,1,0:T(8,128)(2,1)}), bf16[32,40,128]{2,1,0:T(8,128)(2,1)S(1)}, u32[]{:S(2)}, u32[]{:S(2)}) %all-to-all-start) | async-done | bytes 327712 | tf_op jit(solution)/shard_map/all_to_all | solution.py:706
  25.1 0.0 copy-done.1
  25.1 0.0 copy-done.3
  25.1 2.2 %shard_map.113 = (bf16[512,512]{1,0:T(8,128)(2,1)S(1)}, bf16[512,512]{1,0:T(8,128)(2,1)S(1)}, bf16[256,512]{1,0:T(8,128)(2,1)S(1)}, bf16[256,512]{1,0:T(8,128)(2...) custom-call(bf16[32,40,128]{2,1,0:T(8,128)(2,1)S(1)} %all-to-all-done.arr_ref, ...), custom_call_target="tpu_custom_call" | custom-call | flops 1073741824 | bytes 1048576 | tf_op jit(solution)/shard_map/pallas_call | solution.py:72
  27.3 0.2 collective-permute-start.2
  27.5 3.4 %collective-permute-start.3 = (bf16[256,512]{1,0:T(8,128)(2,1)S(1)}, bf16[256,512]{1,0:T(8,128)(2,1)S(1)}, u32[]{:S(2)}, u32[]{:S(2)}) collective-permute-start(bf16[256,512]{1,0:T(8,128)(2,1)S(1)} %get-tuple-element.43), channel_id=1, source_target_pairs={{1,0},{2,1},{3,2},{4,3},{5,4},{6,5},{7,6},{0,7},{9,8},{10,9},{11,1... | collective-permute-start | bytes 786440 | tf_op jit(solution)/shard_map/ppermute | solution.py:740
  30.9 0.0 copy-done
  30.9 0.0 copy-done.4
  30.9 0.0 copy-start.2
  30.9 0.0 copy-start.5
  30.9 0.0 copy-start.6
  30.9 0.0 copy-start.7
  30.9 0.0 copy-start.8
  30.9 5.4 %shard_map.115 = (bf16[512,512]{1,0:T(8,128)(2,1)S(1)}, bf16[512,512]{1,0:T(8,128)(2,1)S(1)}, bf16[512,512]{1,0:T(8,128)(2,1)S(1)}, f32[512,512]{1,0:T(8,128)S(1...) custom-call(bf16[512,512]{1,0:T(8,128)(2,1)S(1)} %get-tuple-element., ...), custom_call_target="tpu_custom_call" | custom-call | flops 4294967296 | bytes 1048576 | tf_op jit(solution)/shard_map/pallas_call | solution.py:72
  36.3 0.0 collective-permute-done.2.nw_ref
  36.3 0.0 collective-permute-done.3.ne_ref
  36.3 0.0 copy-done.2
  36.3 0.0 copy-done.5
  36.3 0.0 copy-done.6
  36.4 0.0 copy-done.7
  36.4 0.0 copy-done.8
  36.4 8.0 %shard_map.116 = (bf16[512,512]{1,0:T(8,128)(2,1)}, bf16[4,4,128,256]{3,2,1,0:T(8,128)(2,1)}, bf16[512,512]{1,0:T(8,128)(2,1)}, bf16[32,40,128]{2,1,0:T(8,128)(2,1)}) custom-call(bf16[256,512]{1,0:T(8,128)(2,1)S(1)} %collective-permute-done.2.nw_ref, bf16[256,512]{1,0:T(8,128)(2,1)S(1)} %collective-permute-done.3.ne_ref, bf16[512,1536]{1,0:T(8,128)(2,1)S(1)} %copy-done, ...), custom_call_target="tpu_custom_call" | custom-call | flops 4294967296 | bytes 1048576 | tf_op jit(solution)/shard_map/pallas_call | solution.py:72
  44.4 2.6 %all-to-all-start.1 = ((bf16[32,40,128]{2,1,0:T(8,128)(2,1)}), bf16[32,40,128]{2,1,0:T(8,128)(2,1)S(1)}, u32[]{:S(2)}, u32[]{:S(2)}) async-start(bf16[32,40,128]{2,1,0:T(8,128)(2,1)} %get-tuple-element.65), calls=%async_computation.1 | async-start | bytes 655360 | tf_op jit(solution)/shard_map/all_to_all | solution.py:766
  47.0 4.9 %shard_map.117 = (bf16[16,32,512]{2,1,0:T(8,128)(2,1)}, bf16[16,32,512]{2,1,0:T(8,128)(2,1)}) custom-call(bf16[2,8,256,256]{3,2,1,0:T(8,128)(2,1)} %get-tuple-element.41.refs_0_, bf16[4,4,128,256]{3,2,1,0:T(8,128)(2,1)} %get-tuple-element.58.refs_1_, bf16[512,512]{1,0:T(8,128)(2,1)} %get-tuple-element.59.refs_2_, ...), custom_call_target="tpu_custom_call" | custom-call | flops 1073741824 | bytes 1048576 | tf_op jit(solution)/shard_map/pallas_call | solution.py:72
  51.8 7.3 %all-to-all-done.1.back_ref = bf16[32,40,128]{2,1,0:T(8,128)(2,1)S(1)} async-done(((bf16[32,40,128]{2,1,0:T(8,128)(2,1)}), bf16[32,40,128]{2,1,0:T(8,128)(2,1)S(1)}, u32[]{:S(2)}, u32[]{:S(2)}) %all-to-all-start.1) | async-done | bytes 327712 | tf_op jit(solution)/shard_map/all_to_all | solution.py:766
  59.1 1.1 %shard_map.118 = bf16[512,256]{1,0:T(8,128)(2,1)} custom-call(bf16[32,40,128]{2,1,0:T(8,128)(2,1)S(1)} %all-to-all-done.1.back_ref, s32[1,512]{1,0:T(1,128)S(1)} %get-tuple-element.66.slot_ref), custom_call_target="tpu_custom_call" | custom-call | flops 268435456 | bytes 1048576 | tf_op jit(solution)/shard_map/pallas_call | solution.py:72
Async XLA Ops:
  3.8 9.3 %collective-permute-start = (bf16[17,16,512]{2,1,0:T(8,128)(2,1)}, bf16[17,16,512]{2,1,0:T(8,128)(2,1)S(1)}, u32[]{:S(2)}, u32[]{:S(2)}) collective-permute-start(bf16[17,16,512]{2,1,0:T(8,128)(2,1)} %get-tuple-element.37), channel_id=1, source_target_pairs={{0,1},{1,2},{2,3},{3,4},{4,5},{5,6},{6,7},{7,0},{8,9},{9,10},{10,1... | collective-permute-start | bytes 835592 | tf_op jit(solution)/shard_map/ppermute | solution.py:704
  4.4 9.4 %collective-permute-start.1 = (bf16[17,16,512]{2,1,0:T(8,128)(2,1)}, bf16[17,16,512]{2,1,0:T(8,128)(2,1)S(1)}, u32[]{:S(2)}, u32[]{:S(2)}) collective-permute-start(bf16[17,16,512]{2,1,0:T(8,128)(2,1)} %get-tuple-element.38), channel_id=1, source_target_pairs={{1,0},{2,1},{3,2},{4,3},{5,4},{6,5},{7,6},{0,7},{9,8},{10,9},{11,1... | collective-permute-start | bytes 835592 | tf_op jit(solution)/shard_map/ppermute | solution.py:705
  8.5 16.6 %all-to-all-start = ((bf16[32,40,128]{2,1,0:T(8,128)(2,1)}), bf16[32,40,128]{2,1,0:T(8,128)(2,1)S(1)}, u32[]{:S(2)}, u32[]{:S(2)}) async-start(bf16[32,40,128]{2,1,0:T(8,128)(2,1)} %get-tuple-element.35), calls=%async_computation | async-start | bytes 655360 | tf_op jit(solution)/shard_map/all_to_all | solution.py:706
  13.0 12.1 %copy-start.1 = (bf16[16,32,512]{2,1,0:T(8,128)(2,1)S(1)}, bf16[16,32,512]{2,1,0:T(8,128)(2,1)}, u32[]{:S(2)}) copy-start(bf16[16,32,512]{2,1,0:T(8,128)(2,1)} %bg_ref.1) | copy-start | bytes 1572868
  13.0 12.1 %copy-start.3 = (bf16[256,512]{1,0:T(8,128)(2,1)S(1)}, bf16[256,512]{1,0:T(8,128)(2,1)}, u32[]{:S(2)}) copy-start(bf16[256,512]{1,0:T(8,128)(2,1)} %wenc_ref.5) | copy-start | bytes 786436
  16.9 14.0 %copy-start = (bf16[512,1536]{1,0:T(8,128)(2,1)S(1)}, bf16[512,1536]{1,0:T(8,128)(2,1)}, u32[]{:S(2)}) copy-start(bf16[512,1536]{1,0:T(8,128)(2,1)} %wqkv_ref.3) | copy-start | bytes 4718596
  16.9 14.0 %copy-start.4 = (bf16[512,512]{1,0:T(8,128)(2,1)S(1)}, bf16[512,512]{1,0:T(8,128)(2,1)}, u32[]{:S(2)}) copy-start(bf16[512,512]{1,0:T(8,128)(2,1)} %get-tuple-element.39.gm_ref) | copy-start | bytes 1572868
  27.3 9.0 %collective-permute-start.2 = (bf16[256,512]{1,0:T(8,128)(2,1)S(1)}, bf16[256,512]{1,0:T(8,128)(2,1)S(1)}, u32[]{:S(2)}, u32[]{:S(2)}) collective-permute-start(bf16[256,512]{1,0:T(8,128)(2,1)S(1)} %get-tuple-element.42), channel_id=1, source_target_pairs={{0,1},{1,2},{2,3},{3,4},{4,5},{5,6},{6,7},{7,0},{8,9},{9,10},{10,1... | collective-permute-start | bytes 786440 | tf_op jit(solution)/shard_map/ppermute | solution.py:739
  27.5 8.9 %collective-permute-start.3 = (bf16[256,512]{1,0:T(8,128)(2,1)S(1)}, bf16[256,512]{1,0:T(8,128)(2,1)S(1)}, u32[]{:S(2)}, u32[]{:S(2)}) collective-permute-start(bf16[256,512]{1,0:T(8,128)(2,1)S(1)} %get-tuple-element.43), channel_id=1, source_target_pairs={{1,0},{2,1},{3,2},{4,3},{5,4},{6,5},{7,6},{0,7},{9,8},{10,9},{11,1... | collective-permute-start | bytes 786440 | tf_op jit(solution)/shard_map/ppermute | solution.py:740
  30.9 5.4 %copy-start.2 = (bf16[16,32,512]{2,1,0:T(8,128)(2,1)S(1)}, bf16[16,32,512]{2,1,0:T(8,128)(2,1)}, u32[]{:S(2)}) copy-start(bf16[16,32,512]{2,1,0:T(8,128)(2,1)} %cot_ref.1) | copy-start | bytes 1572868
  30.9 5.4 %copy-start.5 = (bf16[256,512]{1,0:T(8,128)(2,1)S(1)}, bf16[256,512]{1,0:T(8,128)(2,1)}, u32[]{:S(2)}) copy-start(bf16[256,512]{1,0:T(8,128)(2,1)} %get-tuple-element.47.gw_ref) | copy-start | bytes 786436
  30.9 5.4 %copy-start.6 = (bf16[256,512]{1,0:T(8,128)(2,1)S(1)}, bf16[256,512]{1,0:T(8,128)(2,1)}, u32[]{:S(2)}) copy-start(bf16[256,512]{1,0:T(8,128)(2,1)} %get-tuple-element.48.ge_ref) | copy-start | bytes 786436
  30.9 5.4 %copy-start.7 = (f32[256,128]{1,0:T(8,128)S(1)}, f32[256,128]{1,0:T(8,128)}, u32[]{:S(2)}) copy-start(f32[256,128]{1,0:T(8,128)} %get-tuple-element.49.bw_ref) | copy-start | bytes 393220
  30.9 5.4 %copy-start.8 = (f32[256,128]{1,0:T(8,128)S(1)}, f32[256,128]{1,0:T(8,128)}, u32[]{:S(2)}) copy-start(f32[256,128]{1,0:T(8,128)} %get-tuple-element.50.be_ref) | copy-start | bytes 393220
  44.4 14.8 %all-to-all-start.1 = ((bf16[32,40,128]{2,1,0:T(8,128)(2,1)}), bf16[32,40,128]{2,1,0:T(8,128)(2,1)S(1)}, u32[]{:S(2)}, u32[]{:S(2)}) async-start(bf16[32,40,128]{2,1,0:T(8,128)(2,1)} %get-tuple-element.65), calls=%async_computation.1 | async-start | bytes 655360 | tf_op jit(solution)/shard_map/all_to_all | solution.py:766
